TPU v7x, 32 devices: a whole 2x2x4 slice. The times are simulated.
32 devices in a mesh: pot: 8 (over y, x, core), grid: 4 (over z).
Axes of the slice: x: 2, y: 2, z: 4, core: 2. Of those that a mesh axis runs over, the one named last changes fastest.
Arguments:
- potentials: float32 [8, 32, 4096], P('pot', 'grid'), may hold values from -6 to 6
- orbitals: bfloat16 [32, 32, 4096], P(None, 'grid', 'pot'), may hold values from -0.5 to 2
- energies: float32 [32], replicated, may hold values from -2 to -0.2
- local_potential: float32 [32, 4096], replicated, may hold values from 0 to 3
- inverse_factor: bfloat16 [8, 8], replicated, may hold values from -8 to 8, as said below
Outputs:
- updated: float32 [8, 32, 4096], P('pot', 'grid')
- margins: float32 [8, 8], P('pot')
Inputs may be any that keep to these rules, and one draw needn't show every extreme that they name: `inverse_factor`: lower triangular with a positive diagonal.
All inputs are finite; a program needn't handle non-finite values.
Results may differ from a plain program's by a relative error of at most 0.0029.
Values may be sent and summed in bfloat16 or wider, within the bound.
No kernel may reach another device: no remote copies, remote signals or barrier semaphores. Data moves between devices by JAX's collectives and lax.ppermute only.
A program may use at most 64 MiB of HBM per device.

v0:
```python
import functools
import math

import jax
import jax.numpy as jnp
from jax import lax
from jax.experimental import pallas as pl
from jax.experimental.pallas import tpu as pltpu
from jax.sharding import PartitionSpec as P


NX = 64
SWEEPS = 4
DAMPING = 0.8
COEFFS = tuple(
    sum(math.comb(n, m) * (1.0 - DAMPING) ** (n - m) for n in range(m, SWEEPS))
    for m in range(SWEEPS)
)
HALO = SWEEPS - 1
LEAD = HALO + HALO % 2
LANES = 128
SUBLANES = 8
VMEM_LIMIT = 24 << 20


def padded_2(block, sides, width):
    for axis, dim in sides:
        count = lax.axis_size(axis)
        forward = [(i, i + 1) for i in range(count - 1)]
        backward = [(target, source) for source, target in forward]
        low = lax.ppermute(
            lax.slice_in_dim(block, block.shape[dim] - width, None, axis=dim), axis, forward
        )
        high = lax.ppermute(lax.slice_in_dim(block, 0, width, axis=dim), axis, backward)
        block = jnp.concatenate([low, block, high], axis=dim)
    return block


def plane_neighbours(field, row_width):
    plane_size = field.shape[-1]
    widths = [(0, 0)] * (field.ndim - 1)
    padded = jnp.pad(field, widths + [(row_width, row_width)])
    along_y = padded[..., 2 * row_width :] + padded[..., :plane_size]
    column = jnp.arange(plane_size, dtype=jnp.int32) % row_width
    padded = jnp.pad(field, widths + [(1, 1)])
    right_side = jnp.where(column == row_width - 1, 0.0, padded[..., 2:])
    left_side = jnp.where(column == 0, 0.0, padded[..., :plane_size])
    return along_y + right_side + left_side


def across_slabs(answer):
    padded = padded_2(answer, (("grid", 2),), 1)
    return padded[:, :, 2:] + padded[:, :, :-2]


def absorb(orbital_block, energy_block, fields, local_here, along_planes):
    orbital = orbital_block.astype(jnp.float32)[:, None]
    diagonal = (3.0 + local_here[None] - energy_block[:, None, None])[:, None]
    source = -orbital * fields[None]
    answer = DAMPING * source / diagonal
    for _ in range(SWEEPS - 1):
        nearby = along_planes(answer) + plane_neighbours(answer, NX)
        answer = answer + DAMPING * (source - diagonal * answer + 0.5 * nearby) / diagonal
    return jnp.sum(orbital * answer, axis=0)


def gathered_plan(potentials, orbitals, energies, local_potential, inverse_factor):
    slab_depth = potentials.shape[1]
    count = orbitals.shape[0]
    cells = local_potential.size
    grid_index = lax.axis_index("grid")
    local_here = lax.dynamic_slice_in_dim(local_potential, grid_index * slab_depth, slab_depth, 0)
    blocks = 4 if count % 4 == 0 else 1
    block_size = count // blocks
    response = jnp.zeros(potentials.shape, jnp.float32)
    for number in range(blocks):
        orbital_block = orbitals[number * block_size : (number + 1) * block_size]
        gathered = lax.all_gather(orbital_block, "pot", axis=2, tiled=True)
        energy_block = energies[number * block_size : (number + 1) * block_size]
        response = response + absorb(gathered, energy_block, potentials, local_here, across_slabs)
    trial_block = (potentials + 4.0 / count * response).astype(jnp.bfloat16)
    by_cells = lax.all_to_all(trial_block, "pot", split_axis=2, concat_axis=0, tiled=True)
    row_count = by_cells.shape[0]
    flattened = by_cells.reshape(row_count, -1)
    partial_margins = lax.dot_general(
        flattened, flattened, (((1,), (1,)), ((), ())), preferred_element_type=jnp.float32
    )
    combined = jnp.dot(inverse_factor, flattened, preferred_element_type=jnp.float32).reshape(
        by_cells.shape
    )
    updated = lax.all_to_all(combined, "pot", split_axis=0, concat_axis=2, tiled=True)
    scattered = lax.psum_scatter(partial_margins, "pot", scatter_dimension=0, tiled=True)
    own_rows = lax.psum(scattered, "grid")
    margins = own_rows / cells
    return (updated, margins)


def row_cells(depth):
    return [(d, z) for d in range(1, HALO + 1) for z in range(depth)]


def plane_cells(rows):
    return [(d, y) for d in range(1, HALO + 1) for y in range(d - HALO, rows + HALO - d)]


def iota(shape, dim):
    return lax.broadcasted_iota(jnp.int32, shape, dim)


def bf16_dot(a, b):
    return jnp.dot(a, b, preferred_element_type=jnp.float32)


def one_hot(mask):
    return mask.astype(jnp.float32).astype(jnp.bfloat16)


def lane_halves(shape):
    return iota(shape, len(shape) - 1) < NX


SPLIT = 4
STEPS = NX // SPLIT
BATCH = LANES // STEPS


def orbital_kernel(orb_ref, own_ref, a_ref, b_ref, s_ref):
    count, depth, width = orb_ref.shape
    groups = count // BATCH
    rows = width // NX
    lane_in, lane_out = iota((LANES, LANES), 0), iota((LANES, LANES), 1)
    wanted = (lane_out // NX) * NX + SPLIT * (lane_out % STEPS) + lane_out // STEPS % SPLIT
    permute = one_hot(lane_in == wanted)
    lane = iota((depth, LANES), 1) // STEPS
    for t in range(width // LANES):
        lanes = slice(t * LANES, (t + 1) * LANES)
        tile = orb_ref[:, :, lanes].astype(jnp.float32).reshape(count * depth, LANES)
        tile = bf16_dot(tile.astype(jnp.bfloat16), permute)
        for g in range(groups):
            first = g * BATCH * depth
            regs = [tile[first + b * depth : first + (b + 1) * depth] for b in range(BATCH)]
            step = BATCH // 2
            while step:
                stays = lane // step % 2 == 0
                for b in range(BATCH):
                    if b & step == 0:
                        lo, hi = regs[b], regs[b + step]
                        regs[b] = jnp.where(stays, lo, pltpu.roll(hi, step * STEPS, 1))
                        regs[b + step] = jnp.where(
                            stays, pltpu.roll(lo, LANES - step * STEPS, 1), hi
                        )
                step //= 2
            for c in range(BATCH):
                y, m = 2 * t + c // SPLIT, c % SPLIT
                at = ((m * groups + g) * rows + y) * depth
                s_ref[at : at + depth] = regs[c]
    for z in range(depth):
        for y in range(rows):
            tile = s_ref[pl.ds(y * depth + z, SPLIT * groups, stride=rows * depth), :]
            own_ref[z, y] = tile.astype(jnp.bfloat16)
    even = lax.rem(lax.axis_index("pot"), 2) == 0
    for at, (d, z) in enumerate(row_cells(depth)):
        a_ref[at] = own_ref[z, jnp.where(even, rows - d, d - 1)]
        b_ref[at] = own_ref[z, jnp.where(even, d - 1, rows - d)]


def window_kernel(v_ref, out_ref):
    receivers, pieces = out_ref.shape[:2]
    total = v_ref.shape[2] // LANES
    stride = total // receivers
    ahead = LEAD * NX // LANES
    for p in range(receivers):
        for t in range(pieces):
            at = p * stride + t - ahead
            if 0 <= at < total:
                out_ref[p, t] = v_ref[0, :, at * LANES : (at + 1) * LANES]
            else:
                out_ref[p, t] = jnp.zeros(out_ref.shape[2:], out_ref.dtype)


def two_parts(value, y):
    left = lane_halves(value.shape)
    upper = value.astype(jnp.bfloat16).astype(jnp.float32)
    lower = value - upper
    if y % 2:
        return jnp.where(left, pltpu.roll(upper, NX, 1), lower)
    return jnp.where(left, upper, pltpu.roll(lower, NX, 1))


def row_tile(own_ref, a_ref, b_ref, z, y):
    depth, rows = own_ref.shape[:2]
    even = lax.rem(lax.axis_index("pot"), 2) == 0
    if 0 <= y < rows:
        return own_ref[z, y]
    at = (-y - 1 if y < 0 else y - rows) * depth + z
    a, b = a_ref[at].astype(jnp.float32), b_ref[at].astype(jnp.float32)
    return jnp.where(even == (y < 0), b, a).astype(jnp.bfloat16)


def send_kernel(v_ref, own_ref, a_ref, b_ref, to_a_ref, to_b_ref):
    depth, rows = own_ref.shape[:2]
    pieces = rows * NX // LANES + 2 * (LEAD * NX // LANES)
    fields = v_ref.shape[0] // (pieces * depth)
    even = lax.rem(lax.axis_index("grid"), 2) == 0

    def tile_of(z, y):
        start = (y + LEAD) // 2 * depth + z
        value = v_ref[pl.ds(start, fields, stride=pieces * depth), :]
        orbitals = row_tile(own_ref, a_ref, b_ref, z, y).astype(jnp.float32)
        return jnp.concatenate([orbitals, two_parts(value, y)], axis=0)

    for at, (d, y) in enumerate(plane_cells(rows)):
        top, bottom = tile_of(depth - d, y), tile_of(d - 1, y)
        to_a_ref[at] = jnp.where(even, top, bottom).astype(jnp.bfloat16)
        to_b_ref[at] = jnp.where(even, bottom, top).astype(jnp.bfloat16)


def diagonal_kernel(energy_ref, lp_ref, r_ref, lp_ref2, *part_refs):
    planes_all, plane_cells = lp_ref.shape
    rows_all = plane_cells // NX
    region_z, region_y, size, _ = r_ref.shape
    depth, rows = region_z - 2 * HALO, region_y - 2 * HALO
    groups = size // SPLIT
    z_base = lax.axis_index("grid") * depth
    y_base = lax.axis_index("pot") * rows

    shift = jnp.zeros((size, LANES), jnp.float32)
    group_of = iota((size, LANES), 0) % groups
    member = iota((size, LANES), 1) // STEPS
    for g in range(groups):
        for b in range(BATCH):
            here = (group_of == g) & (member == b)
            shift = jnp.where(here, 3.0 - energy_ref[g * BATCH + b], shift)

    pairs = part_refs[0].shape[0]
    for p in range(pairs):
        at = jnp.clip((y_base - LEAD) // 2 + p, 0, rows_all // 2 - 1) * LANES
        rest = lp_ref[:, pl.ds(pl.multiple_of(at, LANES), LANES)]
        for part_ref in part_refs:
            part = rest.astype(jnp.bfloat16).astype(jnp.float32)
            part_ref[p] = part
            rest = rest - part
    from_lane, to_lane = iota((LANES, 2 * LANES), 0), iota((LANES, 2 * LANES), 1)
    pick = one_hot(
        (from_lane // NX == to_lane // LANES) & (from_lane % NX // SPLIT == to_lane % STEPS)
    )
    tile = (SUBLANES, LANES)
    keep = iota(tile, 1) % SPLIT == iota(tile, 0) % SPLIT
    per_tile = SUBLANES // SPLIT
    plane_of = iota(tile, 0) // SPLIT

    def clipped(zi):
        return jnp.clip(z_base + zi - HALO, 0, planes_all - 1)

    def chosen(index, values):
        out = jnp.broadcast_to(values[0], tile)
        for number, value in enumerate(values[1:], 1):
            out = jnp.where(index == number, jnp.broadcast_to(value, tile), out)
        return out

    for p in range(pairs):
        stacked = []
        for ref in part_refs:
            for zi in range(0, region_z, per_tile):
                values = [ref[p, pl.ds(clipped(zi + i), 1), :] for i in range(per_tile)]
                stacked.append(jnp.where(keep, chosen(plane_of, values), 0.0))
        parts = bf16_dot(jnp.concatenate(stacked, axis=0).astype(jnp.bfloat16), pick)
        length = region_z * SPLIT
        lp = (parts[:length] + parts[length : 2 * length]) + parts[2 * length :]
        lp_ref2[2 * p] = lp[:, :LANES]
        lp_ref2[2 * p + 1] = lp[:, LANES:]

    m_of = iota(tile, 0) // groups
    ms = SUBLANES // groups

    def plane(zi, carry):
        zg = z_base + zi - HALO
        z_inside = (zg >= 0) & (zg < planes_all)
        for y in range(-HALO, rows + HALO):
            yg = y_base + y
            inside = z_inside & (yg >= 0) & (yg < rows_all)
            scale = jnp.where(inside, 0.5 * DAMPING, 0.0)
            for part in range(size // SUBLANES):
                values = [
                    lp_ref2[y + LEAD, pl.ds(zi * SPLIT + part * ms + i, 1), :] for i in range(ms)
                ]
                at = slice(part * SUBLANES, (part + 1) * SUBLANES)
                r_ref[zi, y + HALO, at] = scale / (shift[at] + chosen(m_of, values))
        return carry

    lax.fori_loop(0, region_z, plane, 0)


def spread_matrix():
    from_lane = iota((LANES, SPLIT * LANES), 0)
    to_lane = iota((LANES, SPLIT * LANES), 1)
    return one_hot(from_lane % NX == SPLIT * (to_lane % STEPS) + to_lane // LANES)


def place(cells, r_ref, ro_ref, first_ref, then=None):
    fields = first_ref.shape[4]
    packed = jnp.concatenate([parts for _, parts, _, _ in cells], axis=0).astype(jnp.bfloat16)
    values = bf16_dot(packed, spread_matrix())
    for number, (orbitals, _, z, y) in enumerate(cells):
        zi, yi = z + HALO, y + HALO
        o = -2.0 * orbitals.astype(jnp.float32)
        ro = r_ref[zi, yi] * o
        ro_ref[zi, yi] = ro
        own = [
            values[number * fields : (number + 1) * fields, m * LANES : (m + 1) * LANES]
            for m in range(SPLIT)
        ]
        first_sweep(ro_ref, first_ref, z, y, own)
        if then is not None:
            then(z, y, o * ro, own)


def first_sweep(ro_ref, first_ref, z, y, values):
    groups = first_ref.shape[0]
    zi, yi = z + HALO, y + HALO
    for g in range(groups):
        for m in range(SPLIT):
            at = m * groups + g
            ro = jnp.broadcast_to(ro_ref[zi, yi, at : at + 1], values[m].shape)
            first_ref[g, zi, yi, m] = ro * values[m]


def prepare_kernel(
    parts_ref, own_ref, a_ref, b_ref, r_ref, ro_ref, first_ref, acc_ref, w_ref
):
    depth, rows = own_ref.shape[:2]
    fields = first_ref.shape[4]
    size = ro_ref.shape[2]
    groups = size // SPLIT
    pieces = parts_ref.shape[0] // (depth * fields)

    def first_term(z, y, weight, values):
        if not 0 <= y < rows:
            return
        turn = groups // 2
        while turn:
            weight = weight + pltpu.roll(weight, size - turn, 0)
            turn //= 2
        w_ref[y] = COEFFS[0] * weight
        for m in range(SPLIT):
            at = m * groups
            w = jnp.broadcast_to(w_ref[y, at : at + 1], (fields, LANES))
            acc_ref[z, y, m] = w * values[m]

    def plane(z, carry):
        cells = []
        for y in range(-HALO, rows + HALO):
            start = (y + LEAD) // 2 * depth + z
            value = parts_ref[pl.ds(start, fields, stride=pieces * depth), :]
            cells.append((row_tile(own_ref, a_ref, b_ref, z, y), two_parts(value, y), z, y))
        place(cells, r_ref, ro_ref, first_ref, first_term)
        return carry

    lax.fori_loop(0, depth, plane, 0)


def sweep_kernel(
    parts_ref, a_ref, b_ref, r_ref, inverse_ref, ro_in, first_in, acc_in,
    out_ref, ro_ref, first_ref, acc_ref, x_ref, y_ref, m_ref,
):
    depth, rows = acc_ref.shape[:2]
    fields = first_ref.shape[4]
    size = ro_ref.shape[2]
    groups = size // SPLIT
    count = groups * BATCH
    even = lax.rem(lax.axis_index("grid"), 2) == 0
    all_cells = list(enumerate(plane_cells(rows)))
    for d in range(1, HALO + 1):
        z_a = jnp.where(even, depth - 1 + d, -d)
        z_b = jnp.where(even, -d, depth - 1 + d)
        cells = []
        for at, (distance, y) in all_cells:
            if distance == d:
                for ref, z in ((a_ref, z_a), (b_ref, z_b)):
                    tile = ref[at].astype(jnp.float32)
                    cells.append((tile[:size], tile[size:], z, y))
        place(cells, r_ref, ro_ref, first_ref)

    step = iota((fields, LANES), 1) % STEPS
    first_k = step == 0
    last_k = step == STEPS - 1

    def group(g, carry):
        buffers = (first_ref.at[g], x_ref, y_ref)

        def stage(number, z, reach, deep):
            coeff = COEFFS[SWEEPS - 1 - number]
            target = buffers[min(number, SWEEPS - 2)]
            source = buffers[number - 1]

            def of_group(ref, i, y, m):
                return jnp.broadcast_to(ref[z + i, y, pl.ds(m * groups + g, 1), :], (fields, LANES))

            def row(i, y):
                return [source[z + i, y, m] for m in range(SPLIT)]

            ys = range(HALO - reach, HALO + rows + reach)
            before = [row(i, ys[0] - 1) for i in range(deep)]
            here = [row(i, ys[0]) for i in range(deep)]
            for y in ys:
                after = [row(i, y + 1) for i in range(deep)]
                under, over = row(-1, y), row(deep, y)
                for i in range(deep):
                    lower = here[i - 1] if i else under
                    upper = here[i + 1] if i + 1 < deep else over
                    mid = here[i]
                    for m in range(SPLIT):
                        if m:
                            left = mid[m - 1]
                        else:
                            left = jnp.where(first_k, 0.0, pltpu.roll(mid[SPLIT - 1], 1, 1))
                        if m + 1 < SPLIT:
                            right = mid[m + 1]
                        else:
                            right = jnp.where(last_k, 0.0, pltpu.roll(mid[0], LANES - 1, 1))
                        near = (before[i][m] + after[i][m]) + (lower[m] + upper[m])
                        near = near + (left + right)
                        if number == SWEEPS - 1:
                            term = of_group(ro_ref, i, y, m) * near
                            acc_ref[z + i - HALO, y - HALO, m] += term
                            continue
                        base = mid[m] if number == 1 else buffers[0][z + i, y, m]
                        target[z + i, y, m] = of_group(r_ref, i, y, m) * near + coeff * base
                before, here = here, after

        for number in range(1, SWEEPS):
            reach = HALO - number

            def inner(pair, c, number=number, reach=reach):
                stage(number, HALO + 2 * pair, reach, 2)
                return c

            for d in range(1, reach + 1):
                stage(number, HALO - d, reach - d, 1)
                stage(number, HALO + depth - 1 + d, reach - d, 1)
            lax.fori_loop(0, depth // 2, inner, 0)
        return carry

    lax.fori_loop(0, groups, group, 0)

    lane_in, x_out = iota((SPLIT * LANES, LANES), 0), iota((SPLIT * LANES, LANES), 1) % NX
    gather = one_hot(x_out == SPLIT * (lane_in % STEPS) + lane_in // LANES)
    left = lane_halves((fields, LANES))
    factor = 4.0 / count * -0.5
    planes = []
    for z in range(depth):
        parts = [
            jnp.concatenate([acc_ref[z, y, m] for y in range(rows)], axis=0) for m in range(SPLIT)
        ]
        acc = jnp.concatenate(parts, axis=1)
        upper = acc.astype(jnp.bfloat16)
        lower = (acc - upper.astype(jnp.float32)).astype(jnp.bfloat16)
        total = bf16_dot(upper, gather) + bf16_dot(lower, gather)
        tiles = []
        for y in range(rows):
            tiles.append(total[y * fields : (y + 1) * fields])
        pieces = []
        for y in range(0, rows, 2):
            start = (y + LEAD) // 2 * depth + z
            value = parts_ref[pl.ds(start, fields, stride=parts_ref.shape[0] // fields), :]
            pieces.append(value + factor * jnp.where(left, tiles[y], tiles[y + 1]))
        planes.append(jnp.concatenate(pieces, axis=1))
    stacked = jnp.concatenate(planes, axis=0).astype(jnp.bfloat16)
    all_rows = depth * fields

    pick = one_hot(iota((all_rows, fields), 0) // depth == iota((all_rows, fields), 1))
    tile = one_hot(iota((fields, all_rows), 1) % fields == iota((fields, all_rows), 0))
    wide = bf16_dot(bf16_dot(pick, inverse_ref[...]).astype(jnp.bfloat16), tile)
    square = (all_rows, all_rows)
    same = iota(square, 0) % depth == iota(square, 1) // fields
    wide = jnp.where(same, wide, 0.0).astype(jnp.bfloat16)
    updated = bf16_dot(wide, stacked)

    m_ref[...] = jnp.zeros_like(m_ref)
    gram = jnp.zeros((fields, fields), jnp.float32)
    for z in range(depth):
        one = planes[z].astype(jnp.bfloat16)
        gram = gram + lax.dot_general(
            one, one, (((1,), (1,)), ((), ())), preferred_element_type=jnp.float32
        )
    m_ref[:, :fields] = gram
    pieces = rows * NX // LANES
    for p in range(fields):
        for t in range(pieces):
            out_ref[p, t] = updated[p * depth : (p + 1) * depth, t * LANES : (t + 1) * LANES]
        out_ref[p, pieces] = jnp.broadcast_to(m_ref[p : p + 1, :], (depth, LANES))


VMEM = pl.BlockSpec(memory_space=pltpu.VMEM)
SMEM = pl.BlockSpec(memory_space=pltpu.SMEM)


def in_vmem(*arrays):
    return [pltpu.with_memory_space_constraint(array, pltpu.VMEM) for array in arrays]


def in_hbm(array):
    return pltpu.with_memory_space_constraint(array, pltpu.HBM)


def swapped(to_a, to_b, axis):
    count = lax.axis_size(axis)
    pairs_a = [(i, i ^ 1) for i in range(count)]
    pairs_b = [(i, i + 1 if i % 2 else i - 1) for i in range(1, count - 1)]
    got_a = lax.ppermute(to_a, axis, pairs_a)
    got_b = lax.ppermute(to_b, axis, pairs_b)
    return got_a, got_b


def rows_plan(potentials, orbitals, energies, local_potential, inverse_factor):
    pots = lax.axis_size("pot")
    grids = lax.axis_size("grid")
    depth = potentials.shape[1]
    count, _, width = orbitals.shape
    rows = width // NX
    fields = pots
    half = count // 2
    f32, bf16 = jnp.float32, jnp.bfloat16
    shape = pltpu.VMEM
    tile = (half + fields, LANES)

    region = (depth + 2 * HALO, rows + 2 * HALO)
    pieces = width // LANES
    window = pieces + 2 * (LEAD * NX // LANES)
    limit = pltpu.CompilerParams(vmem_limit_bytes=VMEM_LIMIT)
    call = functools.partial(pl.pallas_call, compiler_params=limit)
    side = len(row_cells(depth))
    own, to_a, to_b = call(
        orbital_kernel,
        out_shape=[
            shape((depth, rows, half, LANES), bf16),
            shape((side, half, LANES), bf16),
            shape((side, half, LANES), bf16),
        ],
        in_specs=[VMEM],
        out_specs=[VMEM] * 3,
        scratch_shapes=[pltpu.VMEM((half * rows * depth, LANES), f32)],
        name="orbitals",
    )(in_hbm(orbitals))
    got_a, got_b = swapped(to_a, to_b, "pot")

    windows = call(
        window_kernel,
        out_shape=shape((pots, window, depth, LANES), f32),
        in_specs=[VMEM],
        out_specs=VMEM,
        name="windows",
    )(in_hbm(potentials))
    parts = lax.all_to_all(windows, "pot", 0, 0, tiled=True)
    parts = parts.reshape(pots * window * depth, LANES)

    inverse_diagonal = call(
        diagonal_kernel,
        out_shape=shape(region + (half, LANES), f32),
        in_specs=[SMEM, VMEM],
        out_specs=VMEM,
        scratch_shapes=[pltpu.VMEM((rows + 2 * LEAD, region[0] * SPLIT, LANES), f32)]
        + [pltpu.VMEM((rows // 2 + LEAD, local_potential.shape[0], LANES), f32)] * 3,
        name="diagonal",
    )(energies, local_potential)

    parts, inverse_diagonal = lax.optimization_barrier((parts, inverse_diagonal))
    edge = len(plane_cells(rows))
    up, down = call(
        send_kernel,
        out_shape=[shape((edge,) + tile, bf16)] * 2,
        in_specs=[VMEM] * 4,
        out_specs=[VMEM] * 2,
        name="sends",
    )(*in_vmem(parts, own, got_a, got_b))
    z_a, z_b = swapped(up, down, "grid")

    own_values = [
        shape(region + (half, LANES), f32),
        shape((half // SPLIT,) + region + (SPLIT, fields, LANES), f32),
        shape((depth, rows, SPLIT, fields, LANES), f32),
    ]
    prepared = call(
        prepare_kernel,
        out_shape=own_values,
        in_specs=[VMEM] * 5,
        out_specs=[VMEM] * 3,
        scratch_shapes=[pltpu.VMEM((rows, half, LANES), f32)],
        name="prepare",
    )(*in_vmem(parts, own, got_a, got_b, inverse_diagonal))
    sent, *_ = call(
        sweep_kernel,
        out_shape=[shape((fields, pieces + 1, depth, LANES), f32)] + own_values,
        in_specs=[VMEM] * 8,
        out_specs=[VMEM] * 4,
        scratch_shapes=[
            pltpu.VMEM(region + (SPLIT, fields, LANES), f32),
            pltpu.VMEM(region + (SPLIT, fields, LANES), f32),
            pltpu.VMEM((fields, LANES), f32),
        ],
        input_output_aliases={5: 1, 6: 2, 7: 3},
        name="sweeps",
    )(*in_vmem(parts, z_a, z_b, inverse_diagonal), inverse_factor, *in_vmem(*prepared))

    back = lax.all_to_all(sent, "pot", 0, 0, tiled=True)
    updated = back[:, :pieces].reshape(pots * pieces, depth, LANES).transpose(1, 0, 2)
    updated = updated.reshape(1, depth, pots * width)
    margins = jnp.sum(back[:, pieces], axis=0)
    step = 1
    while step < grids:
        margins = margins + lax.ppermute(margins, "grid", [(i, i ^ step) for i in range(grids)])
        step *= 2
    margins = margins[:1, :fields] / local_potential.size
    return updated, margins


def local(potentials, orbitals, energies, local_potential, inverse_factor):
    pots = lax.axis_size("pot")
    grids = lax.axis_size("grid")
    depth = potentials.shape[1]
    count, _, width = orbitals.shape
    fits = (
        potentials.shape[0] == 1
        and pots == 8
        and width % LANES == 0
        and LANES == 2 * NX
        and width // NX >= HALO
        and depth == 8
        and count % (BATCH * SPLIT) == 0
        and count // BATCH in (2, 4)
        and grids & (grids - 1) == 0
    )
    plan = rows_plan if fits else gathered_plan
    return plan(potentials, orbitals, energies, local_potential, inverse_factor)


def solution(mesh):
    in_specs = (P("pot", "grid", None), P(None, "grid", "pot"), P(), P(), P())
    out_specs = (P("pot", "grid", None), P("pot", None))
    return jax.shard_map(local, mesh=mesh, in_specs=in_specs, out_specs=out_specs, check_vma=False)
```

profile of v0, /device:TPU:0, one launch (start us, length us, event | category | flops | bytes accessed | tf_op | source)
XLA Modules:
  0.0 52.7 jit_solution(2978550652073858123)
XLA Ops:
  0.6 1.6 %windows.1 = f32[8,8,8,128]{3,2,1,0:T(8,128)} custom-call(f32[1,8,4096]{2,1,0:T(8,128)} %v_ref.1), custom_call_target="tpu_custom_call" | custom-call | tf_op jit(solution)/shard_map/windows/pallas_call | solution.py:547
  2.3 5.2 %all-to-all-start = ((f32[8,8,8,128]{3,2,1,0:T(8,128)}), f32[8,8,8,128]{3,2,1,0:T(8,128)S(1)}, u32[]{:S(2)}, u32[]{:S(2)}) async-start(f32[8,8,8,128]{3,2,1,0:T(8,128)} %windows.1), calls=%async_computation | async-start | bytes 524288 | tf_op jit(solution)/shard_map/all_to_all | solution.py:554
  7.5 1.9 %orbitals.1 = (bf16[8,8,16,128]{3,2,1,0:T(8,128)(2,1)S(1)}, bf16[24,16,128]{2,1,0:T(8,128)(2,1)S(1)}, bf16[24,16,128]{2,1,0:T(8,128)(2,1)S(1)}) custom-call(bf16[32,8,512]{2,1,0:T(8,128)(2,1)} %orb_ref.1), custom_call_target="tpu_custom_call" | custom-call | tf_op jit(solution)/shard_map/orbitals/pallas_call | solution.py:533
  9.4 0.6 %collective-permute-start = (bf16[24,16,128]{2,1,0:T(8,128)(2,1)S(1)}, bf16[24,16,128]{2,1,0:T(8,128)(2,1)S(1)}, u32[]{:S(2)}, u32[]{:S(2)}) collective-permute-start(bf16[24,16,128]{2,1,0:T(8,128)(2,1)S(1)} %get-tuple-element.15), channel_id=1, source_target_pairs={{0,4},{4,0},{8,12},{12,8},{16,20},{20,16},{24,28},{28,24},{1,5},{5... | collective-permute-start | bytes 294920 | tf_op jit(solution)/shard_map/ppermute | solution.py:510
  9.9 0.7 %collective-permute-start.1 = (bf16[24,16,128]{2,1,0:T(8,128)(2,1)S(1)}, bf16[24,16,128]{2,1,0:T(8,128)(2,1)S(1)}, u32[]{:S(2)}, u32[]{:S(2)}) collective-permute-start(bf16[24,16,128]{2,1,0:T(8,128)(2,1)S(1)} %get-tuple-element.16), channel_id=1, source_target_pairs={{4,8},{8,4},{12,16},{16,12},{20,24},{24,20},{5,9},{9,5},{13,17},{1... | collective-permute-start | bytes 294920 | tf_op jit(solution)/shard_map/ppermute | solution.py:511
  10.6 0.0 copy-start
  10.6 1.0 %copy-done = f32[32,4096]{1,0:T(8,128)S(1)} copy-done((f32[32,4096]{1,0:T(8,128)S(1)}, f32[32,4096]{1,0:T(8,128)}, u32[]{:S(2)}) %copy-start) | copy-done | bytes 524312
  11.7 0.7 %copy-done.2 = f32[32]{0:T(128)S(1)} copy-done((f32[32]{0:T(128)S(1)}, f32[32]{0:T(128)}, u32[]{:S(2)}) %copy-start.2) | copy-done | bytes 152
  12.3 1.5 %diagonal.1.r_ref = f32[14,14,16,128]{3,2,1,0:T(8,128)S(1)} custom-call(f32[32]{0:T(128)S(1)} %copy-done.2, f32[32,4096]{1,0:T(8,128)S(1)} %copy-done), custom_call_target="tpu_custom_call" | custom-call | tf_op jit(solution)/shard_map/diagonal/pallas_call | solution.py:557
  13.8 0.0 copy-start.1
  13.8 0.5 %all-to-all-done = f32[8,8,8,128]{3,2,1,0:T(8,128)S(1)} async-done(((f32[8,8,8,128]{3,2,1,0:T(8,128)}), f32[8,8,8,128]{3,2,1,0:T(8,128)S(1)}, u32[]{:S(2)}, u32[]{:S(2)}) %all-to-all-start) | async-done | bytes 262176 | tf_op jit(solution)/shard_map/all_to_all | solution.py:554
  14.4 0.2 sends.1
  14.5 1.6 %collective-permute-start.2 = (bf16[30,24,128]{2,1,0:T(8,128)(2,1)S(1)}, bf16[30,24,128]{2,1,0:T(8,128)(2,1)S(1)}, u32[]{:S(2)}, u32[]{:S(2)}) collective-permute-start(bf16[30,24,128]{2,1,0:T(8,128)(2,1)S(1)} %get-tuple-element.17), channel_id=1, source_target_pairs={{0,1},{1,0},{2,3},{3,2},{4,5},{5,4},{6,7},{7,6},{8,9},{9,8},{10,11... | collective-permute-start | bytes 552968 | tf_op jit(solution)/shard_map/ppermute | solution.py:510
  16.2 0.7 %collective-permute-start.3 = (bf16[30,24,128]{2,1,0:T(8,128)(2,1)S(1)}, bf16[30,24,128]{2,1,0:T(8,128)(2,1)S(1)}, u32[]{:S(2)}, u32[]{:S(2)}) collective-permute-start(bf16[30,24,128]{2,1,0:T(8,128)(2,1)S(1)} %get-tuple-element.18), channel_id=1, source_target_pairs={{1,2},{2,1},{5,6},{6,5},{9,10},{10,9},{13,14},{14,13},{17,18},{18,... | collective-permute-start | bytes 552968 | tf_op jit(solution)/shard_map/ppermute | solution.py:511
  16.9 2.2 %prepare.1 = (f32[14,14,16,128]{3,2,1,0:T(8,128)S(1)}, f32[4,14,14,4,8,128]{5,4,3,2,1,0:T(8,128)S(1)}, f32[8,8,4,8,128]{4,3,2,1,0:T(8,128)S(1)}) custom-call(f32[512,128]{1,0:T(8,128)S(1)} %bitcast.7, bf16[8,8,16,128]{3,2,1,0:T(8,128)(2,1)S(1)} %get-tuple-element.14.own_ref, bf16[24,16,128]{2,1,0:T(8,128)(2,1)S(1)} %collective-permute-done.a_ref, ...), custom_call_target="tpu_custom_call" | custom-call | tf_op jit(solution)/shard_map/prepare/pallas_call | solution.py:583
  19.1 1.5 %collective-permute-done.2.a_ref = bf16[30,24,128]{2,1,0:T(8,128)(2,1)S(1)} collective-permute-done((bf16[30,24,128]{2,1,0:T(8,128)(2,1)S(1)}, bf16[30,24,128]{2,1,0:T(8,128)(2,1)S(1)}, u32[]{:S(2)}, u32[]{:S(2)}) %collective-permute-start.2) | collective-permute-done | bytes 184352 | tf_op jit(solution)/shard_map/ppermute | solution.py:510
  20.6 9.2 %sweeps.1 = (f32[8,5,8,128]{3,2,1,0:T(8,128)S(1)}, f32[14,14,16,128]{3,2,1,0:T(8,128)S(1)}, f32[4,14,14,4,8,128]{5,4,3,2,1,0:T(8,128)S(1)}, f32[8,8,4,8,128]{4,3,2,1,0:T(8,128)S(1)}) custom-call(f32[512,128]{1,0:T(8,128)S(1)} %bitcast.8, ...), custom_call_target="tpu_custom_call", output_to_operand_aliasing={{1}: (5, {}), {2}: (6, {}), {3}: (7, {})} | custom-call | tf_op jit(solution)/shard_map/sweeps/pallas_call | solution.py:591
  29.8 11.4 %all_to_all.10 = f32[8,5,8,128]{3,2,1,0:T(8,128)S(1)} all-to-all(f32[8,5,8,128]{3,2,1,0:T(8,128)S(1)} %get-tuple-element.23), channel_id=1, replica_groups=mesh['pot'=8,'grid'=4] {'pot'}, dimensions={0} | all-to-all | bytes 327680 | tf_op jit(solution)/shard_map/all_to_all | solution.py:605
  41.3 4.6 %collective-permute-start.4 = (f32[8,128]{1,0:T(8,128)S(1)}, f32[8,128]{1,0:T(8,128)S(1)}, u32[]{:S(2)}, u32[]{:S(2)}) collective-permute-start(f32[8,128]{1,0:T(8,128)S(1)} %slice_reduce_fusion), channel_id=1, source_target_pairs={{0,1},{1,0},{2,3},{3,2},{4,5},{5,4},{6,7},{7,6},{8,9},{9,8},{10,11... | collective-permute-start | bytes 12296 | tf_op jit(solution)/shard_map/ppermute | solution.py:611
  45.9 1.6 %collective-permute-done.4 = f32[8,128]{1,0:T(8,128)S(1)} collective-permute-done((f32[8,128]{1,0:T(8,128)S(1)}, f32[8,128]{1,0:T(8,128)S(1)}, u32[]{:S(2)}, u32[]{:S(2)}) %collective-permute-start.4) | collective-permute-done | bytes 4128 | tf_op jit(solution)/shard_map/ppermute | solution.py:611
  47.4 3.2 %collective-permute-start.5 = (f32[8,128]{1,0:T(8,128)S(1)}, f32[8,128]{1,0:T(8,128)S(1)}, u32[]{:S(2)}, u32[]{:S(2)}) collective-permute-start(f32[8,128]{1,0:T(8,128)S(1)} %add.6), channel_id=1, source_target_pairs={{0,2},{1,3},{2,0},{3,1},{4,6},{5,7},{6,4},{7,5},{8,10},{9,11},{10,... | collective-permute-start | bytes 12296 | tf_op jit(solution)/shard_map/ppermute | solution.py:611
  50.6 0.7 %slice.12 = f32[8,4,8,128]{3,2,1,0:T(8,128)} slice(f32[8,5,8,128]{3,2,1,0:T(8,128)S(1)} %all_to_all.10), slice={[0:8], [0:4], [0:8], [0:128]} | slice | bytes 262144 | tf_op jit(solution)/shard_map/slice | solution.py:606
  51.3 0.9 %collective-permute-done.5 = f32[8,128]{1,0:T(8,128)S(1)} collective-permute-done((f32[8,128]{1,0:T(8,128)S(1)}, f32[8,128]{1,0:T(8,128)S(1)}, u32[]{:S(2)}, u32[]{:S(2)}) %collective-permute-start.5) | collective-permute-done | bytes 4128 | tf_op jit(solution)/shard_map/ppermute | solution.py:611
  52.2 0.5 slice_multiply_fusion
  (8 shorter events, 0.0 us)
Async XLA Ops:
  2.3 12.1 %all-to-all-start = ((f32[8,8,8,128]{3,2,1,0:T(8,128)}), f32[8,8,8,128]{3,2,1,0:T(8,128)S(1)}, u32[]{:S(2)}, u32[]{:S(2)}) async-start(f32[8,8,8,128]{3,2,1,0:T(8,128)} %windows.1), calls=%async_computation | async-start | bytes 524288 | tf_op jit(solution)/shard_map/all_to_all | solution.py:554
  9.4 5.0 %collective-permute-start = (bf16[24,16,128]{2,1,0:T(8,128)(2,1)S(1)}, bf16[24,16,128]{2,1,0:T(8,128)(2,1)S(1)}, u32[]{:S(2)}, u32[]{:S(2)}) collective-permute-start(bf16[24,16,128]{2,1,0:T(8,128)(2,1)S(1)} %get-tuple-element.15), channel_id=1, source_target_pairs={{0,4},{4,0},{8,12},{12,8},{16,20},{20,16},{24,28},{28,24},{1,5},{5... | collective-permute-start | bytes 294920 | tf_op jit(solution)/shard_map/ppermute | solution.py:510
  9.9 4.4 %collective-permute-start.1 = (bf16[24,16,128]{2,1,0:T(8,128)(2,1)S(1)}, bf16[24,16,128]{2,1,0:T(8,128)(2,1)S(1)}, u32[]{:S(2)}, u32[]{:S(2)}) collective-permute-start(bf16[24,16,128]{2,1,0:T(8,128)(2,1)S(1)} %get-tuple-element.16), channel_id=1, source_target_pairs={{4,8},{8,4},{12,16},{16,12},{20,24},{24,20},{5,9},{9,5},{13,17},{1... | collective-permute-start | bytes 294920 | tf_op jit(solution)/shard_map/ppermute | solution.py:511
  10.6 1.0 %copy-start = (f32[32,4096]{1,0:T(8,128)S(1)}, f32[32,4096]{1,0:T(8,128)}, u32[]{:S(2)}) copy-start(f32[32,4096]{1,0:T(8,128)} %lp_ref.1) | copy-start | bytes 1572868
  11.7 0.7 %copy-start.2 = (f32[32]{0:T(128)S(1)}, f32[32]{0:T(128)}, u32[]{:S(2)}) copy-start(f32[32]{0:T(128)} %energy_ref.1) | copy-start | bytes 388
  13.8 6.8 %copy-start.1 = (bf16[8,8]{1,0:T(8,128)(2,1)S(1)}, bf16[8,8]{1,0:T(8,128)(2,1)}, u32[]{:S(2)}) copy-start(bf16[8,8]{1,0:T(8,128)(2,1)} %inverse_ref.1) | copy-start | bytes 388
  14.5 6.1 %collective-permute-start.2 = (bf16[30,24,128]{2,1,0:T(8,128)(2,1)S(1)}, bf16[30,24,128]{2,1,0:T(8,128)(2,1)S(1)}, u32[]{:S(2)}, u32[]{:S(2)}) collective-permute-start(bf16[30,24,128]{2,1,0:T(8,128)(2,1)S(1)} %get-tuple-element.17), channel_id=1, source_target_pairs={{0,1},{1,0},{2,3},{3,2},{4,5},{5,4},{6,7},{7,6},{8,9},{9,8},{10,11... | collective-permute-start | bytes 552968 | tf_op jit(solution)/shard_map/ppermute | solution.py:510
  16.2 4.4 %collective-permute-start.3 = (bf16[30,24,128]{2,1,0:T(8,128)(2,1)S(1)}, bf16[30,24,128]{2,1,0:T(8,128)(2,1)S(1)}, u32[]{:S(2)}, u32[]{:S(2)}) collective-permute-start(bf16[30,24,128]{2,1,0:T(8,128)(2,1)S(1)} %get-tuple-element.18), channel_id=1, source_target_pairs={{1,2},{2,1},{5,6},{6,5},{9,10},{10,9},{13,14},{14,13},{17,18},{18,... | collective-permute-start | bytes 552968 | tf_op jit(solution)/shard_map/ppermute | solution.py:511
  41.3 6.2 %collective-permute-start.4 = (f32[8,128]{1,0:T(8,128)S(1)}, f32[8,128]{1,0:T(8,128)S(1)}, u32[]{:S(2)}, u32[]{:S(2)}) collective-permute-start(f32[8,128]{1,0:T(8,128)S(1)} %slice_reduce_fusion), channel_id=1, source_target_pairs={{0,1},{1,0},{2,3},{3,2},{4,5},{5,4},{6,7},{7,6},{8,9},{9,8},{10,11... | collective-permute-start | bytes 12296 | tf_op jit(solution)/shard_map/ppermute | solution.py:611
  47.4 4.8 %collective-permute-start.5 = (f32[8,128]{1,0:T(8,128)S(1)}, f32[8,128]{1,0:T(8,128)S(1)}, u32[]{:S(2)}, u32[]{:S(2)}) collective-permute-start(f32[8,128]{1,0:T(8,128)S(1)} %add.6), channel_id=1, source_target_pairs={{0,2},{1,3},{2,0},{3,1},{4,6},{5,7},{6,4},{7,5},{8,10},{9,11},{10,... | collective-permute-start | bytes 12296 | tf_op jit(solution)/shard_map/ppermute | solution.py:611
where the time goes:
time: 53.1 us; the launch traced here: 52.7 us
  Pallas kernels  16.6 us (31%)
  starting transfers between devices  16.5 us (31%)
  blocking collectives  11.4 us (21%)
  waiting for transfers between devices  4.57 us (9%)
  local copies, waits for them, and re-layouts  2.36 us (4%)
  between operations  0.7 us (1%)
    all_to_all x1, blocking collectives, rows_plan(): back = lax.all_to_all(sent, 'pot', 0, 0, tiled=True)  11.4 us
    pallas_call x1, Pallas kernels, rows_plan(): call(sweep_kernel, out_shape=[shape((fields, pieces + 1, depth, LANES), f...  9.22 us
    ppermute x2, starting transfers between devices, rows_plan(): lax.ppermute(margins, 'grid', [(i, i ^ step) for i in range(grids)])  7.78 us
    all_to_all x1, starting transfers between devices, rows_plan(): parts = lax.all_to_all(windows, 'pot', 0, 0, tiled=True)  5.2 us
    ppermute x2, waiting for transfers between devices, rows_plan(): lax.ppermute(margins, 'grid', [(i, i ^ step) for i in range(grids)])  2.5 us
    pallas_call x1, Pallas kernels, rows_plan(): call(prepare_kernel, out_shape=own_values, in_specs=[VMEM] * 5, out_specs...  2.22 us
    ppermute x2, starting transfers between devices, swapped(): got_a = lax.ppermute(to_a, axis, pairs_a)  2.21 us
    pallas_call x1, Pallas kernels, rows_plan(): call(orbital_kernel, out_shape=[shape((depth, rows, half, LANES), bf16),...  1.91 us
  transfers between devices with their start and end apart: 7, of which 4 were waited for; matrix products, arithmetic and copies ran while one was open for 1% of the time, Pallas kernels for 11%

commit v1 on v0

--- a/solution.py
+++ b/solution.py
@@ -16,6 +16,12 @@
     sum(math.comb(n, m) * (1.0 - DAMPING) ** (n - m) for n in range(m, SWEEPS))
     for m in range(SWEEPS)
 )
+START = COEFFS[SWEEPS - 2]
+WEIGHTS = [COEFFS[SWEEPS - 2 - n] / START for n in range(SWEEPS - 2)]
+INNER = tuple(
+    ((1.0 / START) if n == 0 else WEIGHTS[n - 1]) / WEIGHTS[n] for n in range(SWEEPS - 2)
+)
+LAST = WEIGHTS[-1]
 HALO = SWEEPS - 1
 LEAD = HALO + HALO % 2
 LANES = 128
@@ -124,7 +130,35 @@
 BATCH = LANES // STEPS
 
 
-def orbital_kernel(orb_ref, own_ref, a_ref, b_ref, s_ref):
+def first_kernel(
+    fields_ref, orbitals_ref, windows_ref, own_ref, a_ref, b_ref, wide_ref, orb_ref, s_ref, sem_ref
+):
+    receivers, window = windows_ref.shape[:2]
+    total = fields_ref.shape[0]
+    ahead = LEAD * NX // LANES
+    fetch = pltpu.make_async_copy(fields_ref, wide_ref.at[pl.ds(ahead, total)], sem_ref.at[0])
+    fetch_orbitals = pltpu.make_async_copy(orbitals_ref, orb_ref, sem_ref.at[1])
+    fetch.start()
+    fetch_orbitals.start()
+    for t in range(ahead):
+        wide_ref[t] = jnp.zeros(wide_ref.shape[1:], wide_ref.dtype)
+        wide_ref[ahead + total + t] = jnp.zeros(wide_ref.shape[1:], wide_ref.dtype)
+    fetch.wait()
+    copies = [
+        pltpu.make_async_copy(
+            wide_ref.at[pl.ds(p * (total // receivers), window)], windows_ref.at[p], sem_ref.at[2 + p]
+        )
+        for p in range(receivers)
+    ]
+    for copy in copies:
+        copy.start()
+    fetch_orbitals.wait()
+    relayout(orb_ref, own_ref, a_ref, b_ref, s_ref)
+    for copy in copies:
+        copy.wait()
+
+
+def relayout(orb_ref, own_ref, a_ref, b_ref, s_ref):
     count, depth, width = orb_ref.shape
     groups = count // BATCH
     rows = width // NX
@@ -164,20 +198,6 @@
         b_ref[at] = own_ref[z, jnp.where(even, d - 1, rows - d)]
 
 
-def window_kernel(v_ref, out_ref):
-    receivers, pieces = out_ref.shape[:2]
-    total = v_ref.shape[2] // LANES
-    stride = total // receivers
-    ahead = LEAD * NX // LANES
-    for p in range(receivers):
-        for t in range(pieces):
-            at = p * stride + t - ahead
-            if 0 <= at < total:
-                out_ref[p, t] = v_ref[0, :, at * LANES : (at + 1) * LANES]
-            else:
-                out_ref[p, t] = jnp.zeros(out_ref.shape[2:], out_ref.dtype)
-
-
 def two_parts(value, y):
     left = lane_halves(value.shape)
     upper = value.astype(jnp.bfloat16).astype(jnp.float32)
@@ -279,7 +299,7 @@
         for y in range(-HALO, rows + HALO):
             yg = y_base + y
             inside = z_inside & (yg >= 0) & (yg < rows_all)
-            scale = jnp.where(inside, 0.5 * DAMPING, 0.0)
+            scale = jnp.where(inside, INNER[0] * 0.5 * DAMPING, 0.0)
             for part in range(size // SUBLANES):
                 values = [
                     lp_ref2[y + LEAD, pl.ds(zi * SPLIT + part * ms + i, 1), :] for i in range(ms)
@@ -300,10 +320,10 @@
 def place(cells, r_ref, ro_ref, first_ref, then=None):
     fields = first_ref.shape[4]
     packed = jnp.concatenate([parts for _, parts, _, _ in cells], axis=0).astype(jnp.bfloat16)
-    values = bf16_dot(packed, spread_matrix())
+    values = (START / LAST) * bf16_dot(packed, spread_matrix())
     for number, (orbitals, _, z, y) in enumerate(cells):
         zi, yi = z + HALO, y + HALO
-        o = -2.0 * orbitals.astype(jnp.float32)
+        o = (-2.0 * START * LAST) * orbitals.astype(jnp.float32)
         ro = r_ref[zi, yi] * o
         ro_ref[zi, yi] = ro
         own = [
@@ -326,7 +346,7 @@
 
 
 def prepare_kernel(
-    parts_ref, own_ref, a_ref, b_ref, r_ref, ro_ref, first_ref, acc_ref, w_ref
+    parts_ref, own_ref, a_ref, b_ref, r_ref, ro_ref, first_ref, acc_ref, later_ref, w_ref
 ):
     depth, rows = own_ref.shape[:2]
     fields = first_ref.shape[4]
@@ -341,7 +361,7 @@
         while turn:
             weight = weight + pltpu.roll(weight, size - turn, 0)
             turn //= 2
-        w_ref[y] = COEFFS[0] * weight
+        w_ref[y] = (COEFFS[0] / (START * START * LAST)) * weight
         for m in range(SPLIT):
             at = m * groups
             w = jnp.broadcast_to(w_ref[y, at : at + 1], (fields, LANES))
@@ -358,9 +378,15 @@
 
     lax.fori_loop(0, depth, plane, 0)
 
+    def scaled(z, carry):
+        later_ref[z] = (INNER[-1] / INNER[0]) * r_ref[z]
+        return carry
+
+    lax.fori_loop(0, r_ref.shape[0], scaled, 0)
+
 
 def sweep_kernel(
-    parts_ref, a_ref, b_ref, r_ref, inverse_ref, ro_in, first_in, acc_in,
+    parts_ref, a_ref, b_ref, r_ref, later_ref, inverse_ref, ro_in, first_in, acc_in,
     out_ref, ro_ref, first_ref, acc_ref, x_ref, y_ref, m_ref,
 ):
     depth, rows = acc_ref.shape[:2]
@@ -387,9 +413,9 @@
 
     def group(g, carry):
         buffers = (first_ref.at[g], x_ref, y_ref)
+        scales = (r_ref, later_ref)
 
         def stage(number, z, reach, deep):
-            coeff = COEFFS[SWEEPS - 1 - number]
             target = buffers[min(number, SWEEPS - 2)]
             source = buffers[number - 1]
 
@@ -425,7 +451,7 @@
                             acc_ref[z + i - HALO, y - HALO, m] += term
                             continue
                         base = mid[m] if number == 1 else buffers[0][z + i, y, m]
-                        target[z + i, y, m] = of_group(r_ref, i, y, m) * near + coeff * base
+                        target[z + i, y, m] = of_group(scales[number - 1], i, y, m) * near + base
                 before, here = here, after
 
         for number in range(1, SWEEPS):
@@ -438,7 +464,7 @@
             for d in range(1, reach + 1):
                 stage(number, HALO - d, reach - d, 1)
                 stage(number, HALO + depth - 1 + d, reach - d, 1)
-            lax.fori_loop(0, depth // 2, inner, 0)
+            lax.fori_loop(0, depth // 2, inner, 0, unroll=2)
         return carry
 
     lax.fori_loop(0, groups, group, 0)
@@ -493,6 +519,7 @@
 
 VMEM = pl.BlockSpec(memory_space=pltpu.VMEM)
 SMEM = pl.BlockSpec(memory_space=pltpu.SMEM)
+ANY = pl.BlockSpec(memory_space=pl.ANY)
 
 
 def in_vmem(*arrays):
@@ -530,27 +557,26 @@
     limit = pltpu.CompilerParams(vmem_limit_bytes=VMEM_LIMIT)
     call = functools.partial(pl.pallas_call, compiler_params=limit)
     side = len(row_cells(depth))
-    own, to_a, to_b = call(
-        orbital_kernel,
+    fields_tiles = potentials.reshape(depth, pots * pieces, LANES).transpose(1, 0, 2)
+    windows, own, to_a, to_b = call(
+        first_kernel,
         out_shape=[
+            pltpu.HBM((pots, window, depth, LANES), f32),
             shape((depth, rows, half, LANES), bf16),
             shape((side, half, LANES), bf16),
             shape((side, half, LANES), bf16),
         ],
-        in_specs=[VMEM],
-        out_specs=[VMEM] * 3,
-        scratch_shapes=[pltpu.VMEM((half * rows * depth, LANES), f32)],
-        name="orbitals",
-    )(in_hbm(orbitals))
+        in_specs=[ANY] * 2,
+        out_specs=[ANY] + [VMEM] * 3,
+        scratch_shapes=[
+            pltpu.VMEM((pots * pieces + window - pieces, depth, LANES), f32),
+            pltpu.VMEM(orbitals.shape, bf16),
+            pltpu.VMEM((half * rows * depth, LANES), f32),
+            pltpu.SemaphoreType.DMA((2 + pots,)),
+        ],
+        name="first",
+    )(in_hbm(fields_tiles), in_hbm(orbitals))
     got_a, got_b = swapped(to_a, to_b, "pot")
-
-    windows = call(
-        window_kernel,
-        out_shape=shape((pots, window, depth, LANES), f32),
-        in_specs=[VMEM],
-        out_specs=VMEM,
-        name="windows",
-    )(in_hbm(potentials))
     parts = lax.all_to_all(windows, "pot", 0, 0, tiled=True)
     parts = parts.reshape(pots * window * depth, LANES)
 
@@ -580,27 +606,27 @@
         shape((half // SPLIT,) + region + (SPLIT, fields, LANES), f32),
         shape((depth, rows, SPLIT, fields, LANES), f32),
     ]
-    prepared = call(
+    *prepared, later = call(
         prepare_kernel,
-        out_shape=own_values,
+        out_shape=own_values + own_values[:1],
         in_specs=[VMEM] * 5,
-        out_specs=[VMEM] * 3,
+        out_specs=[VMEM] * 4,
         scratch_shapes=[pltpu.VMEM((rows, half, LANES), f32)],
         name="prepare",
     )(*in_vmem(parts, own, got_a, got_b, inverse_diagonal))
     sent, *_ = call(
         sweep_kernel,
         out_shape=[shape((fields, pieces + 1, depth, LANES), f32)] + own_values,
-        in_specs=[VMEM] * 8,
+        in_specs=[VMEM] * 9,
         out_specs=[VMEM] * 4,
         scratch_shapes=[
             pltpu.VMEM(region + (SPLIT, fields, LANES), f32),
             pltpu.VMEM(region + (SPLIT, fields, LANES), f32),
             pltpu.VMEM((fields, LANES), f32),
         ],
-        input_output_aliases={5: 1, 6: 2, 7: 3},
+        input_output_aliases={6: 1, 7: 2, 8: 3},
         name="sweeps",
-    )(*in_vmem(parts, z_a, z_b, inverse_diagonal), inverse_factor, *in_vmem(*prepared))
+    )(*in_vmem(parts, z_a, z_b, inverse_diagonal, later), inverse_factor, *in_vmem(*prepared))
 
     back = lax.all_to_all(sent, "pot", 0, 0, tiled=True)
     updated = back[:, :pieces].reshape(pots * pieces, depth, LANES).transpose(1, 0, 2)

time: 53.1 us -> 51 us (0.960)
  blocking collectives: 11.4 us -> 8.32 us
  waiting for transfers between devices: 4.57 us -> 7.37 us
  Pallas kernels: 16.6 us -> 14.9 us
    all_to_all x1, blocking collectives: 11.4 us -> 8.32 us  [rows_plan(): back = lax.all_to_all(sent, 'pot', 0, 0, tiled=True)]
    all_to_all x1, waiting for transfers between devices: 0.53 us -> 2.51 us  [rows_plan(): parts = lax.all_to_all(windows, 'pot', 0, 0, tiled=True)]
    pallas_call x3 -> x2, Pallas kernels: 5.76 us -> 4.61 us  [the longest x1 2.52 us: rows_plan(): call(prepare_kernel, out_shape=own_values + own_values[:1], in_specs=[VME...]
    ppermute x2, waiting for transfers between devices: 1.53 us -> 2.35 us  [swapped(): got_a = lax.ppermute(to_a, axis, pairs_a)]
    pallas_call x1, Pallas kernels: 9.22 us -> 8.61 us  [rows_plan(): call(sweep_kernel, out_shape=[shape((fields, pieces + 1, depth, LANES), f...]
  transfers between devices with their start and end apart: 7 -> 7, of which waited for: 4 -> 4; matrix products, arithmetic and copies ran while one was open for 1% -> 1% of each run, Pallas kernels for 11% -> 8%
where the time goes in v1:
time: 51 us; the launch traced here: 50.6 us
  starting transfers between devices  16.5 us (32%)
  Pallas kernels  14.9 us (29%)
  blocking collectives  8.32 us (16%)
  waiting for transfers between devices  7.37 us (14%)
  local copies, waits for them, and re-layouts  2.36 us (5%)
  between operations  0.7 us (1%)
  other arithmetic  0.53 us (1%)
    pallas_call x1, Pallas kernels, rows_plan(): call(sweep_kernel, out_shape=[shape((fields, pieces + 1, depth, LANES), f...  8.61 us
    all_to_all x1, blocking collectives, rows_plan(): back = lax.all_to_all(sent, 'pot', 0, 0, tiled=True)  8.32 us
    ppermute x2, starting transfers between devices, rows_plan(): lax.ppermute(margins, 'grid', [(i, i ^ step) for i in range(grids)])  7.79 us
    all_to_all x1, starting transfers between devices, rows_plan(): parts = lax.all_to_all(windows, 'pot', 0, 0, tiled=True)  5.21 us
    pallas_call x1, Pallas kernels, rows_plan(): call(prepare_kernel, out_shape=own_values + own_values[:1], in_specs=[VME...  2.52 us
    all_to_all x1, waiting for transfers between devices, rows_plan(): parts = lax.all_to_all(windows, 'pot', 0, 0, tiled=True)  2.51 us
    ppermute x2, waiting for transfers between devices, rows_plan(): lax.ppermute(margins, 'grid', [(i, i ^ step) for i in range(grids)])  2.5 us
    ppermute x2, waiting for transfers between devices, swapped(): got_a = lax.ppermute(to_a, axis, pairs_a)  2.35 us
  transfers between devices with their start and end apart: 7, of which 4 were waited for; matrix products, arithmetic and copies ran while one was open for 1% of the time, Pallas kernels for 8%

profile of v1, /device:TPU:0, one launch (start us, length us, event | category | flops | bytes accessed | tf_op | source)
XLA Modules:
  0.0 50.6 jit_solution(6112462564241504001)
XLA Ops:
  0.6 2.1 %first.1 = (f32[8,8,8,128]{3,2,1,0:T(8,128)}, bf16[8,8,16,128]{3,2,1,0:T(8,128)(2,1)S(1)}, bf16[24,16,128]{2,1,0:T(8,128)(2,1)S(1)}, bf16[24,16,128]{2,1,0:T(8,128)(2,1)S(1)}) custom-call(f32[32,8,128]{2,1,0:T(8,128)} %bitcast.12, bf16[32,8,512]{2,1,0:T(8,128)(2,1)} %orbitals_ref.1), custom_call_target="tpu_custom_call" | custom-call | tf_op jit(solution)/shard_map/first/pallas_call | solution.py:561
  2.7 5.2 %all-to-all-start = ((f32[8,8,8,128]{3,2,1,0:T(8,128)}), f32[8,8,8,128]{3,2,1,0:T(8,128)S(1)}, u32[]{:S(2)}, u32[]{:S(2)}) async-start(f32[8,8,8,128]{3,2,1,0:T(8,128)} %get-tuple-element.15), calls=%async_computation | async-start | bytes 524288 | tf_op jit(solution)/shard_map/all_to_all | solution.py:580
  7.9 0.5 collective-permute-start
  8.4 0.7 %collective-permute-start.1 = (bf16[24,16,128]{2,1,0:T(8,128)(2,1)S(1)}, bf16[24,16,128]{2,1,0:T(8,128)(2,1)S(1)}, u32[]{:S(2)}, u32[]{:S(2)}) collective-permute-start(bf16[24,16,128]{2,1,0:T(8,128)(2,1)S(1)} %get-tuple-element.19), channel_id=1, source_target_pairs={{4,8},{8,4},{12,16},{16,12},{20,24},{24,20},{5,9},{9,5},{13,17},{1... | collective-permute-start | bytes 294920 | tf_op jit(solution)/shard_map/ppermute | solution.py:538
  9.1 0.0 copy-start
  9.1 1.0 %copy-done = f32[32,4096]{1,0:T(8,128)S(1)} copy-done((f32[32,4096]{1,0:T(8,128)S(1)}, f32[32,4096]{1,0:T(8,128)}, u32[]{:S(2)}) %copy-start) | copy-done | bytes 524312
  10.2 0.7 %copy-done.2 = f32[32]{0:T(128)S(1)} copy-done((f32[32]{0:T(128)S(1)}, f32[32]{0:T(128)}, u32[]{:S(2)}) %copy-start.2) | copy-done | bytes 152
  10.8 1.5 %diagonal.1.r_ref = f32[14,14,16,128]{3,2,1,0:T(8,128)S(1)} custom-call(f32[32]{0:T(128)S(1)} %copy-done.2, f32[32,4096]{1,0:T(8,128)S(1)} %copy-done), custom_call_target="tpu_custom_call" | custom-call | tf_op jit(solution)/shard_map/diagonal/pallas_call | solution.py:583
  12.3 0.0 copy-start.1
  12.3 2.5 %all-to-all-done = f32[8,8,8,128]{3,2,1,0:T(8,128)S(1)} async-done(((f32[8,8,8,128]{3,2,1,0:T(8,128)}), f32[8,8,8,128]{3,2,1,0:T(8,128)S(1)}, u32[]{:S(2)}, u32[]{:S(2)}) %all-to-all-start) | async-done | bytes 262176 | tf_op jit(solution)/shard_map/all_to_all | solution.py:580
  14.9 0.2 sends.1
  15.0 1.6 %collective-permute-start.2 = (bf16[30,24,128]{2,1,0:T(8,128)(2,1)S(1)}, bf16[30,24,128]{2,1,0:T(8,128)(2,1)S(1)}, u32[]{:S(2)}, u32[]{:S(2)}) collective-permute-start(bf16[30,24,128]{2,1,0:T(8,128)(2,1)S(1)} %get-tuple-element.20), channel_id=1, source_target_pairs={{0,1},{1,0},{2,3},{3,2},{4,5},{5,4},{6,7},{7,6},{8,9},{9,8},{10,11... | collective-permute-start | bytes 552968 | tf_op jit(solution)/shard_map/ppermute | solution.py:537
  16.7 0.7 %collective-permute-start.3 = (bf16[30,24,128]{2,1,0:T(8,128)(2,1)S(1)}, bf16[30,24,128]{2,1,0:T(8,128)(2,1)S(1)}, u32[]{:S(2)}, u32[]{:S(2)}) collective-permute-start(bf16[30,24,128]{2,1,0:T(8,128)(2,1)S(1)} %get-tuple-element.21), channel_id=1, source_target_pairs={{1,2},{2,1},{5,6},{6,5},{9,10},{10,9},{13,14},{14,13},{17,18},{18,... | collective-permute-start | bytes 552968 | tf_op jit(solution)/shard_map/ppermute | solution.py:538
  17.3 2.5 %prepare.1 = (f32[14,14,16,128]{3,2,1,0:T(8,128)S(1)}, f32[4,14,14,4,8,128]{5,4,3,2,1,0:T(8,128)S(1)}, f32[8,8,4,8,128]{4,3,2,1,0:T(8,128)S(1)}, f32[14,14,16,128]{3,2,1,0:T(8,128)S(1)}) custom-call(f32[512,128]{1,0:T(8,128)S(1)} %bitcast.10, bf16[8,8,16,128]{3,2,1,0:T(8,128)(2,1)S(1)} %get-tuple-element.17.own_ref, ...), custom_call_target="tpu_custom_call" | custom-call | tf_op jit(solution)/shard_map/prepare/pallas_call | solution.py:609
  19.9 2.3 %collective-permute-done.2.a_ref = bf16[30,24,128]{2,1,0:T(8,128)(2,1)S(1)} collective-permute-done((bf16[30,24,128]{2,1,0:T(8,128)(2,1)S(1)}, bf16[30,24,128]{2,1,0:T(8,128)(2,1)S(1)}, u32[]{:S(2)}, u32[]{:S(2)}) %collective-permute-start.2) | collective-permute-done | bytes 184352 | tf_op jit(solution)/shard_map/ppermute | solution.py:537
  22.2 0.0 collective-permute-done.3.b_ref
  22.2 8.6 %sweeps.1 = (f32[8,5,8,128]{3,2,1,0:T(8,128)S(1)}, f32[14,14,16,128]{3,2,1,0:T(8,128)S(1)}, f32[4,14,14,4,8,128]{5,4,3,2,1,0:T(8,128)S(1)}, f32[8,8,4,8,128]{4,3,2,1,0:T(8,128)S(1)}) custom-call(f32[512,128]{1,0:T(8,128)S(1)} %bitcast.11, ...), custom_call_target="tpu_custom_call", output_to_operand_aliasing={{1}: (6, {}), {2}: (7, {}), {3}: (8, {})} | custom-call | tf_op jit(solution)/shard_map/sweeps/pallas_call | solution.py:617
  30.8 8.3 %all_to_all.10 = f32[8,5,8,128]{3,2,1,0:T(8,128)S(1)} all-to-all(f32[8,5,8,128]{3,2,1,0:T(8,128)S(1)} %get-tuple-element.27), channel_id=1, replica_groups=mesh['pot'=8,'grid'=4] {'pot'}, dimensions={0} | all-to-all | bytes 327680 | tf_op jit(solution)/shard_map/all_to_all | solution.py:631
  39.2 4.6 %collective-permute-start.4 = (f32[8,128]{1,0:T(8,128)S(1)}, f32[8,128]{1,0:T(8,128)S(1)}, u32[]{:S(2)}, u32[]{:S(2)}) collective-permute-start(f32[8,128]{1,0:T(8,128)S(1)} %slice_reduce_fusion), channel_id=1, source_target_pairs={{0,1},{1,0},{2,3},{3,2},{4,5},{5,4},{6,7},{7,6},{8,9},{9,8},{10,11... | collective-permute-start | bytes 12296 | tf_op jit(solution)/shard_map/ppermute | solution.py:637
  43.8 1.6 %collective-permute-done.4 = f32[8,128]{1,0:T(8,128)S(1)} collective-permute-done((f32[8,128]{1,0:T(8,128)S(1)}, f32[8,128]{1,0:T(8,128)S(1)}, u32[]{:S(2)}, u32[]{:S(2)}) %collective-permute-start.4) | collective-permute-done | bytes 4128 | tf_op jit(solution)/shard_map/ppermute | solution.py:637
  45.3 3.2 %collective-permute-start.5 = (f32[8,128]{1,0:T(8,128)S(1)}, f32[8,128]{1,0:T(8,128)S(1)}, u32[]{:S(2)}, u32[]{:S(2)}) collective-permute-start(f32[8,128]{1,0:T(8,128)S(1)} %add.6), channel_id=1, source_target_pairs={{0,2},{1,3},{2,0},{3,1},{4,6},{5,7},{6,4},{7,5},{8,10},{9,11},{10,... | collective-permute-start | bytes 12296 | tf_op jit(solution)/shard_map/ppermute | solution.py:637
  48.5 0.7 %slice.12 = f32[8,4,8,128]{3,2,1,0:T(8,128)} slice(f32[8,5,8,128]{3,2,1,0:T(8,128)S(1)} %all_to_all.10), slice={[0:8], [0:4], [0:8], [0:128]} | slice | bytes 262144 | tf_op jit(solution)/shard_map/slice | solution.py:632
  49.2 0.9 %collective-permute-done.5 = f32[8,128]{1,0:T(8,128)S(1)} collective-permute-done((f32[8,128]{1,0:T(8,128)S(1)}, f32[8,128]{1,0:T(8,128)S(1)}, u32[]{:S(2)}, u32[]{:S(2)}) %collective-permute-start.5) | collective-permute-done | bytes 4128 | tf_op jit(solution)/shard_map/ppermute | solution.py:637
  50.1 0.5 %slice_multiply_fusion = f32[1,8]{1,0:T(1,128)} fusion(f32[8,128]{1,0:T(8,128)S(1)} %add.7), kind=kLoop, calls=%fused_computation.1 | loop fusion | flops 8 | bytes 64 | tf_op jit(solution)/shard_map/div | solution.py:639
  (7 shorter events, 0.0 us)
Async XLA Ops:
  2.7 12.1 %all-to-all-start = ((f32[8,8,8,128]{3,2,1,0:T(8,128)}), f32[8,8,8,128]{3,2,1,0:T(8,128)S(1)}, u32[]{:S(2)}, u32[]{:S(2)}) async-start(f32[8,8,8,128]{3,2,1,0:T(8,128)} %get-tuple-element.15), calls=%async_computation | async-start | bytes 524288 | tf_op jit(solution)/shard_map/all_to_all | solution.py:580
  7.9 6.9 %collective-permute-start = (bf16[24,16,128]{2,1,0:T(8,128)(2,1)S(1)}, bf16[24,16,128]{2,1,0:T(8,128)(2,1)S(1)}, u32[]{:S(2)}, u32[]{:S(2)}) collective-permute-start(bf16[24,16,128]{2,1,0:T(8,128)(2,1)S(1)} %get-tuple-element.18), channel_id=1, source_target_pairs={{0,4},{4,0},{8,12},{12,8},{16,20},{20,16},{24,28},{28,24},{1,5},{5... | collective-permute-start | bytes 294920 | tf_op jit(solution)/shard_map/ppermute | solution.py:537
  8.4 6.4 %collective-permute-start.1 = (bf16[24,16,128]{2,1,0:T(8,128)(2,1)S(1)}, bf16[24,16,128]{2,1,0:T(8,128)(2,1)S(1)}, u32[]{:S(2)}, u32[]{:S(2)}) collective-permute-start(bf16[24,16,128]{2,1,0:T(8,128)(2,1)S(1)} %get-tuple-element.19), channel_id=1, source_target_pairs={{4,8},{8,4},{12,16},{16,12},{20,24},{24,20},{5,9},{9,5},{13,17},{1... | collective-permute-start | bytes 294920 | tf_op jit(solution)/shard_map/ppermute | solution.py:538
  9.1 1.0 %copy-start = (f32[32,4096]{1,0:T(8,128)S(1)}, f32[32,4096]{1,0:T(8,128)}, u32[]{:S(2)}) copy-start(f32[32,4096]{1,0:T(8,128)} %lp_ref.1) | copy-start | bytes 1572868
  10.2 0.7 %copy-start.2 = (f32[32]{0:T(128)S(1)}, f32[32]{0:T(128)}, u32[]{:S(2)}) copy-start(f32[32]{0:T(128)} %energy_ref.1) | copy-start | bytes 388
  12.3 9.9 %copy-start.1 = (bf16[8,8]{1,0:T(8,128)(2,1)S(1)}, bf16[8,8]{1,0:T(8,128)(2,1)}, u32[]{:S(2)}) copy-start(bf16[8,8]{1,0:T(8,128)(2,1)} %inverse_ref.1) | copy-start | bytes 388
  15.0 7.2 %collective-permute-start.2 = (bf16[30,24,128]{2,1,0:T(8,128)(2,1)S(1)}, bf16[30,24,128]{2,1,0:T(8,128)(2,1)S(1)}, u32[]{:S(2)}, u32[]{:S(2)}) collective-permute-start(bf16[30,24,128]{2,1,0:T(8,128)(2,1)S(1)} %get-tuple-element.20), channel_id=1, source_target_pairs={{0,1},{1,0},{2,3},{3,2},{4,5},{5,4},{6,7},{7,6},{8,9},{9,8},{10,11... | collective-permute-start | bytes 552968 | tf_op jit(solution)/shard_map/ppermute | solution.py:537
  16.7 5.5 %collective-permute-start.3 = (bf16[30,24,128]{2,1,0:T(8,128)(2,1)S(1)}, bf16[30,24,128]{2,1,0:T(8,128)(2,1)S(1)}, u32[]{:S(2)}, u32[]{:S(2)}) collective-permute-start(bf16[30,24,128]{2,1,0:T(8,128)(2,1)S(1)} %get-tuple-element.21), channel_id=1, source_target_pairs={{1,2},{2,1},{5,6},{6,5},{9,10},{10,9},{13,14},{14,13},{17,18},{18,... | collective-permute-start | bytes 552968 | tf_op jit(solution)/shard_map/ppermute | solution.py:538
  39.2 6.2 %collective-permute-start.4 = (f32[8,128]{1,0:T(8,128)S(1)}, f32[8,128]{1,0:T(8,128)S(1)}, u32[]{:S(2)}, u32[]{:S(2)}) collective-permute-start(f32[8,128]{1,0:T(8,128)S(1)} %slice_reduce_fusion), channel_id=1, source_target_pairs={{0,1},{1,0},{2,3},{3,2},{4,5},{5,4},{6,7},{7,6},{8,9},{9,8},{10,11... | collective-permute-start | bytes 12296 | tf_op jit(solution)/shard_map/ppermute | solution.py:637
  45.3 4.8 %collective-permute-start.5 = (f32[8,128]{1,0:T(8,128)S(1)}, f32[8,128]{1,0:T(8,128)S(1)}, u32[]{:S(2)}, u32[]{:S(2)}) collective-permute-start(f32[8,128]{1,0:T(8,128)S(1)} %add.6), channel_id=1, source_target_pairs={{0,2},{1,3},{2,0},{3,1},{4,6},{5,7},{6,4},{7,5},{8,10},{9,11},{10,... | collective-permute-start | bytes 12296 | tf_op jit(solution)/shard_map/ppermute | solution.py:637

commit v2 on v1

--- a/solution.py
+++ b/solution.py
@@ -22,11 +22,12 @@
     ((1.0 / START) if n == 0 else WEIGHTS[n - 1]) / WEIGHTS[n] for n in range(SWEEPS - 2)
 )
 LAST = WEIGHTS[-1]
+assert SWEEPS == 4
 HALO = SWEEPS - 1
 LEAD = HALO + HALO % 2
 LANES = 128
 SUBLANES = 8
-VMEM_LIMIT = 24 << 20
+VMEM_LIMIT = 8 << 20
 
 
 def padded_2(block, sides, width):
@@ -131,7 +132,8 @@
 
 
 def first_kernel(
-    fields_ref, orbitals_ref, windows_ref, own_ref, a_ref, b_ref, wide_ref, orb_ref, s_ref, sem_ref
+    fields_ref, orbitals_ref, windows_ref, own_ref, a_ref, b_ref,
+    wide_ref, outer_ref, orb_ref, s_ref, sem_ref,
 ):
     receivers, window = windows_ref.shape[:2]
     total = fields_ref.shape[0]
@@ -144,12 +146,17 @@
         wide_ref[t] = jnp.zeros(wide_ref.shape[1:], wide_ref.dtype)
         wide_ref[ahead + total + t] = jnp.zeros(wide_ref.shape[1:], wide_ref.dtype)
     fetch.wait()
-    copies = [
-        pltpu.make_async_copy(
-            wide_ref.at[pl.ds(p * (total // receivers), window)], windows_ref.at[p], sem_ref.at[2 + p]
-        )
-        for p in range(receivers)
-    ]
+    copies = []
+    for p in range(receivers):
+        at = p * (total // receivers)
+        left = lane_halves(outer_ref.shape[1:])
+        outer_ref[p] = jnp.where(left, wide_ref[at + window], wide_ref[at])
+        inner = wide_ref.at[pl.ds(at + 1, window - 1)]
+        for source, target in (
+            (outer_ref.at[pl.ds(p, 1)], windows_ref.at[p, pl.ds(0, 1)]),
+            (inner, windows_ref.at[p, pl.ds(1, window - 1)]),
+        ):
+            copies.append(pltpu.make_async_copy(source, target, sem_ref.at[2 + len(copies)]))
     for copy in copies:
         copy.start()
     fetch_orbitals.wait()
@@ -198,6 +205,12 @@
         b_ref[at] = own_ref[z, jnp.where(even, d - 1, rows - d)]
 
 
+def of_fields(parts_ref, fields, depth, z, y):
+    pieces = parts_ref.shape[0] // (fields * depth)
+    start = (y + LEAD) // 2 % pieces * depth + z
+    return parts_ref[pl.ds(start, fields, stride=pieces * depth), :]
+
+
 def two_parts(value, y):
     left = lane_halves(value.shape)
     upper = value.astype(jnp.bfloat16).astype(jnp.float32)
@@ -219,13 +232,11 @@
 
 def send_kernel(v_ref, own_ref, a_ref, b_ref, to_a_ref, to_b_ref):
     depth, rows = own_ref.shape[:2]
-    pieces = rows * NX // LANES + 2 * (LEAD * NX // LANES)
-    fields = v_ref.shape[0] // (pieces * depth)
+    fields = lax.axis_size("pot")
     even = lax.rem(lax.axis_index("grid"), 2) == 0
 
     def tile_of(z, y):
-        start = (y + LEAD) // 2 * depth + z
-        value = v_ref[pl.ds(start, fields, stride=pieces * depth), :]
+        value = of_fields(v_ref, fields, depth, z, y)
         orbitals = row_tile(own_ref, a_ref, b_ref, z, y).astype(jnp.float32)
         return jnp.concatenate([orbitals, two_parts(value, y)], axis=0)
 
@@ -335,6 +346,52 @@
             then(z, y, o * ro, own)
 
 
+def sweep(number, g, z, reaches, rows, scale_ref, first_ref, source_ref, target_ref):
+    groups, fields = first_ref.shape[0], first_ref.shape[4]
+    deep = len(reaches)
+    before_number = number - 1
+    last = number == SWEEPS - 1
+    step = iota((fields, LANES), 1) % STEPS
+    first_k = step == 0
+    last_k = step == STEPS - 1
+
+    def row(i, y):
+        return [source_ref[g, z + i - before_number, y - before_number, m] for m in range(SPLIT)]
+
+    most = max(reaches)
+    ys = range(HALO - most, HALO + rows + most)
+    before = [row(i, ys[0] - 1) for i in range(deep)]
+    here = [row(i, ys[0]) for i in range(deep)]
+    for y in ys:
+        after = [row(i, y + 1) for i in range(deep)]
+        under, over = row(-1, y), row(deep, y)
+        for i in range(deep):
+            if not -reaches[i] <= y - HALO < rows + reaches[i]:
+                continue
+            lower = here[i - 1] if i else under
+            upper = here[i + 1] if i + 1 < deep else over
+            mid = here[i]
+            for m in range(SPLIT):
+                if m:
+                    left = mid[m - 1]
+                else:
+                    left = jnp.where(first_k, 0.0, pltpu.roll(mid[SPLIT - 1], 1, 1))
+                if m + 1 < SPLIT:
+                    right = mid[m + 1]
+                else:
+                    right = jnp.where(last_k, 0.0, pltpu.roll(mid[0], LANES - 1, 1))
+                near = (before[i][m] + after[i][m]) + (lower[m] + upper[m])
+                near = near + (left + right)
+                scale = scale_ref[z + i, y, pl.ds(m * groups + g, 1), :]
+                near = jnp.broadcast_to(scale, (fields, LANES)) * near
+                if last:
+                    target_ref[z + i - HALO, y - HALO, m] += near
+                else:
+                    base = mid[m] if number == 1 else first_ref[g, z + i, y, m]
+                    target_ref[g, z + i - number, y - number, m] = near + base
+        before, here = here, after
+
+
 def first_sweep(ro_ref, first_ref, z, y, values):
     groups = first_ref.shape[0]
     zi, yi = z + HALO, y + HALO
@@ -346,13 +403,13 @@
 
 
 def prepare_kernel(
-    parts_ref, own_ref, a_ref, b_ref, r_ref, ro_ref, first_ref, acc_ref, later_ref, w_ref
+    parts_ref, own_ref, a_ref, b_ref, r_ref, inverse_ref,
+    ro_ref, first_ref, x_ref, y_ref, acc_ref, later_ref, wide_ref, w_ref,
 ):
     depth, rows = own_ref.shape[:2]
     fields = first_ref.shape[4]
     size = ro_ref.shape[2]
     groups = size // SPLIT
-    pieces = parts_ref.shape[0] // (depth * fields)
 
     def first_term(z, y, weight, values):
         if not 0 <= y < rows:
@@ -370,8 +427,7 @@
     def plane(z, carry):
         cells = []
         for y in range(-HALO, rows + HALO):
-            start = (y + LEAD) // 2 * depth + z
-            value = parts_ref[pl.ds(start, fields, stride=pieces * depth), :]
+            value = of_fields(parts_ref, fields, depth, z, y)
             cells.append((row_tile(own_ref, a_ref, b_ref, z, y), two_parts(value, y), z, y))
         place(cells, r_ref, ro_ref, first_ref, first_term)
         return carry
@@ -384,10 +440,28 @@
 
     lax.fori_loop(0, r_ref.shape[0], scaled, 0)
 
+    all_rows = depth * fields
+
+    pick = one_hot(iota((all_rows, fields), 0) // depth == iota((all_rows, fields), 1))
+    tile = one_hot(iota((fields, all_rows), 1) % fields == iota((fields, all_rows), 0))
+    wide = bf16_dot(bf16_dot(pick, inverse_ref[...]).astype(jnp.bfloat16), tile)
+    square = (all_rows, all_rows)
+    same = iota(square, 0) % depth == iota(square, 1) // fields
+    wide_ref[...] = jnp.where(same, wide, 0.0).astype(jnp.bfloat16)
+
+    def group(g, carry):
+        for z in range(1, depth - 1, 2):
+            sweep(1, g, HALO + z, (HALO - 1,) * 2, rows, r_ref, first_ref, first_ref, x_ref)
+        for z in range(2, depth - 2, 2):
+            sweep(2, g, HALO + z, (HALO - 2,) * 2, rows, later_ref, first_ref, x_ref, y_ref)
+        return carry
+
+    lax.fori_loop(0, groups, group, 0)
+
 
 def sweep_kernel(
-    parts_ref, a_ref, b_ref, r_ref, later_ref, inverse_ref, ro_in, first_in, acc_in,
-    out_ref, ro_ref, first_ref, acc_ref, x_ref, y_ref, m_ref,
+    parts_ref, a_ref, b_ref, r_ref, later_ref, wide_ref, ro_in, first_in, x_in, y_in, acc_in,
+    out_ref, ro_ref, first_ref, x_ref, y_ref, acc_ref, m_ref,
 ):
     depth, rows = acc_ref.shape[:2]
     fields = first_ref.shape[4]
@@ -407,64 +481,24 @@
                     cells.append((tile[:size], tile[size:], z, y))
         place(cells, r_ref, ro_ref, first_ref)
 
-    step = iota((fields, LANES), 1) % STEPS
-    first_k = step == 0
-    last_k = step == STEPS - 1
+    top = HALO + depth
 
     def group(g, carry):
-        buffers = (first_ref.at[g], x_ref, y_ref)
-        scales = (r_ref, later_ref)
-
-        def stage(number, z, reach, deep):
-            target = buffers[min(number, SWEEPS - 2)]
-            source = buffers[number - 1]
-
-            def of_group(ref, i, y, m):
-                return jnp.broadcast_to(ref[z + i, y, pl.ds(m * groups + g, 1), :], (fields, LANES))
-
-            def row(i, y):
-                return [source[z + i, y, m] for m in range(SPLIT)]
-
-            ys = range(HALO - reach, HALO + rows + reach)
-            before = [row(i, ys[0] - 1) for i in range(deep)]
-            here = [row(i, ys[0]) for i in range(deep)]
-            for y in ys:
-                after = [row(i, y + 1) for i in range(deep)]
-                under, over = row(-1, y), row(deep, y)
-                for i in range(deep):
-                    lower = here[i - 1] if i else under
-                    upper = here[i + 1] if i + 1 < deep else over
-                    mid = here[i]
-                    for m in range(SPLIT):
-                        if m:
-                            left = mid[m - 1]
-                        else:
-                            left = jnp.where(first_k, 0.0, pltpu.roll(mid[SPLIT - 1], 1, 1))
-                        if m + 1 < SPLIT:
-                            right = mid[m + 1]
-                        else:
-                            right = jnp.where(last_k, 0.0, pltpu.roll(mid[0], LANES - 1, 1))
-                        near = (before[i][m] + after[i][m]) + (lower[m] + upper[m])
-                        near = near + (left + right)
-                        if number == SWEEPS - 1:
-                            term = of_group(ro_ref, i, y, m) * near
-                            acc_ref[z + i - HALO, y - HALO, m] += term
-                            continue
-                        base = mid[m] if number == 1 else buffers[0][z + i, y, m]
-                        target[z + i, y, m] = of_group(scales[number - 1], i, y, m) * near + base
-                before, here = here, after
-
-        for number in range(1, SWEEPS):
-            reach = HALO - number
-
-            def inner(pair, c, number=number, reach=reach):
-                stage(number, HALO + 2 * pair, reach, 2)
-                return c
-
-            for d in range(1, reach + 1):
-                stage(number, HALO - d, reach - d, 1)
-                stage(number, HALO + depth - 1 + d, reach - d, 1)
-            lax.fori_loop(0, depth // 2, inner, 0, unroll=2)
+        for z, reaches in (
+            (HALO - 2, (0,)),
+            (HALO - 1, (1, 2)),
+            (top - 1, (2, 1)),
+            (top + 1, (0,)),
+        ):
+            sweep(1, g, z, reaches, rows, r_ref, first_ref, first_ref, x_ref)
+        for z, reaches in ((HALO - 1, (0,)), (HALO, (1, 1)), (top - 2, (1, 1)), (top, (0,))):
+            sweep(2, g, z, reaches, rows, later_ref, first_ref, x_ref, y_ref)
+
+        def inner(pair, c):
+            sweep(3, g, HALO + 2 * pair, (0, 0), rows, ro_ref, first_ref, y_ref, acc_ref)
+            return c
+
+        lax.fori_loop(0, depth // 2, inner, 0, unroll=2)
         return carry
 
     lax.fori_loop(0, groups, group, 0)
@@ -487,20 +521,11 @@
             tiles.append(total[y * fields : (y + 1) * fields])
         pieces = []
         for y in range(0, rows, 2):
-            start = (y + LEAD) // 2 * depth + z
-            value = parts_ref[pl.ds(start, fields, stride=parts_ref.shape[0] // fields), :]
+            value = of_fields(parts_ref, fields, depth, z, y)
             pieces.append(value + factor * jnp.where(left, tiles[y], tiles[y + 1]))
         planes.append(jnp.concatenate(pieces, axis=1))
     stacked = jnp.concatenate(planes, axis=0).astype(jnp.bfloat16)
-    all_rows = depth * fields
-
-    pick = one_hot(iota((all_rows, fields), 0) // depth == iota((all_rows, fields), 1))
-    tile = one_hot(iota((fields, all_rows), 1) % fields == iota((fields, all_rows), 0))
-    wide = bf16_dot(bf16_dot(pick, inverse_ref[...]).astype(jnp.bfloat16), tile)
-    square = (all_rows, all_rows)
-    same = iota(square, 0) % depth == iota(square, 1) // fields
-    wide = jnp.where(same, wide, 0.0).astype(jnp.bfloat16)
-    updated = bf16_dot(wide, stacked)
+    updated = bf16_dot(wide_ref[...], stacked)
 
     m_ref[...] = jnp.zeros_like(m_ref)
     gram = jnp.zeros((fields, fields), jnp.float32)
@@ -553,7 +578,7 @@
 
     region = (depth + 2 * HALO, rows + 2 * HALO)
     pieces = width // LANES
-    window = pieces + 2 * (LEAD * NX // LANES)
+    window = pieces + 2 * (LEAD * NX // LANES) - 1
     limit = pltpu.CompilerParams(vmem_limit_bytes=VMEM_LIMIT)
     call = functools.partial(pl.pallas_call, compiler_params=limit)
     side = len(row_cells(depth))
@@ -569,10 +594,11 @@
         in_specs=[ANY] * 2,
         out_specs=[ANY] + [VMEM] * 3,
         scratch_shapes=[
-            pltpu.VMEM((pots * pieces + window - pieces, depth, LANES), f32),
+            pltpu.VMEM((pots * pieces + window + 1 - pieces, depth, LANES), f32),
+            pltpu.VMEM((pots, depth, LANES), f32),
             pltpu.VMEM(orbitals.shape, bf16),
             pltpu.VMEM((half * rows * depth, LANES), f32),
-            pltpu.SemaphoreType.DMA((2 + pots,)),
+            pltpu.SemaphoreType.DMA((2 + 2 * pots,)),
         ],
         name="first",
     )(in_hbm(fields_tiles), in_hbm(orbitals))
@@ -603,30 +629,29 @@
 
     own_values = [
         shape(region + (half, LANES), f32),
-        shape((half // SPLIT,) + region + (SPLIT, fields, LANES), f32),
+        *(
+            shape((half // SPLIT, region[0] - 2 * n, region[1] - 2 * n, SPLIT, fields, LANES), f32)
+            for n in range(SWEEPS - 1)
+        ),
         shape((depth, rows, SPLIT, fields, LANES), f32),
     ]
-    *prepared, later = call(
+    *prepared, later, wide = call(
         prepare_kernel,
-        out_shape=own_values + own_values[:1],
-        in_specs=[VMEM] * 5,
-        out_specs=[VMEM] * 4,
+        out_shape=own_values + own_values[:1] + [shape((depth * fields,) * 2, bf16)],
+        in_specs=[VMEM] * 6,
+        out_specs=[VMEM] * 7,
         scratch_shapes=[pltpu.VMEM((rows, half, LANES), f32)],
         name="prepare",
-    )(*in_vmem(parts, own, got_a, got_b, inverse_diagonal))
+    )(*in_vmem(parts, own, got_a, got_b, inverse_diagonal), in_hbm(inverse_factor))
     sent, *_ = call(
         sweep_kernel,
         out_shape=[shape((fields, pieces + 1, depth, LANES), f32)] + own_values,
-        in_specs=[VMEM] * 9,
-        out_specs=[VMEM] * 4,
-        scratch_shapes=[
-            pltpu.VMEM(region + (SPLIT, fields, LANES), f32),
-            pltpu.VMEM(region + (SPLIT, fields, LANES), f32),
-            pltpu.VMEM((fields, LANES), f32),
-        ],
-        input_output_aliases={6: 1, 7: 2, 8: 3},
+        in_specs=[VMEM] * 11,
+        out_specs=[VMEM] * 6,
+        scratch_shapes=[pltpu.VMEM((fields, LANES), f32)],
+        input_output_aliases={6 + i: 1 + i for i in range(5)},
         name="sweeps",
-    )(*in_vmem(parts, z_a, z_b, inverse_diagonal, later), inverse_factor, *in_vmem(*prepared))
+    )(*in_vmem(parts, z_a, z_b, inverse_diagonal, later, wide, *prepared))
 
     back = lax.all_to_all(sent, "pot", 0, 0, tiled=True)
     updated = back[:, :pieces].reshape(pots * pieces, depth, LANES).transpose(1, 0, 2)

time: 51 us -> 48.9 us (0.959)
  starting transfers between devices: 16.5 us -> 14.5 us
  blocking collectives: 8.32 us -> 9.8 us
  waiting for transfers between devices: 7.37 us -> 6.14 us
    pallas_call x1, Pallas kernels: 8.61 us -> 5.05 us  [rows_plan(): call(sweep_kernel, out_shape=[shape((fields, pieces + 1, depth, LANES), f...]
    pallas_call x1, Pallas kernels: 2.52 us -> 5.62 us  [rows_plan(): call(prepare_kernel, out_shape=own_values + own_values[:1] + [shape((dept...]
    ppermute x2, waiting for transfers between devices: 2.35 us -> 0.01 us  [swapped(): got_a = lax.ppermute(to_a, axis, pairs_a)]
    ppermute x2, starting transfers between devices: 7.79 us -> 5.87 us  [rows_plan(): lax.ppermute(margins, 'grid', [(i, i ^ step) for i in range(grids)])]
    all_to_all x1, blocking collectives: 8.32 us -> 9.8 us  [rows_plan(): back = lax.all_to_all(sent, 'pot', 0, 0, tiled=True)]
    ppermute x2, waiting for transfers between devices: 2.5 us -> 3.95 us  [rows_plan(): lax.ppermute(margins, 'grid', [(i, i ^ step) for i in range(grids)])]
    unnamed x6 -> x4, local copies, waits for them, and re-layouts: 1.7 us -> 1.69 us
  transfers between devices with their start and end apart: 7 -> 7, of which waited for: 4 -> 3; matrix products, arithmetic and copies ran while one was open for 1% -> 1% of each run, Pallas kernels for 8% -> 15%
where the time goes in v2:
time: 48.9 us; the launch traced here: 48.5 us
  starting transfers between devices  14.5 us (30%)
  Pallas kernels  14.4 us (29%)
  blocking collectives  9.8 us (20%)
  waiting for transfers between devices  6.14 us (13%)
  local copies, waits for them, and re-layouts  2.36 us (5%)
  between operations  0.71 us (1%)
  other arithmetic  0.53 us (1%)
    all_to_all x1, blocking collectives, rows_plan(): back = lax.all_to_all(sent, 'pot', 0, 0, tiled=True)  9.8 us
    ppermute x2, starting transfers between devices, rows_plan(): lax.ppermute(margins, 'grid', [(i, i ^ step) for i in range(grids)])  5.87 us
    pallas_call x1, Pallas kernels, rows_plan(): call(prepare_kernel, out_shape=own_values + own_values[:1] + [shape((dept...  5.62 us
    all_to_all x1, starting transfers between devices, rows_plan(): parts = lax.all_to_all(windows, 'pot', 0, 0, tiled=True)  5.21 us
    pallas_call x1, Pallas kernels, rows_plan(): call(sweep_kernel, out_shape=[shape((fields, pieces + 1, depth, LANES), f...  5.05 us
    ppermute x2, waiting for transfers between devices, rows_plan(): lax.ppermute(margins, 'grid', [(i, i ^ step) for i in range(grids)])  3.95 us
    all_to_all x1, waiting for transfers between devices, rows_plan(): parts = lax.all_to_all(windows, 'pot', 0, 0, tiled=True)  2.18 us
    pallas_call x1, Pallas kernels, rows_plan(): call(first_kernel, out_shape=[pltpu.HBM((pots, window, depth, LANES), f32...  2.17 us
  transfers between devices with their start and end apart: 7, of which 3 were waited for; matrix products, arithmetic and copies ran while one was open for 1% of the time, Pallas kernels for 15%

profile of v2, /device:TPU:0, one launch (start us, length us, event | category | flops | bytes accessed | tf_op | source)
XLA Modules:
  0.0 48.5 jit_solution(13186772141126997691)
XLA Ops:
  0.6 2.2 %first.1 = (f32[8,7,8,128]{3,2,1,0:T(8,128)}, bf16[8,8,16,128]{3,2,1,0:T(8,128)(2,1)S(1)}, bf16[24,16,128]{2,1,0:T(8,128)(2,1)S(1)}, bf16[24,16,128]{2,1,0:T(8,128)(2,1)S(1)}) custom-call(f32[32,8,128]{2,1,0:T(8,128)} %bitcast.12, bf16[32,8,512]{2,1,0:T(8,128)(2,1)} %orbitals_ref.1), custom_call_target="tpu_custom_call" | custom-call | tf_op jit(solution)/shard_map/first/pallas_call | solution.py:586
  2.8 5.2 %all-to-all-start = ((f32[8,7,8,128]{3,2,1,0:T(8,128)}), f32[8,7,8,128]{3,2,1,0:T(8,128)S(1)}, u32[]{:S(2)}, u32[]{:S(2)}) async-start(f32[8,7,8,128]{3,2,1,0:T(8,128)} %get-tuple-element.18), calls=%async_computation | async-start | bytes 458752 | tf_op jit(solution)/shard_map/all_to_all | solution.py:606
  8.0 0.5 %collective-permute-start = (bf16[24,16,128]{2,1,0:T(8,128)(2,1)S(1)}, bf16[24,16,128]{2,1,0:T(8,128)(2,1)S(1)}, u32[]{:S(2)}, u32[]{:S(2)}) collective-permute-start(bf16[24,16,128]{2,1,0:T(8,128)(2,1)S(1)} %get-tuple-element.21), channel_id=1, source_target_pairs={{0,4},{4,0},{8,12},{12,8},{16,20},{20,16},{24,28},{28,24},{1,5},{5... | collective-permute-start | bytes 294920 | tf_op jit(solution)/shard_map/ppermute | solution.py:562
  8.5 0.7 %collective-permute-start.1 = (bf16[24,16,128]{2,1,0:T(8,128)(2,1)S(1)}, bf16[24,16,128]{2,1,0:T(8,128)(2,1)S(1)}, u32[]{:S(2)}, u32[]{:S(2)}) collective-permute-start(bf16[24,16,128]{2,1,0:T(8,128)(2,1)S(1)} %get-tuple-element.22), channel_id=1, source_target_pairs={{4,8},{8,4},{12,16},{16,12},{20,24},{24,20},{5,9},{9,5},{13,17},{1... | collective-permute-start | bytes 294920 | tf_op jit(solution)/shard_map/ppermute | solution.py:563
  9.2 0.0 copy-start
  9.2 1.0 %copy-done = f32[32,4096]{1,0:T(8,128)S(1)} copy-done((f32[32,4096]{1,0:T(8,128)S(1)}, f32[32,4096]{1,0:T(8,128)}, u32[]{:S(2)}) %copy-start) | copy-done | bytes 524312
  10.2 0.7 %copy-done.1 = f32[32]{0:T(128)S(1)} copy-done((f32[32]{0:T(128)S(1)}, f32[32]{0:T(128)}, u32[]{:S(2)}) %copy-start.1) | copy-done | bytes 152
  10.9 1.5 %diagonal.1.r_ref = f32[14,14,16,128]{3,2,1,0:T(8,128)S(1)} custom-call(f32[32]{0:T(128)S(1)} %copy-done.1, f32[32,4096]{1,0:T(8,128)S(1)} %copy-done), custom_call_target="tpu_custom_call" | custom-call | tf_op jit(solution)/shard_map/diagonal/pallas_call | solution.py:609
  12.4 2.2 %all-to-all-done = f32[8,7,8,128]{3,2,1,0:T(8,128)S(1)} async-done(((f32[8,7,8,128]{3,2,1,0:T(8,128)}), f32[8,7,8,128]{3,2,1,0:T(8,128)S(1)}, u32[]{:S(2)}, u32[]{:S(2)}) %all-to-all-start) | async-done | bytes 229408 | tf_op jit(solution)/shard_map/all_to_all | solution.py:606
  14.6 0.0 collective-permute-done.1.b_ref
  14.6 0.1 sends.1
  14.7 1.6 %collective-permute-start.2 = (bf16[30,24,128]{2,1,0:T(8,128)(2,1)S(1)}, bf16[30,24,128]{2,1,0:T(8,128)(2,1)S(1)}, u32[]{:S(2)}, u32[]{:S(2)}) collective-permute-start(bf16[30,24,128]{2,1,0:T(8,128)(2,1)S(1)} %get-tuple-element.23), channel_id=1, source_target_pairs={{0,1},{1,0},{2,3},{3,2},{4,5},{5,4},{6,7},{7,6},{8,9},{9,8},{10,11... | collective-permute-start | bytes 552968 | tf_op jit(solution)/shard_map/ppermute | solution.py:562
  16.3 0.7 %collective-permute-start.3 = (bf16[30,24,128]{2,1,0:T(8,128)(2,1)S(1)}, bf16[30,24,128]{2,1,0:T(8,128)(2,1)S(1)}, u32[]{:S(2)}, u32[]{:S(2)}) collective-permute-start(bf16[30,24,128]{2,1,0:T(8,128)(2,1)S(1)} %get-tuple-element.24), channel_id=1, source_target_pairs={{1,2},{2,1},{5,6},{6,5},{9,10},{10,9},{13,14},{14,13},{17,18},{18,... | collective-permute-start | bytes 552968 | tf_op jit(solution)/shard_map/ppermute | solution.py:563
  17.0 5.6 %prepare.1 = (f32[14,14,16,128]{3,2,1,0:T(8,128)S(1)}, f32[4,14,14,4,8,128]{5,4,3,2,1,0:T(8,128)S(1)}, f32[4,12,12,4,8,128]{5,4,3,2,1,0:T(8,128)S(1)}, f32[4,10,...) custom-call(f32[448,128]{1,0:T(8,128)S(1)} %bitcast.10, ...), custom_call_target="tpu_custom_call" | custom-call | tf_op jit(solution)/shard_map/prepare/pallas_call | solution.py:638
  22.6 0.0 collective-permute-done.2.a_ref
  22.6 0.0 collective-permute-done.3.b_ref
  22.7 5.1 %sweeps.1 = (f32[8,5,8,128]{3,2,1,0:T(8,128)S(1)}, f32[14,14,16,128]{3,2,1,0:T(8,128)S(1)}, f32[4,14,14,4,8,128]{5,4,3,2,1,0:T(8,128)S(1)}, f32[4,12,12,4,8,128]...) custom-call(f32[448,128]{1,0:T(8,128)S(1)} %bitcast.11, ...), custom_call_target="tpu_custom_call", output_to_operand_aliasing={{1}: (6, {}), {2}: (7, {}), {3}: (8, {}), {4}: (9, {}), {5}... | custom-call | tf_op jit(solution)/shard_map/sweeps/pallas_call | solution.py:646
  27.7 9.8 %all_to_all.10 = f32[8,5,8,128]{3,2,1,0:T(8,128)S(1)} all-to-all(f32[8,5,8,128]{3,2,1,0:T(8,128)S(1)} %get-tuple-element.33), channel_id=1, replica_groups=mesh['pot'=8,'grid'=4] {'pot'}, dimensions={0} | all-to-all | bytes 327680 | tf_op jit(solution)/shard_map/all_to_all | solution.py:656
  37.5 4.4 %collective-permute-start.4 = (f32[8,128]{1,0:T(8,128)S(1)}, f32[8,128]{1,0:T(8,128)S(1)}, u32[]{:S(2)}, u32[]{:S(2)}) collective-permute-start(f32[8,128]{1,0:T(8,128)S(1)} %slice_reduce_fusion), channel_id=1, source_target_pairs={{0,1},{1,0},{2,3},{3,2},{4,5},{5,4},{6,7},{7,6},{8,9},{9,8},{10,11... | collective-permute-start | bytes 12296 | tf_op jit(solution)/shard_map/ppermute | solution.py:662
  41.9 1.6 %collective-permute-done.4 = f32[8,128]{1,0:T(8,128)S(1)} collective-permute-done((f32[8,128]{1,0:T(8,128)S(1)}, f32[8,128]{1,0:T(8,128)S(1)}, u32[]{:S(2)}, u32[]{:S(2)}) %collective-permute-start.4) | collective-permute-done | bytes 4128 | tf_op jit(solution)/shard_map/ppermute | solution.py:662
  43.5 1.5 %collective-permute-start.5 = (f32[8,128]{1,0:T(8,128)S(1)}, f32[8,128]{1,0:T(8,128)S(1)}, u32[]{:S(2)}, u32[]{:S(2)}) collective-permute-start(f32[8,128]{1,0:T(8,128)S(1)} %add.6), channel_id=1, source_target_pairs={{0,2},{1,3},{2,0},{3,1},{4,6},{5,7},{6,4},{7,5},{8,10},{9,11},{10,... | collective-permute-start | bytes 12296 | tf_op jit(solution)/shard_map/ppermute | solution.py:662
  45.0 0.7 %slice.12 = f32[8,4,8,128]{3,2,1,0:T(8,128)} slice(f32[8,5,8,128]{3,2,1,0:T(8,128)S(1)} %all_to_all.10), slice={[0:8], [0:4], [0:8], [0:128]} | slice | bytes 262144 | tf_op jit(solution)/shard_map/slice | solution.py:657
  45.6 2.4 %collective-permute-done.5 = f32[8,128]{1,0:T(8,128)S(1)} collective-permute-done((f32[8,128]{1,0:T(8,128)S(1)}, f32[8,128]{1,0:T(8,128)S(1)}, u32[]{:S(2)}, u32[]{:S(2)}) %collective-permute-start.5) | collective-permute-done | bytes 4128 | tf_op jit(solution)/shard_map/ppermute | solution.py:662
  48.0 0.5 %slice_multiply_fusion = f32[1,8]{1,0:T(1,128)} fusion(f32[8,128]{1,0:T(8,128)S(1)} %add.7), kind=kLoop, calls=%fused_computation.1 | loop fusion | flops 8 | bytes 64 | tf_op jit(solution)/shard_map/div | solution.py:664
  (5 shorter events, 0.0 us)
Async XLA Ops:
  2.8 11.8 %all-to-all-start = ((f32[8,7,8,128]{3,2,1,0:T(8,128)}), f32[8,7,8,128]{3,2,1,0:T(8,128)S(1)}, u32[]{:S(2)}, u32[]{:S(2)}) async-start(f32[8,7,8,128]{3,2,1,0:T(8,128)} %get-tuple-element.18), calls=%async_computation | async-start | bytes 458752 | tf_op jit(solution)/shard_map/all_to_all | solution.py:606
  8.0 6.6 %collective-permute-start = (bf16[24,16,128]{2,1,0:T(8,128)(2,1)S(1)}, bf16[24,16,128]{2,1,0:T(8,128)(2,1)S(1)}, u32[]{:S(2)}, u32[]{:S(2)}) collective-permute-start(bf16[24,16,128]{2,1,0:T(8,128)(2,1)S(1)} %get-tuple-element.21), channel_id=1, source_target_pairs={{0,4},{4,0},{8,12},{12,8},{16,20},{20,16},{24,28},{28,24},{1,5},{5... | collective-permute-start | bytes 294920 | tf_op jit(solution)/shard_map/ppermute | solution.py:562
  8.5 6.1 %collective-permute-start.1 = (bf16[24,16,128]{2,1,0:T(8,128)(2,1)S(1)}, bf16[24,16,128]{2,1,0:T(8,128)(2,1)S(1)}, u32[]{:S(2)}, u32[]{:S(2)}) collective-permute-start(bf16[24,16,128]{2,1,0:T(8,128)(2,1)S(1)} %get-tuple-element.22), channel_id=1, source_target_pairs={{4,8},{8,4},{12,16},{16,12},{20,24},{24,20},{5,9},{9,5},{13,17},{1... | collective-permute-start | bytes 294920 | tf_op jit(solution)/shard_map/ppermute | solution.py:563
  9.2 1.0 %copy-start = (f32[32,4096]{1,0:T(8,128)S(1)}, f32[32,4096]{1,0:T(8,128)}, u32[]{:S(2)}) copy-start(f32[32,4096]{1,0:T(8,128)} %lp_ref.1) | copy-start | bytes 1572868
  10.2 0.7 %copy-start.1 = (f32[32]{0:T(128)S(1)}, f32[32]{0:T(128)}, u32[]{:S(2)}) copy-start(f32[32]{0:T(128)} %energy_ref.1) | copy-start | bytes 388
  14.7 7.9 %collective-permute-start.2 = (bf16[30,24,128]{2,1,0:T(8,128)(2,1)S(1)}, bf16[30,24,128]{2,1,0:T(8,128)(2,1)S(1)}, u32[]{:S(2)}, u32[]{:S(2)}) collective-permute-start(bf16[30,24,128]{2,1,0:T(8,128)(2,1)S(1)} %get-tuple-element.23), channel_id=1, source_target_pairs={{0,1},{1,0},{2,3},{3,2},{4,5},{5,4},{6,7},{7,6},{8,9},{9,8},{10,11... | collective-permute-start | bytes 552968 | tf_op jit(solution)/shard_map/ppermute | solution.py:562
  16.3 6.3 %collective-permute-start.3 = (bf16[30,24,128]{2,1,0:T(8,128)(2,1)S(1)}, bf16[30,24,128]{2,1,0:T(8,128)(2,1)S(1)}, u32[]{:S(2)}, u32[]{:S(2)}) collective-permute-start(bf16[30,24,128]{2,1,0:T(8,128)(2,1)S(1)} %get-tuple-element.24), channel_id=1, source_target_pairs={{1,2},{2,1},{5,6},{6,5},{9,10},{10,9},{13,14},{14,13},{17,18},{18,... | collective-permute-start | bytes 552968 | tf_op jit(solution)/shard_map/ppermute | solution.py:563
  37.5 6.0 %collective-permute-start.4 = (f32[8,128]{1,0:T(8,128)S(1)}, f32[8,128]{1,0:T(8,128)S(1)}, u32[]{:S(2)}, u32[]{:S(2)}) collective-permute-start(f32[8,128]{1,0:T(8,128)S(1)} %slice_reduce_fusion), channel_id=1, source_target_pairs={{0,1},{1,0},{2,3},{3,2},{4,5},{5,4},{6,7},{7,6},{8,9},{9,8},{10,11... | collective-permute-start | bytes 12296 | tf_op jit(solution)/shard_map/ppermute | solution.py:662
  43.5 4.5 %collective-permute-start.5 = (f32[8,128]{1,0:T(8,128)S(1)}, f32[8,128]{1,0:T(8,128)S(1)}, u32[]{:S(2)}, u32[]{:S(2)}) collective-permute-start(f32[8,128]{1,0:T(8,128)S(1)} %add.6), channel_id=1, source_target_pairs={{0,2},{1,3},{2,0},{3,1},{4,6},{5,7},{6,4},{7,5},{8,10},{9,11},{10,... | collective-permute-start | bytes 12296 | tf_op jit(solution)/shard_map/ppermute | solution.py:662

commit v3 on v2

--- a/solution.py
+++ b/solution.py
@@ -132,8 +132,8 @@
 
 
 def first_kernel(
-    fields_ref, orbitals_ref, windows_ref, own_ref, a_ref, b_ref,
-    wide_ref, outer_ref, orb_ref, s_ref, sem_ref,
+    fields_ref, orbitals_ref, potential_ref, windows_ref, own_ref, a_ref, b_ref, lp_ref,
+    wide_ref, outer_ref, orb_ref, s_ref, sem_ref, lp_sem_ref,
 ):
     receivers, window = windows_ref.shape[:2]
     total = fields_ref.shape[0]
@@ -142,6 +142,15 @@
     fetch_orbitals = pltpu.make_async_copy(orbitals_ref, orb_ref, sem_ref.at[1])
     fetch.start()
     fetch_orbitals.start()
+    first_pair = (lax.axis_index("pot") * own_ref.shape[1] - LEAD) // 2
+    last_pair = potential_ref.shape[1] // LANES - 1
+    fetches = []
+    for p in range(lp_ref.shape[0]):
+        at = pl.multiple_of(jnp.clip(first_pair + p, 0, last_pair) * LANES, LANES)
+        source = potential_ref.at[:, pl.ds(at, LANES)]
+        fetches.append(pltpu.make_async_copy(source, lp_ref.at[p], lp_sem_ref.at[p]))
+    for copy in fetches:
+        copy.start()
     for t in range(ahead):
         wide_ref[t] = jnp.zeros(wide_ref.shape[1:], wide_ref.dtype)
         wide_ref[ahead + total + t] = jnp.zeros(wide_ref.shape[1:], wide_ref.dtype)
@@ -161,7 +170,7 @@
         copy.start()
     fetch_orbitals.wait()
     relayout(orb_ref, own_ref, a_ref, b_ref, s_ref)
-    for copy in copies:
+    for copy in fetches + copies:
         copy.wait()
 
 
@@ -247,13 +256,13 @@
 
 
 def diagonal_kernel(energy_ref, lp_ref, r_ref, lp_ref2, *part_refs):
-    planes_all, plane_cells = lp_ref.shape
-    rows_all = plane_cells // NX
+    pairs, planes_all, _ = lp_ref.shape
     region_z, region_y, size, _ = r_ref.shape
     depth, rows = region_z - 2 * HALO, region_y - 2 * HALO
     groups = size // SPLIT
     z_base = lax.axis_index("grid") * depth
     y_base = lax.axis_index("pot") * rows
+    rows_all = lax.axis_size("pot") * rows
 
     shift = jnp.zeros((size, LANES), jnp.float32)
     group_of = iota((size, LANES), 0) % groups
@@ -263,10 +272,8 @@
             here = (group_of == g) & (member == b)
             shift = jnp.where(here, 3.0 - energy_ref[g * BATCH + b], shift)
 
-    pairs = part_refs[0].shape[0]
     for p in range(pairs):
-        at = jnp.clip((y_base - LEAD) // 2 + p, 0, rows_all // 2 - 1) * LANES
-        rest = lp_ref[:, pl.ds(pl.multiple_of(at, LANES), LANES)]
+        rest = lp_ref[p]
         for part_ref in part_refs:
             part = rest.astype(jnp.bfloat16).astype(jnp.float32)
             part_ref[p] = part
@@ -403,8 +410,7 @@
 
 
 def prepare_kernel(
-    parts_ref, own_ref, a_ref, b_ref, r_ref, inverse_ref,
-    ro_ref, first_ref, x_ref, y_ref, acc_ref, later_ref, wide_ref, w_ref,
+    parts_ref, own_ref, a_ref, b_ref, r_ref, ro_ref, first_ref, acc_ref, later_ref, w_ref
 ):
     depth, rows = own_ref.shape[:2]
     fields = first_ref.shape[4]
@@ -440,6 +446,10 @@
 
     lax.fori_loop(0, r_ref.shape[0], scaled, 0)
 
+
+def inner_kernel(first_ref, r_ref, later_ref, inverse_ref, x_ref, y_ref, wide_ref):
+    groups, region_z, region_y, _, fields = first_ref.shape[:5]
+    depth, rows = region_z - 2 * HALO, region_y - 2 * HALO
     all_rows = depth * fields
 
     pick = one_hot(iota((all_rows, fields), 0) // depth == iota((all_rows, fields), 1))
@@ -539,7 +549,8 @@
     for p in range(fields):
         for t in range(pieces):
             out_ref[p, t] = updated[p * depth : (p + 1) * depth, t * LANES : (t + 1) * LANES]
-        out_ref[p, pieces] = jnp.broadcast_to(m_ref[p : p + 1, :], (depth, LANES))
+        mine, other = m_ref[p : p + 1, :], m_ref[p ^ 1 : (p ^ 1) + 1, :]
+        out_ref[p, pieces] = jnp.where(iota((depth, LANES), 0) == 1, other, mine)
 
 
 VMEM = pl.BlockSpec(memory_space=pltpu.VMEM)
@@ -582,26 +593,29 @@
     limit = pltpu.CompilerParams(vmem_limit_bytes=VMEM_LIMIT)
     call = functools.partial(pl.pallas_call, compiler_params=limit)
     side = len(row_cells(depth))
+    lp_shape = (rows // 2 + LEAD, local_potential.shape[0], LANES)
     fields_tiles = potentials.reshape(depth, pots * pieces, LANES).transpose(1, 0, 2)
-    windows, own, to_a, to_b = call(
+    windows, own, to_a, to_b, lp = call(
         first_kernel,
         out_shape=[
             pltpu.HBM((pots, window, depth, LANES), f32),
             shape((depth, rows, half, LANES), bf16),
             shape((side, half, LANES), bf16),
             shape((side, half, LANES), bf16),
+            shape(lp_shape, f32),
         ],
-        in_specs=[ANY] * 2,
-        out_specs=[ANY] + [VMEM] * 3,
+        in_specs=[ANY] * 3,
+        out_specs=[ANY] + [VMEM] * 4,
         scratch_shapes=[
             pltpu.VMEM((pots * pieces + window + 1 - pieces, depth, LANES), f32),
             pltpu.VMEM((pots, depth, LANES), f32),
             pltpu.VMEM(orbitals.shape, bf16),
             pltpu.VMEM((half * rows * depth, LANES), f32),
             pltpu.SemaphoreType.DMA((2 + 2 * pots,)),
+            pltpu.SemaphoreType.DMA(lp_shape[:1]),
         ],
         name="first",
-    )(in_hbm(fields_tiles), in_hbm(orbitals))
+    )(in_hbm(fields_tiles), in_hbm(orbitals), in_hbm(local_potential))
     got_a, got_b = swapped(to_a, to_b, "pot")
     parts = lax.all_to_all(windows, "pot", 0, 0, tiled=True)
     parts = parts.reshape(pots * window * depth, LANES)
@@ -612,9 +626,9 @@
         in_specs=[SMEM, VMEM],
         out_specs=VMEM,
         scratch_shapes=[pltpu.VMEM((rows + 2 * LEAD, region[0] * SPLIT, LANES), f32)]
-        + [pltpu.VMEM((rows // 2 + LEAD, local_potential.shape[0], LANES), f32)] * 3,
+        + [pltpu.VMEM(lp_shape, f32)] * 3,
         name="diagonal",
-    )(energies, local_potential)
+    )(in_hbm(energies), *in_vmem(lp))
 
     parts, inverse_diagonal = lax.optimization_barrier((parts, inverse_diagonal))
     edge = len(plane_cells(rows))
@@ -627,22 +641,30 @@
     )(*in_vmem(parts, own, got_a, got_b))
     z_a, z_b = swapped(up, down, "grid")
 
-    own_values = [
-        shape(region + (half, LANES), f32),
-        *(
-            shape((half // SPLIT, region[0] - 2 * n, region[1] - 2 * n, SPLIT, fields, LANES), f32)
-            for n in range(SWEEPS - 1)
-        ),
-        shape((depth, rows, SPLIT, fields, LANES), f32),
+    group_count = half // SPLIT
+    iterates = [
+        shape((group_count, region[0] - 2 * n, region[1] - 2 * n, SPLIT, fields, LANES), f32)
+        for n in range(SWEEPS - 1)
     ]
-    *prepared, later, wide = call(
+    per_orbital = shape(region + (half, LANES), f32)
+    sums = shape((depth, rows, SPLIT, fields, LANES), f32)
+    ro, first, acc, later = call(
         prepare_kernel,
-        out_shape=own_values + own_values[:1] + [shape((depth * fields,) * 2, bf16)],
-        in_specs=[VMEM] * 6,
-        out_specs=[VMEM] * 7,
+        out_shape=[per_orbital, iterates[0], sums, per_orbital],
+        in_specs=[VMEM] * 5,
+        out_specs=[VMEM] * 4,
         scratch_shapes=[pltpu.VMEM((rows, half, LANES), f32)],
         name="prepare",
-    )(*in_vmem(parts, own, got_a, got_b, inverse_diagonal), in_hbm(inverse_factor))
+    )(*in_vmem(parts, own, got_a, got_b, inverse_diagonal))
+    second, third, wide = call(
+        inner_kernel,
+        out_shape=iterates[1:] + [shape((depth * fields,) * 2, bf16)],
+        in_specs=[VMEM] * 4,
+        out_specs=[VMEM] * 3,
+        name="inner",
+    )(*in_vmem(first, inverse_diagonal, later), in_hbm(inverse_factor))
+    prepared = [ro, first, second, third, acc]
+    own_values = [per_orbital, *iterates, sums]
     sent, *_ = call(
         sweep_kernel,
         out_shape=[shape((fields, pieces + 1, depth, LANES), f32)] + own_values,
@@ -659,9 +681,14 @@
     margins = jnp.sum(back[:, pieces], axis=0)
     step = 1
     while step < grids:
-        margins = margins + lax.ppermute(margins, "grid", [(i, i ^ step) for i in range(grids)])
+        pairs = [
+            (i * grids + g, i * grids + (g ^ step)) for i in range(1, pots, 2) for g in range(grids)
+        ]
+        margins = margins + lax.ppermute(margins, ("pot", "grid"), pairs)
         step *= 2
-    margins = margins[:1, :fields] / local_potential.size
+    handed = lax.ppermute(margins, "pot", [(i, i - 1) for i in range(1, pots, 2)])
+    odd = lax.rem(lax.axis_index("pot"), 2) == 1
+    margins = jnp.where(odd, margins[:1, :fields], handed[1:2, :fields]) / local_potential.size
     return updated, margins
 
 

time: 48.9 us -> 52.9 us (1.082)
  waiting for transfers between devices: 6.14 us -> 14.1 us
  starting transfers between devices: 14.5 us -> 11.3 us
  local copies, waits for them, and re-layouts: 2.36 us -> 0.66 us
  Pallas kernels: 14.4 us -> 15.3 us
    ppermute x2 -> x3, waiting for transfers between devices: 3.95 us -> 10.4 us  [the longest x1 10.4 us: rows_plan(): lax.ppermute(margins, 'pot', [(i, i - 1) for i in range(1, pots, 2)])]
    ppermute x2 -> x3, starting transfers between devices: 5.87 us -> 2.6 us  [the longest x2 1.31 us: rows_plan(): margins = margins + lax.ppermute(margins, ('pot', 'grid'), pairs)]
    unnamed x4 -> x0, local copies, waits for them, and re-layouts: 1.69 us -> none
    all_to_all x1, waiting for transfers between devices: 2.18 us -> 3.75 us  [rows_plan(): parts = lax.all_to_all(windows, 'pot', 0, 0, tiled=True)]
    pallas_call x1 -> x2, Pallas kernels: 5.62 us -> 5.77 us  [the longest x1 3.31 us: rows_plan(): call(inner_kernel, out_shape=iterates[1:] + [shape((depth * fields,) * 2,...]
  transfers between devices with their start and end apart: 7 -> 8, of which waited for: 3 -> 2; matrix products, arithmetic and copies ran while one was open for 1% -> 1% of each run, Pallas kernels for 15% -> 14%
where the time goes in v3:
time: 52.9 us; the launch traced here: 52.5 us
  Pallas kernels  15.3 us (29%)
  waiting for transfers between devices  14.1 us (27%)
  starting transfers between devices  11.3 us (21%)
  blocking collectives  9.8 us (19%)
  between operations  0.77 us (1%)
  local copies, waits for them, and re-layouts  0.66 us (1%)
  other arithmetic  0.53 us (1%)
    ppermute x1, waiting for transfers between devices, rows_plan(): lax.ppermute(margins, 'pot', [(i, i - 1) for i in range(1, pots, 2)])  10.4 us
    all_to_all x1, blocking collectives, rows_plan(): back = lax.all_to_all(sent, 'pot', 0, 0, tiled=True)  9.8 us
    pallas_call x1, Pallas kernels, rows_plan(): call(sweep_kernel, out_shape=[shape((fields, pieces + 1, depth, LANES), f...  5.57 us
    all_to_all x1, starting transfers between devices, rows_plan(): parts = lax.all_to_all(windows, 'pot', 0, 0, tiled=True)  5.22 us
    all_to_all x1, waiting for transfers between devices, rows_plan(): parts = lax.all_to_all(windows, 'pot', 0, 0, tiled=True)  3.75 us
    pallas_call x1, Pallas kernels, rows_plan(): call(inner_kernel, out_shape=iterates[1:] + [shape((depth * fields,) * 2,...  3.31 us
    pallas_call x1, Pallas kernels, rows_plan(): call(prepare_kernel, out_shape=[per_orbital, iterates[0], sums, per_orbit...  2.46 us
    pallas_call x1, Pallas kernels, rows_plan(): call(first_kernel, out_shape=[pltpu.HBM((pots, window, depth, LANES), f32...  2.26 us
  transfers between devices with their start and end apart: 8, of which 2 were waited for; matrix products, arithmetic and copies ran while one was open for 1% of the time, Pallas kernels for 14%

profile of v3, /device:TPU:0, one launch (start us, length us, event | category | flops | bytes accessed | tf_op | source)
XLA Modules:
  0.0 52.5 jit_solution(1932155319320092836)
XLA Ops:
  0.6 2.3 %first.1 = (f32[8,7,8,128]{3,2,1,0:T(8,128)}, bf16[8,8,16,128]{3,2,1,0:T(8,128)(2,1)S(1)}, bf16[24,16,128]{2,1,0:T(8,128)(2,1)S(1)}, bf16[24,16,128]{2,1,0:T(8,128)(2,1)S(1)}, f32[8,32,128]{2,1,0:T(8,128)S(1)}) custom-call(f32[32,8,128]{2,1,0:T(8,128)} %bitcast.12, bf16[32,8,512]{2,1,0:T(8,128)(2,1)} %orbitals_ref.1, f32[32,4096]{1,0:T(8,128)} %potential_ref.1), custom_call_target="tpu_custom_call" | custom-call | tf_op jit(solution)/shard_map/first/pallas_call | solution.py:598
  2.9 5.2 %all-to-all-start = ((f32[8,7,8,128]{3,2,1,0:T(8,128)}), f32[8,7,8,128]{3,2,1,0:T(8,128)S(1)}, u32[]{:S(2)}, u32[]{:S(2)}) async-start(f32[8,7,8,128]{3,2,1,0:T(8,128)} %get-tuple-element.19), calls=%async_computation | async-start | bytes 458752 | tf_op jit(solution)/shard_map/all_to_all | solution.py:620
  8.1 0.5 collective-permute-start
  8.6 0.7 %collective-permute-start.1 = (bf16[24,16,128]{2,1,0:T(8,128)(2,1)S(1)}, bf16[24,16,128]{2,1,0:T(8,128)(2,1)S(1)}, u32[]{:S(2)}, u32[]{:S(2)}) collective-permute-start(bf16[24,16,128]{2,1,0:T(8,128)(2,1)S(1)} %get-tuple-element.24), channel_id=1, source_target_pairs={{4,8},{8,4},{12,16},{16,12},{20,24},{24,20},{5,9},{9,5},{13,17},{1... | collective-permute-start | bytes 294920 | tf_op jit(solution)/shard_map/ppermute | solution.py:574
  9.3 1.6 %diagonal.1.r_ref = f32[14,14,16,128]{3,2,1,0:T(8,128)S(1)} custom-call(f32[32]{0:T(128)} %energy_ref.1, f32[8,32,128]{2,1,0:T(8,128)S(1)} %get-tuple-element.20.lp_ref), custom_call_target="tpu_custom_call" | custom-call | tf_op jit(solution)/shard_map/diagonal/pallas_call | solution.py:623
  10.9 3.7 %all-to-all-done = f32[8,7,8,128]{3,2,1,0:T(8,128)S(1)} async-done(((f32[8,7,8,128]{3,2,1,0:T(8,128)}), f32[8,7,8,128]{3,2,1,0:T(8,128)S(1)}, u32[]{:S(2)}, u32[]{:S(2)}) %all-to-all-start) | async-done | bytes 229408 | tf_op jit(solution)/shard_map/all_to_all | solution.py:620
  14.7 0.0 collective-permute-done.a_ref
  14.7 0.0 collective-permute-done.1.b_ref
  14.7 0.1 sends.1
  14.8 1.6 %collective-permute-start.2 = (bf16[30,24,128]{2,1,0:T(8,128)(2,1)S(1)}, bf16[30,24,128]{2,1,0:T(8,128)(2,1)S(1)}, u32[]{:S(2)}, u32[]{:S(2)}) collective-permute-start(bf16[30,24,128]{2,1,0:T(8,128)(2,1)S(1)} %get-tuple-element.25), channel_id=1, source_target_pairs={{0,1},{1,0},{2,3},{3,2},{4,5},{5,4},{6,7},{7,6},{8,9},{9,8},{10,11... | collective-permute-start | bytes 552968 | tf_op jit(solution)/shard_map/ppermute | solution.py:573
  16.4 0.7 %collective-permute-start.3 = (bf16[30,24,128]{2,1,0:T(8,128)(2,1)S(1)}, bf16[30,24,128]{2,1,0:T(8,128)(2,1)S(1)}, u32[]{:S(2)}, u32[]{:S(2)}) collective-permute-start(bf16[30,24,128]{2,1,0:T(8,128)(2,1)S(1)} %get-tuple-element.26), channel_id=1, source_target_pairs={{1,2},{2,1},{5,6},{6,5},{9,10},{10,9},{13,14},{14,13},{17,18},{18,... | collective-permute-start | bytes 552968 | tf_op jit(solution)/shard_map/ppermute | solution.py:574
  17.1 2.5 %prepare.1 = (f32[14,14,16,128]{3,2,1,0:T(8,128)S(1)}, f32[4,14,14,4,8,128]{5,4,3,2,1,0:T(8,128)S(1)}, f32[8,8,4,8,128]{4,3,2,1,0:T(8,128)S(1)}, f32[14,14,16,128]{3,2,1,0:T(8,128)S(1)}) custom-call(f32[448,128]{1,0:T(8,128)S(1)} %bitcast.10, bf16[8,8,16,128]{3,2,1,0:T(8,128)(2,1)S(1)} %get-tuple-element.22.own_ref, ...), custom_call_target="tpu_custom_call" | custom-call | tf_op jit(solution)/shard_map/prepare/pallas_call | solution.py:651
  19.6 3.3 %inner.1 = (f32[4,12,12,4,8,128]{5,4,3,2,1,0:T(8,128)S(1)}, f32[4,10,10,4,8,128]{5,4,3,2,1,0:T(8,128)S(1)}, bf16[64,64]{1,0:T(8,128)(2,1)S(1)}) custom-call(f32[4,14,14,4,8,128]{5,4,3,2,1,0:T(8,128)S(1)} %get-tuple-element.29.first_ref.first_in, f32[14,14,16,128]{3,2,1,0:T(8,128)S(1)} %diagonal.1.r_ref, f32[14,14,16,128]{3,2,1,0:T(8,128)S(1)} %get-tuple-element.28.later_ref, ...), custom_call_target="tpu_custom_call" | custom-call | tf_op jit(solution)/shard_map/inner/pallas_call | solution.py:659
  22.9 0.0 collective-permute-done.2.a_ref
  22.9 0.0 collective-permute-done.3.b_ref
  22.9 5.6 %sweeps.1 = (f32[8,5,8,128]{3,2,1,0:T(8,128)S(1)}, f32[14,14,16,128]{3,2,1,0:T(8,128)S(1)}, f32[4,14,14,4,8,128]{5,4,3,2,1,0:T(8,128)S(1)}, f32[4,12,12,4,8,128]...) custom-call(f32[448,128]{1,0:T(8,128)S(1)} %bitcast.11, ...), custom_call_target="tpu_custom_call", output_to_operand_aliasing={{1}: (6, {}), {2}: (7, {}), {3}: (8, {}), {4}: (9, {}), {5}... | custom-call | tf_op jit(solution)/shard_map/sweeps/pallas_call | solution.py:668
  28.5 9.8 %all_to_all.10 = f32[8,5,8,128]{3,2,1,0:T(8,128)S(1)} all-to-all(f32[8,5,8,128]{3,2,1,0:T(8,128)S(1)} %get-tuple-element.35), channel_id=1, replica_groups=mesh['pot'=8,'grid'=4] {'pot'}, dimensions={0} | all-to-all | bytes 327680 | tf_op jit(solution)/shard_map/all_to_all | solution.py:678
  38.3 0.7 %collective-permute-start.4 = (f32[8,128]{1,0:T(8,128)S(1)}, f32[8,128]{1,0:T(8,128)S(1)}, u32[]{:S(2)}, u32[]{:S(2)}) collective-permute-start(f32[8,128]{1,0:T(8,128)S(1)} %slice_reduce_fusion), channel_id=1, source_target_pairs={{4,5},{5,4},{6,7},{7,6},{12,13},{13,12},{14,15},{15,14},{20,21},{2... | collective-permute-start | bytes 12296 | tf_op jit(solution)/shard_map/ppermute | solution.py:687
  39.0 0.7 %collective-permute-start.5 = (f32[8,128]{1,0:T(8,128)S(1)}, f32[8,128]{1,0:T(8,128)S(1)}, u32[]{:S(2)}, u32[]{:S(2)}) collective-permute-start(f32[8,128]{1,0:T(8,128)S(1)} %add.6), channel_id=1, source_target_pairs={{4,6},{5,7},{6,4},{7,5},{12,14},{13,15},{14,12},{15,13},{20,22},{2... | collective-permute-start | bytes 12296 | tf_op jit(solution)/shard_map/ppermute | solution.py:687
  39.7 0.0 collective-permute-done.5
  39.7 1.3 %collective-permute-start.6 = (f32[8,128]{1,0:T(8,128)S(1)}, f32[8,128]{1,0:T(8,128)S(1)}, u32[]{:S(2)}, u32[]{:S(2)}) collective-permute-start(f32[8,128]{1,0:T(8,128)S(1)} %add.7), channel_id=1, source_target_pairs={{4,0},{12,8},{20,16},{28,24},{5,1},{13,9},{21,17},{29,25},{6,2},{1... | collective-permute-start | bytes 12296 | tf_op jit(solution)/shard_map/ppermute | solution.py:689
  41.0 0.7 %slice.16 = f32[8,4,8,128]{3,2,1,0:T(8,128)} slice(f32[8,5,8,128]{3,2,1,0:T(8,128)S(1)} %all_to_all.10), slice={[0:8], [0:4], [0:8], [0:128]} | slice | bytes 262144 | tf_op jit(solution)/shard_map/slice | solution.py:679
  41.6 10.4 %collective-permute-done.6 = f32[8,128]{1,0:T(8,128)S(1)} collective-permute-done((f32[8,128]{1,0:T(8,128)S(1)}, f32[8,128]{1,0:T(8,128)S(1)}, u32[]{:S(2)}, u32[]{:S(2)}) %collective-permute-start.6) | collective-permute-done | bytes 4128 | tf_op jit(solution)/shard_map/ppermute | solution.py:689
  52.0 0.5 fusion
  (4 shorter events, 0.0 us)
Async XLA Ops:
  2.9 11.8 %all-to-all-start = ((f32[8,7,8,128]{3,2,1,0:T(8,128)}), f32[8,7,8,128]{3,2,1,0:T(8,128)S(1)}, u32[]{:S(2)}, u32[]{:S(2)}) async-start(f32[8,7,8,128]{3,2,1,0:T(8,128)} %get-tuple-element.19), calls=%async_computation | async-start | bytes 458752 | tf_op jit(solution)/shard_map/all_to_all | solution.py:620
  8.1 6.6 %collective-permute-start = (bf16[24,16,128]{2,1,0:T(8,128)(2,1)S(1)}, bf16[24,16,128]{2,1,0:T(8,128)(2,1)S(1)}, u32[]{:S(2)}, u32[]{:S(2)}) collective-permute-start(bf16[24,16,128]{2,1,0:T(8,128)(2,1)S(1)} %get-tuple-element.23), channel_id=1, source_target_pairs={{0,4},{4,0},{8,12},{12,8},{16,20},{20,16},{24,28},{28,24},{1,5},{5... | collective-permute-start | bytes 294920 | tf_op jit(solution)/shard_map/ppermute | solution.py:573
  8.6 6.1 %collective-permute-start.1 = (bf16[24,16,128]{2,1,0:T(8,128)(2,1)S(1)}, bf16[24,16,128]{2,1,0:T(8,128)(2,1)S(1)}, u32[]{:S(2)}, u32[]{:S(2)}) collective-permute-start(bf16[24,16,128]{2,1,0:T(8,128)(2,1)S(1)} %get-tuple-element.24), channel_id=1, source_target_pairs={{4,8},{8,4},{12,16},{16,12},{20,24},{24,20},{5,9},{9,5},{13,17},{1... | collective-permute-start | bytes 294920 | tf_op jit(solution)/shard_map/ppermute | solution.py:574
  14.8 8.1 %collective-permute-start.2 = (bf16[30,24,128]{2,1,0:T(8,128)(2,1)S(1)}, bf16[30,24,128]{2,1,0:T(8,128)(2,1)S(1)}, u32[]{:S(2)}, u32[]{:S(2)}) collective-permute-start(bf16[30,24,128]{2,1,0:T(8,128)(2,1)S(1)} %get-tuple-element.25), channel_id=1, source_target_pairs={{0,1},{1,0},{2,3},{3,2},{4,5},{5,4},{6,7},{7,6},{8,9},{9,8},{10,11... | collective-permute-start | bytes 552968 | tf_op jit(solution)/shard_map/ppermute | solution.py:573
  16.4 6.5 %collective-permute-start.3 = (bf16[30,24,128]{2,1,0:T(8,128)(2,1)S(1)}, bf16[30,24,128]{2,1,0:T(8,128)(2,1)S(1)}, u32[]{:S(2)}, u32[]{:S(2)}) collective-permute-start(bf16[30,24,128]{2,1,0:T(8,128)(2,1)S(1)} %get-tuple-element.26), channel_id=1, source_target_pairs={{1,2},{2,1},{5,6},{6,5},{9,10},{10,9},{13,14},{14,13},{17,18},{18,... | collective-permute-start | bytes 552968 | tf_op jit(solution)/shard_map/ppermute | solution.py:574
  38.3 0.7 %collective-permute-start.4 = (f32[8,128]{1,0:T(8,128)S(1)}, f32[8,128]{1,0:T(8,128)S(1)}, u32[]{:S(2)}, u32[]{:S(2)}) collective-permute-start(f32[8,128]{1,0:T(8,128)S(1)} %slice_reduce_fusion), channel_id=1, source_target_pairs={{4,5},{5,4},{6,7},{7,6},{12,13},{13,12},{14,15},{15,14},{20,21},{2... | collective-permute-start | bytes 12296 | tf_op jit(solution)/shard_map/ppermute | solution.py:687
  39.0 0.7 %collective-permute-start.5 = (f32[8,128]{1,0:T(8,128)S(1)}, f32[8,128]{1,0:T(8,128)S(1)}, u32[]{:S(2)}, u32[]{:S(2)}) collective-permute-start(f32[8,128]{1,0:T(8,128)S(1)} %add.6), channel_id=1, source_target_pairs={{4,6},{5,7},{6,4},{7,5},{12,14},{13,15},{14,12},{15,13},{20,22},{2... | collective-permute-start | bytes 12296 | tf_op jit(solution)/shard_map/ppermute | solution.py:687
  39.7 12.3 %collective-permute-start.6 = (f32[8,128]{1,0:T(8,128)S(1)}, f32[8,128]{1,0:T(8,128)S(1)}, u32[]{:S(2)}, u32[]{:S(2)}) collective-permute-start(f32[8,128]{1,0:T(8,128)S(1)} %add.7), channel_id=1, source_target_pairs={{4,0},{12,8},{20,16},{28,24},{5,1},{13,9},{21,17},{29,25},{6,2},{1... | collective-permute-start | bytes 12296 | tf_op jit(solution)/shard_map/ppermute | solution.py:689

commit v4 on v2

--- a/solution.py
+++ b/solution.py
@@ -132,8 +132,8 @@
 
 
 def first_kernel(
-    fields_ref, orbitals_ref, windows_ref, own_ref, a_ref, b_ref,
-    wide_ref, outer_ref, orb_ref, s_ref, sem_ref,
+    fields_ref, orbitals_ref, potential_ref, windows_ref, own_ref, a_ref, b_ref, lp_ref,
+    wide_ref, outer_ref, orb_ref, s_ref, sem_ref, lp_sem_ref,
 ):
     receivers, window = windows_ref.shape[:2]
     total = fields_ref.shape[0]
@@ -142,6 +142,15 @@
     fetch_orbitals = pltpu.make_async_copy(orbitals_ref, orb_ref, sem_ref.at[1])
     fetch.start()
     fetch_orbitals.start()
+    first_pair = (lax.axis_index("pot") * own_ref.shape[1] - LEAD) // 2
+    last_pair = potential_ref.shape[1] // LANES - 1
+    fetches = []
+    for p in range(lp_ref.shape[0]):
+        at = pl.multiple_of(jnp.clip(first_pair + p, 0, last_pair) * LANES, LANES)
+        source = potential_ref.at[:, pl.ds(at, LANES)]
+        fetches.append(pltpu.make_async_copy(source, lp_ref.at[p], lp_sem_ref.at[p]))
+    for copy in fetches:
+        copy.start()
     for t in range(ahead):
         wide_ref[t] = jnp.zeros(wide_ref.shape[1:], wide_ref.dtype)
         wide_ref[ahead + total + t] = jnp.zeros(wide_ref.shape[1:], wide_ref.dtype)
@@ -161,7 +170,7 @@
         copy.start()
     fetch_orbitals.wait()
     relayout(orb_ref, own_ref, a_ref, b_ref, s_ref)
-    for copy in copies:
+    for copy in fetches + copies:
         copy.wait()
 
 
@@ -247,13 +256,13 @@
 
 
 def diagonal_kernel(energy_ref, lp_ref, r_ref, lp_ref2, *part_refs):
-    planes_all, plane_cells = lp_ref.shape
-    rows_all = plane_cells // NX
+    pairs, planes_all, _ = lp_ref.shape
     region_z, region_y, size, _ = r_ref.shape
     depth, rows = region_z - 2 * HALO, region_y - 2 * HALO
     groups = size // SPLIT
     z_base = lax.axis_index("grid") * depth
     y_base = lax.axis_index("pot") * rows
+    rows_all = lax.axis_size("pot") * rows
 
     shift = jnp.zeros((size, LANES), jnp.float32)
     group_of = iota((size, LANES), 0) % groups
@@ -263,10 +272,8 @@
             here = (group_of == g) & (member == b)
             shift = jnp.where(here, 3.0 - energy_ref[g * BATCH + b], shift)
 
-    pairs = part_refs[0].shape[0]
     for p in range(pairs):
-        at = jnp.clip((y_base - LEAD) // 2 + p, 0, rows_all // 2 - 1) * LANES
-        rest = lp_ref[:, pl.ds(pl.multiple_of(at, LANES), LANES)]
+        rest = lp_ref[p]
         for part_ref in part_refs:
             part = rest.astype(jnp.bfloat16).astype(jnp.float32)
             part_ref[p] = part
@@ -432,7 +439,7 @@
         place(cells, r_ref, ro_ref, first_ref, first_term)
         return carry
 
-    lax.fori_loop(0, depth, plane, 0)
+    lax.fori_loop(0, depth, plane, 0, unroll=2)
 
     def scaled(z, carry):
         later_ref[z] = (INNER[-1] / INNER[0]) * r_ref[z]
@@ -538,8 +545,15 @@
     pieces = rows * NX // LANES
     for p in range(fields):
         for t in range(pieces):
-            out_ref[p, t] = updated[p * depth : (p + 1) * depth, t * LANES : (t + 1) * LANES]
-        out_ref[p, pieces] = jnp.broadcast_to(m_ref[p : p + 1, :], (depth, LANES))
+            block = updated[p * depth : (p + 1) * depth, t * LANES : (t + 1) * LANES]
+            out_ref[p, t] = block.astype(out_ref.dtype)
+        rest = jnp.broadcast_to(m_ref[p : p + 1, :], (depth, LANES))
+        spread = jnp.zeros((depth, LANES), jnp.float32)
+        for number in range(3):
+            part = rest.astype(jnp.bfloat16).astype(jnp.float32)
+            spread = jnp.where(iota((depth, LANES), 0) == number, part, spread)
+            rest = rest - part
+        out_ref[p, pieces] = spread.astype(out_ref.dtype)
 
 
 VMEM = pl.BlockSpec(memory_space=pltpu.VMEM)
@@ -582,26 +596,29 @@
     limit = pltpu.CompilerParams(vmem_limit_bytes=VMEM_LIMIT)
     call = functools.partial(pl.pallas_call, compiler_params=limit)
     side = len(row_cells(depth))
+    lp_shape = (rows // 2 + LEAD, local_potential.shape[0], LANES)
     fields_tiles = potentials.reshape(depth, pots * pieces, LANES).transpose(1, 0, 2)
-    windows, own, to_a, to_b = call(
+    windows, own, to_a, to_b, lp = call(
         first_kernel,
         out_shape=[
             pltpu.HBM((pots, window, depth, LANES), f32),
             shape((depth, rows, half, LANES), bf16),
             shape((side, half, LANES), bf16),
             shape((side, half, LANES), bf16),
+            shape(lp_shape, f32),
         ],
-        in_specs=[ANY] * 2,
-        out_specs=[ANY] + [VMEM] * 3,
+        in_specs=[ANY] * 3,
+        out_specs=[ANY] + [VMEM] * 4,
         scratch_shapes=[
             pltpu.VMEM((pots * pieces + window + 1 - pieces, depth, LANES), f32),
             pltpu.VMEM((pots, depth, LANES), f32),
             pltpu.VMEM(orbitals.shape, bf16),
             pltpu.VMEM((half * rows * depth, LANES), f32),
             pltpu.SemaphoreType.DMA((2 + 2 * pots,)),
+            pltpu.SemaphoreType.DMA(lp_shape[:1]),
         ],
         name="first",
-    )(in_hbm(fields_tiles), in_hbm(orbitals))
+    )(in_hbm(fields_tiles), in_hbm(orbitals), in_hbm(local_potential))
     got_a, got_b = swapped(to_a, to_b, "pot")
     parts = lax.all_to_all(windows, "pot", 0, 0, tiled=True)
     parts = parts.reshape(pots * window * depth, LANES)
@@ -612,9 +629,9 @@
         in_specs=[SMEM, VMEM],
         out_specs=VMEM,
         scratch_shapes=[pltpu.VMEM((rows + 2 * LEAD, region[0] * SPLIT, LANES), f32)]
-        + [pltpu.VMEM((rows // 2 + LEAD, local_potential.shape[0], LANES), f32)] * 3,
+        + [pltpu.VMEM(lp_shape, f32)] * 3,
         name="diagonal",
-    )(energies, local_potential)
+    )(in_hbm(energies), *in_vmem(lp))
 
     parts, inverse_diagonal = lax.optimization_barrier((parts, inverse_diagonal))
     edge = len(plane_cells(rows))
@@ -645,7 +662,7 @@
     )(*in_vmem(parts, own, got_a, got_b, inverse_diagonal), in_hbm(inverse_factor))
     sent, *_ = call(
         sweep_kernel,
-        out_shape=[shape((fields, pieces + 1, depth, LANES), f32)] + own_values,
+        out_shape=[shape((fields, pieces + 1, depth, LANES), bf16)] + own_values,
         in_specs=[VMEM] * 11,
         out_specs=[VMEM] * 6,
         scratch_shapes=[pltpu.VMEM((fields, LANES), f32)],
@@ -654,9 +671,9 @@
     )(*in_vmem(parts, z_a, z_b, inverse_diagonal, later, wide, *prepared))
 
     back = lax.all_to_all(sent, "pot", 0, 0, tiled=True)
-    updated = back[:, :pieces].reshape(pots * pieces, depth, LANES).transpose(1, 0, 2)
+    updated = back[:, :pieces].astype(f32).reshape(pots * pieces, depth, LANES).transpose(1, 0, 2)
     updated = updated.reshape(1, depth, pots * width)
-    margins = jnp.sum(back[:, pieces], axis=0)
+    margins = jnp.sum(back[:, pieces].astype(f32), axis=(0, 1))[None]
     step = 1
     while step < grids:
         margins = margins + lax.ppermute(margins, "grid", [(i, i ^ step) for i in range(grids)])

time: 48.9 us -> 47.5 us (0.971)
  local copies, waits for them, and re-layouts: 2.36 us -> 0.01 us
  waiting for transfers between devices: 6.14 us -> 6.99 us
  blocking collectives: 9.8 us -> 9.06 us
  starting transfers between devices: 14.5 us -> 15.2 us
  other arithmetic: 0.53 us -> 1.22 us
    unnamed x4 -> x0, local copies, waits for them, and re-layouts: 1.69 us -> none
    all_to_all x1, waiting for transfers between devices: 2.18 us -> 3.75 us  [rows_plan(): parts = lax.all_to_all(windows, 'pot', 0, 0, tiled=True)]
    all_to_all x1, blocking collectives: 9.8 us -> 9.06 us  [rows_plan(): back = lax.all_to_all(sent, 'pot', 0, 0, tiled=True)]
    ppermute x2, waiting for transfers between devices: 3.95 us -> 3.23 us  [rows_plan(): lax.ppermute(margins, 'grid', [(i, i ^ step) for i in range(grids)])]
    pallas_call x1, Pallas kernels: 5.62 us -> 4.9 us  [rows_plan(): call(prepare_kernel, out_shape=own_values + own_values[:1] + [shape((dept...]
    ppermute x2, starting transfers between devices: 5.87 us -> 6.54 us  [rows_plan(): lax.ppermute(margins, 'grid', [(i, i ^ step) for i in range(grids)])]
    reshape x0 -> x1, other arithmetic: none -> 0.67 us  [rows_plan(): updated = updated.reshape(1, depth, pots * width)]
    slice x1, local copies, waits for them, and re-layouts: 0.66 us -> 0.01 us  [rows_plan(): back[:, :pieces].astype(f32).reshape(pots * pieces, depth, LANES)]
  transfers between devices with their start and end apart: 7 -> 7, of which waited for: 3 -> 3; matrix products, arithmetic and copies ran while one was open for 1% -> 1% of each run, Pallas kernels for 15% -> 14%
where the time goes in v4:
time: 47.5 us; the launch traced here: 47.2 us
  starting transfers between devices  15.2 us (32%)
  Pallas kernels  14 us (29%)
  blocking collectives  9.06 us (19%)
  waiting for transfers between devices  6.99 us (15%)
  other arithmetic  1.22 us (3%)
  between operations  0.71 us (1%)
    all_to_all x1, blocking collectives, rows_plan(): back = lax.all_to_all(sent, 'pot', 0, 0, tiled=True)  9.06 us
    ppermute x2, starting transfers between devices, rows_plan(): lax.ppermute(margins, 'grid', [(i, i ^ step) for i in range(grids)])  6.54 us
    all_to_all x1, starting transfers between devices, rows_plan(): parts = lax.all_to_all(windows, 'pot', 0, 0, tiled=True)  5.22 us
    pallas_call x1, Pallas kernels, rows_plan(): call(sweep_kernel, out_shape=[shape((fields, pieces + 1, depth, LANES), b...  5.07 us
    pallas_call x1, Pallas kernels, rows_plan(): call(prepare_kernel, out_shape=own_values + own_values[:1] + [shape((dept...  4.9 us
    all_to_all x1, waiting for transfers between devices, rows_plan(): parts = lax.all_to_all(windows, 'pot', 0, 0, tiled=True)  3.75 us
    ppermute x2, waiting for transfers between devices, rows_plan(): lax.ppermute(margins, 'grid', [(i, i ^ step) for i in range(grids)])  3.23 us
    pallas_call x1, Pallas kernels, rows_plan(): call(first_kernel, out_shape=[pltpu.HBM((pots, window, depth, LANES), f32...  2.26 us
  transfers between devices with their start and end apart: 7, of which 3 were waited for; matrix products, arithmetic and copies ran while one was open for 1% of the time, Pallas kernels for 14%

profile of v4, /device:TPU:0, one launch (start us, length us, event | category | flops | bytes accessed | tf_op | source)
XLA Modules:
  0.0 47.2 jit_solution(778566168815903230)
XLA Ops:
  0.6 2.3 %first.1 = (f32[8,7,8,128]{3,2,1,0:T(8,128)}, bf16[8,8,16,128]{3,2,1,0:T(8,128)(2,1)S(1)}, bf16[24,16,128]{2,1,0:T(8,128)(2,1)S(1)}, bf16[24,16,128]{2,1,0:T(8,128)(2,1)S(1)}, f32[8,32,128]{2,1,0:T(8,128)S(1)}) custom-call(f32[32,8,128]{2,1,0:T(8,128)} %bitcast.16, bf16[32,8,512]{2,1,0:T(8,128)(2,1)} %orbitals_ref.1, f32[32,4096]{1,0:T(8,128)} %potential_ref.1), custom_call_target="tpu_custom_call" | custom-call | tf_op jit(solution)/shard_map/first/pallas_call | solution.py:601
  2.9 5.2 %all-to-all-start = ((f32[8,7,8,128]{3,2,1,0:T(8,128)}), f32[8,7,8,128]{3,2,1,0:T(8,128)S(1)}, u32[]{:S(2)}, u32[]{:S(2)}) async-start(f32[8,7,8,128]{3,2,1,0:T(8,128)} %get-tuple-element.19), calls=%async_computation | async-start | bytes 458752 | tf_op jit(solution)/shard_map/all_to_all | solution.py:623
  8.1 0.5 %collective-permute-start = (bf16[24,16,128]{2,1,0:T(8,128)(2,1)S(1)}, bf16[24,16,128]{2,1,0:T(8,128)(2,1)S(1)}, u32[]{:S(2)}, u32[]{:S(2)}) collective-permute-start(bf16[24,16,128]{2,1,0:T(8,128)(2,1)S(1)} %get-tuple-element.23), channel_id=1, source_target_pairs={{0,4},{4,0},{8,12},{12,8},{16,20},{20,16},{24,28},{28,24},{1,5},{5... | collective-permute-start | bytes 294920 | tf_op jit(solution)/shard_map/ppermute | solution.py:576
  8.6 0.7 %collective-permute-start.1 = (bf16[24,16,128]{2,1,0:T(8,128)(2,1)S(1)}, bf16[24,16,128]{2,1,0:T(8,128)(2,1)S(1)}, u32[]{:S(2)}, u32[]{:S(2)}) collective-permute-start(bf16[24,16,128]{2,1,0:T(8,128)(2,1)S(1)} %get-tuple-element.24), channel_id=1, source_target_pairs={{4,8},{8,4},{12,16},{16,12},{20,24},{24,20},{5,9},{9,5},{13,17},{1... | collective-permute-start | bytes 294920 | tf_op jit(solution)/shard_map/ppermute | solution.py:577
  9.3 1.6 %diagonal.1.r_ref = f32[14,14,16,128]{3,2,1,0:T(8,128)S(1)} custom-call(f32[32]{0:T(128)} %energy_ref.1, f32[8,32,128]{2,1,0:T(8,128)S(1)} %get-tuple-element.20.lp_ref), custom_call_target="tpu_custom_call" | custom-call | tf_op jit(solution)/shard_map/diagonal/pallas_call | solution.py:626
  10.9 3.7 %all-to-all-done = f32[8,7,8,128]{3,2,1,0:T(8,128)S(1)} async-done(((f32[8,7,8,128]{3,2,1,0:T(8,128)}), f32[8,7,8,128]{3,2,1,0:T(8,128)S(1)}, u32[]{:S(2)}, u32[]{:S(2)}) %all-to-all-start) | async-done | bytes 229408 | tf_op jit(solution)/shard_map/all_to_all | solution.py:623
  14.7 0.0 collective-permute-done.a_ref
  14.7 0.0 collective-permute-done.1.b_ref
  14.7 0.1 sends.1
  14.8 1.6 %collective-permute-start.2 = (bf16[30,24,128]{2,1,0:T(8,128)(2,1)S(1)}, bf16[30,24,128]{2,1,0:T(8,128)(2,1)S(1)}, u32[]{:S(2)}, u32[]{:S(2)}) collective-permute-start(bf16[30,24,128]{2,1,0:T(8,128)(2,1)S(1)} %get-tuple-element.25), channel_id=1, source_target_pairs={{0,1},{1,0},{2,3},{3,2},{4,5},{5,4},{6,7},{7,6},{8,9},{9,8},{10,11... | collective-permute-start | bytes 552968 | tf_op jit(solution)/shard_map/ppermute | solution.py:576
  16.4 0.7 %collective-permute-start.3 = (bf16[30,24,128]{2,1,0:T(8,128)(2,1)S(1)}, bf16[30,24,128]{2,1,0:T(8,128)(2,1)S(1)}, u32[]{:S(2)}, u32[]{:S(2)}) collective-permute-start(bf16[30,24,128]{2,1,0:T(8,128)(2,1)S(1)} %get-tuple-element.26), channel_id=1, source_target_pairs={{1,2},{2,1},{5,6},{6,5},{9,10},{10,9},{13,14},{14,13},{17,18},{18,... | collective-permute-start | bytes 552968 | tf_op jit(solution)/shard_map/ppermute | solution.py:577
  17.1 4.9 %prepare.1 = (f32[14,14,16,128]{3,2,1,0:T(8,128)S(1)}, f32[4,14,14,4,8,128]{5,4,3,2,1,0:T(8,128)S(1)}, f32[4,12,12,4,8,128]{5,4,3,2,1,0:T(8,128)S(1)}, f32[4,10,...) custom-call(f32[448,128]{1,0:T(8,128)S(1)} %bitcast.14, ...), custom_call_target="tpu_custom_call" | custom-call | tf_op jit(solution)/shard_map/prepare/pallas_call | solution.py:655
  22.0 0.0 collective-permute-done.2.a_ref
  22.0 0.0 collective-permute-done.3.b_ref
  22.0 5.1 %sweeps.1 = (bf16[8,5,8,128]{3,2,1,0:T(8,128)(2,1)S(1)}, f32[14,14,16,128]{3,2,1,0:T(8,128)S(1)}, f32[4,14,14,4,8,128]{5,4,3,2,1,0:T(8,128)S(1)}, f32[4,12,12,4,...) custom-call(f32[448,128]{1,0:T(8,128)S(1)} %bitcast.15, ...), custom_call_target="tpu_custom_call", output_to_operand_aliasing={{1}: (6, {}), {2}: (7, {}), {3}: (8, {}), {4}: (9, {}), {5}... | custom-call | tf_op jit(solution)/shard_map/sweeps/pallas_call | solution.py:663
  27.1 9.1 %all_to_all.10 = bf16[8,5,8,128]{3,2,1,0:T(8,128)(2,1)S(1)} all-to-all(bf16[8,5,8,128]{3,2,1,0:T(8,128)(2,1)S(1)} %get-tuple-element.35), channel_id=1, replica_groups=mesh['pot'=8,'grid'=4] {'pot'}, dimensions={0} | all-to-all | bytes 163840 | tf_op jit(solution)/shard_map/all_to_all | solution.py:673
  36.2 4.4 %collective-permute-start.4 = (f32[1,128]{1,0:T(1,128)S(1)}, f32[1,128]{1,0:T(1,128)S(1)}, u32[]{:S(2)}, u32[]{:S(2)}) collective-permute-start(f32[1,128]{1,0:T(1,128)S(1)} %bitcast.17), channel_id=1, source_target_pairs={{0,1},{1,0},{2,3},{3,2},{4,5},{5,4},{6,7},{7,6},{8,9},{9,8},{10,11... | collective-permute-start | bytes 1544 | tf_op jit(solution)/shard_map/ppermute | solution.py:679
  40.7 1.5 %collective-permute-done.4 = f32[1,128]{1,0:T(1,128)S(1)} collective-permute-done((f32[1,128]{1,0:T(1,128)S(1)}, f32[1,128]{1,0:T(1,128)S(1)}, u32[]{:S(2)}, u32[]{:S(2)}) %collective-permute-start.4) | collective-permute-done | bytes 544 | tf_op jit(solution)/shard_map/ppermute | solution.py:679
  42.2 2.1 %collective-permute-start.5 = (f32[1,128]{1,0:T(1,128)S(1)}, f32[1,128]{1,0:T(1,128)S(1)}, u32[]{:S(2)}, u32[]{:S(2)}) collective-permute-start(f32[1,128]{1,0:T(1,128)S(1)} %bitcast_add_fusion), channel_id=1, source_target_pairs={{0,2},{1,3},{2,0},{3,1},{4,6},{5,7},{6,4},{7,5},{8,10},{9,11},{10,... | collective-permute-start | bytes 1544 | tf_op jit(solution)/shard_map/ppermute | solution.py:679
  44.3 0.7 %convert_bitcast_fusion = f32[1,8,4096]{2,1,0:T(8,128)} fusion(bf16[8,4,8,128]{3,2,1,0:T(8,128)(2,1)S(1)} %slice.12), kind=kLoop, calls=%fused_computation | loop fusion | flops 32768 | bytes 196608 | tf_op jit(solution)/shard_map/reshape | solution.py:675
  45.0 1.7 %collective-permute-done.5 = f32[1,128]{1,0:T(1,128)S(1)} collective-permute-done((f32[1,128]{1,0:T(1,128)S(1)}, f32[1,128]{1,0:T(1,128)S(1)}, u32[]{:S(2)}, u32[]{:S(2)}) %collective-permute-start.5) | collective-permute-done | bytes 544 | tf_op jit(solution)/shard_map/ppermute | solution.py:679
  46.7 0.5 %slice_multiply_fusion = f32[1,8]{1,0:T(1,128)} fusion(f32[1,128]{1,0:T(1,128)S(1)} %add.7), kind=kLoop, calls=%fused_computation.2 | loop fusion | flops 8 | bytes 64 | tf_op jit(solution)/shard_map/div | solution.py:681
  (4 shorter events, 0.0 us)
Async XLA Ops:
  2.9 11.8 %all-to-all-start = ((f32[8,7,8,128]{3,2,1,0:T(8,128)}), f32[8,7,8,128]{3,2,1,0:T(8,128)S(1)}, u32[]{:S(2)}, u32[]{:S(2)}) async-start(f32[8,7,8,128]{3,2,1,0:T(8,128)} %get-tuple-element.19), calls=%async_computation | async-start | bytes 458752 | tf_op jit(solution)/shard_map/all_to_all | solution.py:623
  8.1 6.6 %collective-permute-start = (bf16[24,16,128]{2,1,0:T(8,128)(2,1)S(1)}, bf16[24,16,128]{2,1,0:T(8,128)(2,1)S(1)}, u32[]{:S(2)}, u32[]{:S(2)}) collective-permute-start(bf16[24,16,128]{2,1,0:T(8,128)(2,1)S(1)} %get-tuple-element.23), channel_id=1, source_target_pairs={{0,4},{4,0},{8,12},{12,8},{16,20},{20,16},{24,28},{28,24},{1,5},{5... | collective-permute-start | bytes 294920 | tf_op jit(solution)/shard_map/ppermute | solution.py:576
  8.6 6.1 %collective-permute-start.1 = (bf16[24,16,128]{2,1,0:T(8,128)(2,1)S(1)}, bf16[24,16,128]{2,1,0:T(8,128)(2,1)S(1)}, u32[]{:S(2)}, u32[]{:S(2)}) collective-permute-start(bf16[24,16,128]{2,1,0:T(8,128)(2,1)S(1)} %get-tuple-element.24), channel_id=1, source_target_pairs={{4,8},{8,4},{12,16},{16,12},{20,24},{24,20},{5,9},{9,5},{13,17},{1... | collective-permute-start | bytes 294920 | tf_op jit(solution)/shard_map/ppermute | solution.py:577
  14.8 7.2 %collective-permute-start.2 = (bf16[30,24,128]{2,1,0:T(8,128)(2,1)S(1)}, bf16[30,24,128]{2,1,0:T(8,128)(2,1)S(1)}, u32[]{:S(2)}, u32[]{:S(2)}) collective-permute-start(bf16[30,24,128]{2,1,0:T(8,128)(2,1)S(1)} %get-tuple-element.25), channel_id=1, source_target_pairs={{0,1},{1,0},{2,3},{3,2},{4,5},{5,4},{6,7},{7,6},{8,9},{9,8},{10,11... | collective-permute-start | bytes 552968 | tf_op jit(solution)/shard_map/ppermute | solution.py:576
  16.4 5.6 %collective-permute-start.3 = (bf16[30,24,128]{2,1,0:T(8,128)(2,1)S(1)}, bf16[30,24,128]{2,1,0:T(8,128)(2,1)S(1)}, u32[]{:S(2)}, u32[]{:S(2)}) collective-permute-start(bf16[30,24,128]{2,1,0:T(8,128)(2,1)S(1)} %get-tuple-element.26), channel_id=1, source_target_pairs={{1,2},{2,1},{5,6},{6,5},{9,10},{10,9},{13,14},{14,13},{17,18},{18,... | collective-permute-start | bytes 552968 | tf_op jit(solution)/shard_map/ppermute | solution.py:577
  36.2 6.0 %collective-permute-start.4 = (f32[1,128]{1,0:T(1,128)S(1)}, f32[1,128]{1,0:T(1,128)S(1)}, u32[]{:S(2)}, u32[]{:S(2)}) collective-permute-start(f32[1,128]{1,0:T(1,128)S(1)} %bitcast.17), channel_id=1, source_target_pairs={{0,1},{1,0},{2,3},{3,2},{4,5},{5,4},{6,7},{7,6},{8,9},{9,8},{10,11... | collective-permute-start | bytes 1544 | tf_op jit(solution)/shard_map/ppermute | solution.py:679
  42.2 4.5 %collective-permute-start.5 = (f32[1,128]{1,0:T(1,128)S(1)}, f32[1,128]{1,0:T(1,128)S(1)}, u32[]{:S(2)}, u32[]{:S(2)}) collective-permute-start(f32[1,128]{1,0:T(1,128)S(1)} %bitcast_add_fusion), channel_id=1, source_target_pairs={{0,2},{1,3},{2,0},{3,1},{4,6},{5,7},{6,4},{7,5},{8,10},{9,11},{10,... | collective-permute-start | bytes 1544 | tf_op jit(solution)/shard_map/ppermute | solution.py:679

commit v5 on v4

--- a/solution.py
+++ b/solution.py
@@ -439,7 +439,7 @@
         place(cells, r_ref, ro_ref, first_ref, first_term)
         return carry
 
-    lax.fori_loop(0, depth, plane, 0, unroll=2)
+    lax.fori_loop(0, depth, plane, 0, unroll=4)
 
     def scaled(z, carry):
         later_ref[z] = (INNER[-1] / INNER[0]) * r_ref[z]
@@ -569,10 +569,12 @@
     return pltpu.with_memory_space_constraint(array, pltpu.HBM)
 
 
-def swapped(to_a, to_b, axis):
+def swapped(to_a, to_b, axis, name):
     count = lax.axis_size(axis)
     pairs_a = [(i, i ^ 1) for i in range(count)]
     pairs_b = [(i, i + 1 if i % 2 else i - 1) for i in range(1, count - 1)]
+    if name == "row":
+        pairs_b = [(i, (i + 1 if i % 2 else i - 1) % count) for i in range(count)]
     got_a = lax.ppermute(to_a, axis, pairs_a)
     got_b = lax.ppermute(to_b, axis, pairs_b)
     return got_a, got_b
@@ -619,7 +621,7 @@
         ],
         name="first",
     )(in_hbm(fields_tiles), in_hbm(orbitals), in_hbm(local_potential))
-    got_a, got_b = swapped(to_a, to_b, "pot")
+    got_a, got_b = swapped(to_a, to_b, "pot", "row")
     parts = lax.all_to_all(windows, "pot", 0, 0, tiled=True)
     parts = parts.reshape(pots * window * depth, LANES)
 
@@ -642,7 +644,7 @@
         out_specs=[VMEM] * 2,
         name="sends",
     )(*in_vmem(parts, own, got_a, got_b))
-    z_a, z_b = swapped(up, down, "grid")
+    z_a, z_b = swapped(up, down, "grid", "plane")
 
     own_values = [
         shape(region + (half, LANES), f32),

time: 47.5 us -> 47.1 us (level)
  starting transfers between devices: 15.2 us -> 17.9 us
  blocking collectives: 9.06 us -> 7.49 us
  waiting for transfers between devices: 6.99 us -> 5.9 us
    ppermute x2, starting transfers between devices: 1.32 us -> 3.19 us  [swapped(): got_b = lax.ppermute(to_b, axis, pairs_b)]
    all_to_all x1, blocking collectives: 9.06 us -> 7.49 us  [rows_plan(): back = lax.all_to_all(sent, 'pot', 0, 0, tiled=True)]
    all_to_all x1, waiting for transfers between devices: 3.75 us -> 2.46 us  [rows_plan(): parts = lax.all_to_all(windows, 'pot', 0, 0, tiled=True)]
    ppermute x2, waiting for transfers between devices: 0.01 us -> 0.96 us  [swapped(): got_b = lax.ppermute(to_b, axis, pairs_b)]
    ppermute x2, waiting for transfers between devices: 3.23 us -> 2.48 us  [rows_plan(): lax.ppermute(margins, 'grid', [(i, i ^ step) for i in range(grids)])]
    ppermute x2, starting transfers between devices: 6.54 us -> 7.3 us  [rows_plan(): lax.ppermute(margins, 'grid', [(i, i ^ step) for i in range(grids)])]
  transfers between devices with their start and end apart: 7 -> 7, of which waited for: 3 -> 4; matrix products, arithmetic and copies ran while one was open for 1% -> 1% of each run, Pallas kernels for 14% -> 13%
where the time goes in v5:
time: 47.1 us; the launch traced here: 46.8 us
  starting transfers between devices  17.9 us (38%)
  Pallas kernels  13.7 us (29%)
  blocking collectives  7.49 us (16%)
  waiting for transfers between devices  5.9 us (13%)
  other arithmetic  1.22 us (3%)
  between operations  0.7 us (1%)
    all_to_all x1, blocking collectives, rows_plan(): back = lax.all_to_all(sent, 'pot', 0, 0, tiled=True)  7.49 us
    ppermute x2, starting transfers between devices, rows_plan(): lax.ppermute(margins, 'grid', [(i, i ^ step) for i in range(grids)])  7.3 us
    all_to_all x1, starting transfers between devices, rows_plan(): parts = lax.all_to_all(windows, 'pot', 0, 0, tiled=True)  5.22 us
    pallas_call x1, Pallas kernels, rows_plan(): call(sweep_kernel, out_shape=[shape((fields, pieces + 1, depth, LANES), b...  5.07 us
    pallas_call x1, Pallas kernels, rows_plan(): call(prepare_kernel, out_shape=own_values + own_values[:1] + [shape((dept...  4.6 us
    ppermute x2, starting transfers between devices, swapped(): got_b = lax.ppermute(to_b, axis, pairs_b)  3.19 us
    ppermute x2, waiting for transfers between devices, rows_plan(): lax.ppermute(margins, 'grid', [(i, i ^ step) for i in range(grids)])  2.48 us
    all_to_all x1, waiting for transfers between devices, rows_plan(): parts = lax.all_to_all(windows, 'pot', 0, 0, tiled=True)  2.46 us
  transfers between devices with their start and end apart: 7, of which 4 were waited for; matrix products, arithmetic and copies ran while one was open for 1% of the time, Pallas kernels for 13%

profile of v5, /device:TPU:0, one launch (start us, length us, event | category | flops | bytes accessed | tf_op | source)
XLA Modules:
  0.0 46.8 jit_solution(2167313394336556179)
XLA Ops:
  0.6 2.3 %first.1 = (f32[8,7,8,128]{3,2,1,0:T(8,128)}, bf16[8,8,16,128]{3,2,1,0:T(8,128)(2,1)S(1)}, bf16[24,16,128]{2,1,0:T(8,128)(2,1)S(1)}, bf16[24,16,128]{2,1,0:T(8,128)(2,1)S(1)}, f32[8,32,128]{2,1,0:T(8,128)S(1)}) custom-call(f32[32,8,128]{2,1,0:T(8,128)} %bitcast.16, bf16[32,8,512]{2,1,0:T(8,128)(2,1)} %orbitals_ref.1, f32[32,4096]{1,0:T(8,128)} %potential_ref.1), custom_call_target="tpu_custom_call" | custom-call | tf_op jit(solution)/shard_map/first/pallas_call | solution.py:603
  2.9 5.2 %all-to-all-start = ((f32[8,7,8,128]{3,2,1,0:T(8,128)}), f32[8,7,8,128]{3,2,1,0:T(8,128)S(1)}, u32[]{:S(2)}, u32[]{:S(2)}) async-start(f32[8,7,8,128]{3,2,1,0:T(8,128)} %get-tuple-element.19), calls=%async_computation | async-start | bytes 458752 | tf_op jit(solution)/shard_map/all_to_all | solution.py:625
  8.1 0.5 %collective-permute-start = (bf16[24,16,128]{2,1,0:T(8,128)(2,1)S(1)}, bf16[24,16,128]{2,1,0:T(8,128)(2,1)S(1)}, u32[]{:S(2)}, u32[]{:S(2)}) collective-permute-start(bf16[24,16,128]{2,1,0:T(8,128)(2,1)S(1)} %get-tuple-element.23), channel_id=1, source_target_pairs={{0,4},{4,0},{8,12},{12,8},{16,20},{20,16},{24,28},{28,24},{1,5},{5... | collective-permute-start | bytes 294920 | tf_op jit(solution)/shard_map/ppermute | solution.py:578
  8.6 2.5 %collective-permute-start.1 = (bf16[24,16,128]{2,1,0:T(8,128)(2,1)S(1)}, bf16[24,16,128]{2,1,0:T(8,128)(2,1)S(1)}, u32[]{:S(2)}, u32[]{:S(2)}) collective-permute-start(bf16[24,16,128]{2,1,0:T(8,128)(2,1)S(1)} %get-tuple-element.24), channel_id=1, source_target_pairs={{0,28},{4,8},{8,4},{12,16},{16,12},{20,24},{24,20},{28,0},{1,29},{... | collective-permute-start | bytes 294920 | tf_op jit(solution)/shard_map/ppermute | solution.py:579
  11.2 1.6 %diagonal.1.r_ref = f32[14,14,16,128]{3,2,1,0:T(8,128)S(1)} custom-call(f32[32]{0:T(128)} %energy_ref.1, f32[8,32,128]{2,1,0:T(8,128)S(1)} %get-tuple-element.20.lp_ref), custom_call_target="tpu_custom_call" | custom-call | tf_op jit(solution)/shard_map/diagonal/pallas_call | solution.py:628
  12.8 2.5 %all-to-all-done = f32[8,7,8,128]{3,2,1,0:T(8,128)S(1)} async-done(((f32[8,7,8,128]{3,2,1,0:T(8,128)}), f32[8,7,8,128]{3,2,1,0:T(8,128)S(1)}, u32[]{:S(2)}, u32[]{:S(2)}) %all-to-all-start) | async-done | bytes 229408 | tf_op jit(solution)/shard_map/all_to_all | solution.py:625
  15.2 0.0 collective-permute-done.a_ref
  15.2 1.0 %collective-permute-done.1.b_ref = bf16[24,16,128]{2,1,0:T(8,128)(2,1)S(1)} collective-permute-done((bf16[24,16,128]{2,1,0:T(8,128)(2,1)S(1)}, bf16[24,16,128]{2,1,0:T(8,128)(2,1)S(1)}, u32[]{:S(2)}, u32[]{:S(2)}) %collective-permute-start.1) | collective-permute-done | bytes 98336 | tf_op jit(solution)/shard_map/ppermute | solution.py:579
  16.2 0.1 sends.1
  16.3 1.6 %collective-permute-start.2 = (bf16[30,24,128]{2,1,0:T(8,128)(2,1)S(1)}, bf16[30,24,128]{2,1,0:T(8,128)(2,1)S(1)}, u32[]{:S(2)}, u32[]{:S(2)}) collective-permute-start(bf16[30,24,128]{2,1,0:T(8,128)(2,1)S(1)} %get-tuple-element.25), channel_id=1, source_target_pairs={{0,1},{1,0},{2,3},{3,2},{4,5},{5,4},{6,7},{7,6},{8,9},{9,8},{10,11... | collective-permute-start | bytes 552968 | tf_op jit(solution)/shard_map/ppermute | solution.py:578
  18.0 0.7 %collective-permute-start.3 = (bf16[30,24,128]{2,1,0:T(8,128)(2,1)S(1)}, bf16[30,24,128]{2,1,0:T(8,128)(2,1)S(1)}, u32[]{:S(2)}, u32[]{:S(2)}) collective-permute-start(bf16[30,24,128]{2,1,0:T(8,128)(2,1)S(1)} %get-tuple-element.26), channel_id=1, source_target_pairs={{1,2},{2,1},{5,6},{6,5},{9,10},{10,9},{13,14},{14,13},{17,18},{18,... | collective-permute-start | bytes 552968 | tf_op jit(solution)/shard_map/ppermute | solution.py:579
  18.6 4.6 %prepare.1 = (f32[14,14,16,128]{3,2,1,0:T(8,128)S(1)}, f32[4,14,14,4,8,128]{5,4,3,2,1,0:T(8,128)S(1)}, f32[4,12,12,4,8,128]{5,4,3,2,1,0:T(8,128)S(1)}, f32[4,10,...) custom-call(f32[448,128]{1,0:T(8,128)S(1)} %bitcast.14, ...), custom_call_target="tpu_custom_call" | custom-call | tf_op jit(solution)/shard_map/prepare/pallas_call | solution.py:657
  23.2 0.0 collective-permute-done.2.a_ref
  23.2 0.0 collective-permute-done.3.b_ref
  23.3 5.1 %sweeps.1 = (bf16[8,5,8,128]{3,2,1,0:T(8,128)(2,1)S(1)}, f32[14,14,16,128]{3,2,1,0:T(8,128)S(1)}, f32[4,14,14,4,8,128]{5,4,3,2,1,0:T(8,128)S(1)}, f32[4,12,12,4,...) custom-call(f32[448,128]{1,0:T(8,128)S(1)} %bitcast.15, ...), custom_call_target="tpu_custom_call", output_to_operand_aliasing={{1}: (6, {}), {2}: (7, {}), {3}: (8, {}), {4}: (9, {}), {5}... | custom-call | tf_op jit(solution)/shard_map/sweeps/pallas_call | solution.py:665
  28.3 7.5 %all_to_all.10 = bf16[8,5,8,128]{3,2,1,0:T(8,128)(2,1)S(1)} all-to-all(bf16[8,5,8,128]{3,2,1,0:T(8,128)(2,1)S(1)} %get-tuple-element.35), channel_id=1, replica_groups=mesh['pot'=8,'grid'=4] {'pot'}, dimensions={0} | all-to-all | bytes 163840 | tf_op jit(solution)/shard_map/all_to_all | solution.py:675
  35.9 4.4 %collective-permute-start.4 = (f32[1,128]{1,0:T(1,128)S(1)}, f32[1,128]{1,0:T(1,128)S(1)}, u32[]{:S(2)}, u32[]{:S(2)}) collective-permute-start(f32[1,128]{1,0:T(1,128)S(1)} %bitcast.17), channel_id=1, source_target_pairs={{0,1},{1,0},{2,3},{3,2},{4,5},{5,4},{6,7},{7,6},{8,9},{9,8},{10,11... | collective-permute-start | bytes 1544 | tf_op jit(solution)/shard_map/ppermute | solution.py:681
  40.3 1.5 %collective-permute-done.4 = f32[1,128]{1,0:T(1,128)S(1)} collective-permute-done((f32[1,128]{1,0:T(1,128)S(1)}, f32[1,128]{1,0:T(1,128)S(1)}, u32[]{:S(2)}, u32[]{:S(2)}) %collective-permute-start.4) | collective-permute-done | bytes 544 | tf_op jit(solution)/shard_map/ppermute | solution.py:681
  41.8 2.9 %collective-permute-start.5 = (f32[1,128]{1,0:T(1,128)S(1)}, f32[1,128]{1,0:T(1,128)S(1)}, u32[]{:S(2)}, u32[]{:S(2)}) collective-permute-start(f32[1,128]{1,0:T(1,128)S(1)} %bitcast_add_fusion), channel_id=1, source_target_pairs={{0,2},{1,3},{2,0},{3,1},{4,6},{5,7},{6,4},{7,5},{8,10},{9,11},{10,... | collective-permute-start | bytes 1544 | tf_op jit(solution)/shard_map/ppermute | solution.py:681
  44.7 0.7 %convert_bitcast_fusion = f32[1,8,4096]{2,1,0:T(8,128)} fusion(bf16[8,4,8,128]{3,2,1,0:T(8,128)(2,1)S(1)} %slice.12), kind=kLoop, calls=%fused_computation | loop fusion | flops 32768 | bytes 196608 | tf_op jit(solution)/shard_map/reshape | solution.py:677
  45.4 0.9 %collective-permute-done.5 = f32[1,128]{1,0:T(1,128)S(1)} collective-permute-done((f32[1,128]{1,0:T(1,128)S(1)}, f32[1,128]{1,0:T(1,128)S(1)}, u32[]{:S(2)}, u32[]{:S(2)}) %collective-permute-start.5) | collective-permute-done | bytes 544 | tf_op jit(solution)/shard_map/ppermute | solution.py:681
  46.3 0.5 %slice_multiply_fusion = f32[1,8]{1,0:T(1,128)} fusion(f32[1,128]{1,0:T(1,128)S(1)} %add.7), kind=kLoop, calls=%fused_computation.2 | loop fusion | flops 8 | bytes 64 | tf_op jit(solution)/shard_map/div | solution.py:683
  (4 shorter events, 0.0 us)
Async XLA Ops:
  2.9 12.3 %all-to-all-start = ((f32[8,7,8,128]{3,2,1,0:T(8,128)}), f32[8,7,8,128]{3,2,1,0:T(8,128)S(1)}, u32[]{:S(2)}, u32[]{:S(2)}) async-start(f32[8,7,8,128]{3,2,1,0:T(8,128)} %get-tuple-element.19), calls=%async_computation | async-start | bytes 458752 | tf_op jit(solution)/shard_map/all_to_all | solution.py:625
  8.1 7.1 %collective-permute-start = (bf16[24,16,128]{2,1,0:T(8,128)(2,1)S(1)}, bf16[24,16,128]{2,1,0:T(8,128)(2,1)S(1)}, u32[]{:S(2)}, u32[]{:S(2)}) collective-permute-start(bf16[24,16,128]{2,1,0:T(8,128)(2,1)S(1)} %get-tuple-element.23), channel_id=1, source_target_pairs={{0,4},{4,0},{8,12},{12,8},{16,20},{20,16},{24,28},{28,24},{1,5},{5... | collective-permute-start | bytes 294920 | tf_op jit(solution)/shard_map/ppermute | solution.py:578
  8.6 7.6 %collective-permute-start.1 = (bf16[24,16,128]{2,1,0:T(8,128)(2,1)S(1)}, bf16[24,16,128]{2,1,0:T(8,128)(2,1)S(1)}, u32[]{:S(2)}, u32[]{:S(2)}) collective-permute-start(bf16[24,16,128]{2,1,0:T(8,128)(2,1)S(1)} %get-tuple-element.24), channel_id=1, source_target_pairs={{0,28},{4,8},{8,4},{12,16},{16,12},{20,24},{24,20},{28,0},{1,29},{... | collective-permute-start | bytes 294920 | tf_op jit(solution)/shard_map/ppermute | solution.py:579
  16.3 6.9 %collective-permute-start.2 = (bf16[30,24,128]{2,1,0:T(8,128)(2,1)S(1)}, bf16[30,24,128]{2,1,0:T(8,128)(2,1)S(1)}, u32[]{:S(2)}, u32[]{:S(2)}) collective-permute-start(bf16[30,24,128]{2,1,0:T(8,128)(2,1)S(1)} %get-tuple-element.25), channel_id=1, source_target_pairs={{0,1},{1,0},{2,3},{3,2},{4,5},{5,4},{6,7},{7,6},{8,9},{9,8},{10,11... | collective-permute-start | bytes 552968 | tf_op jit(solution)/shard_map/ppermute | solution.py:578
  18.0 5.3 %collective-permute-start.3 = (bf16[30,24,128]{2,1,0:T(8,128)(2,1)S(1)}, bf16[30,24,128]{2,1,0:T(8,128)(2,1)S(1)}, u32[]{:S(2)}, u32[]{:S(2)}) collective-permute-start(bf16[30,24,128]{2,1,0:T(8,128)(2,1)S(1)} %get-tuple-element.26), channel_id=1, source_target_pairs={{1,2},{2,1},{5,6},{6,5},{9,10},{10,9},{13,14},{14,13},{17,18},{18,... | collective-permute-start | bytes 552968 | tf_op jit(solution)/shard_map/ppermute | solution.py:579
  35.9 6.0 %collective-permute-start.4 = (f32[1,128]{1,0:T(1,128)S(1)}, f32[1,128]{1,0:T(1,128)S(1)}, u32[]{:S(2)}, u32[]{:S(2)}) collective-permute-start(f32[1,128]{1,0:T(1,128)S(1)} %bitcast.17), channel_id=1, source_target_pairs={{0,1},{1,0},{2,3},{3,2},{4,5},{5,4},{6,7},{7,6},{8,9},{9,8},{10,11... | collective-permute-start | bytes 1544 | tf_op jit(solution)/shard_map/ppermute | solution.py:681
  41.8 4.5 %collective-permute-start.5 = (f32[1,128]{1,0:T(1,128)S(1)}, f32[1,128]{1,0:T(1,128)S(1)}, u32[]{:S(2)}, u32[]{:S(2)}) collective-permute-start(f32[1,128]{1,0:T(1,128)S(1)} %bitcast_add_fusion), channel_id=1, source_target_pairs={{0,2},{1,3},{2,0},{3,1},{4,6},{5,7},{6,4},{7,5},{8,10},{9,11},{10,... | collective-permute-start | bytes 1544 | tf_op jit(solution)/shard_map/ppermute | solution.py:681

commit v6 on v5

--- a/solution.py
+++ b/solution.py
@@ -255,7 +255,9 @@
         to_b_ref[at] = jnp.where(even, bottom, top).astype(jnp.bfloat16)
 
 
-def diagonal_kernel(energy_ref, lp_ref, r_ref, lp_ref2, *part_refs):
+def diagonal_kernel(
+    energy_ref, lp_ref, r_ref, spread_ref, gather_ref, lp_ref2, *part_refs
+):
     pairs, planes_all, _ = lp_ref.shape
     region_z, region_y, size, _ = r_ref.shape
     depth, rows = region_z - 2 * HALO, region_y - 2 * HALO
@@ -327,6 +329,8 @@
         return carry
 
     lax.fori_loop(0, region_z, plane, 0)
+    spread_ref[...] = spread_matrix()
+    gather_ref[...] = gather_matrix()
 
 
 def spread_matrix():
@@ -335,10 +339,15 @@
     return one_hot(from_lane % NX == SPLIT * (to_lane % STEPS) + to_lane // LANES)
 
 
-def place(cells, r_ref, ro_ref, first_ref, then=None):
+def gather_matrix():
+    lane_in, x_out = iota((SPLIT * LANES, LANES), 0), iota((SPLIT * LANES, LANES), 1) % NX
+    return one_hot(x_out == SPLIT * (lane_in % STEPS) + lane_in // LANES)
+
+
+def place(cells, spread_ref, r_ref, ro_ref, first_ref, then=None):
     fields = first_ref.shape[4]
     packed = jnp.concatenate([parts for _, parts, _, _ in cells], axis=0).astype(jnp.bfloat16)
-    values = (START / LAST) * bf16_dot(packed, spread_matrix())
+    values = (START / LAST) * bf16_dot(packed, spread_ref[...])
     for number, (orbitals, _, z, y) in enumerate(cells):
         zi, yi = z + HALO, y + HALO
         o = (-2.0 * START * LAST) * orbitals.astype(jnp.float32)
@@ -410,7 +419,7 @@
 
 
 def prepare_kernel(
-    parts_ref, own_ref, a_ref, b_ref, r_ref, inverse_ref,
+    parts_ref, own_ref, a_ref, b_ref, r_ref, spread_ref, inverse_ref,
     ro_ref, first_ref, x_ref, y_ref, acc_ref, later_ref, wide_ref, w_ref,
 ):
     depth, rows = own_ref.shape[:2]
@@ -436,7 +445,7 @@
         for y in range(-HALO, rows + HALO):
             value = of_fields(parts_ref, fields, depth, z, y)
             cells.append((row_tile(own_ref, a_ref, b_ref, z, y), two_parts(value, y), z, y))
-        place(cells, r_ref, ro_ref, first_ref, first_term)
+        place(cells, spread_ref, r_ref, ro_ref, first_ref, first_term)
         return carry
 
     lax.fori_loop(0, depth, plane, 0, unroll=4)
@@ -467,7 +476,7 @@
 
 
 def sweep_kernel(
-    parts_ref, a_ref, b_ref, r_ref, later_ref, wide_ref, ro_in, first_in, x_in, y_in, acc_in,
+    parts_ref, a_ref, b_ref, r_ref, later_ref, wide_ref, spread_ref, gather_ref, ro_in, first_in, x_in, y_in, acc_in,
     out_ref, ro_ref, first_ref, x_ref, y_ref, acc_ref, m_ref,
 ):
     depth, rows = acc_ref.shape[:2]
@@ -486,7 +495,7 @@
                 for ref, z in ((a_ref, z_a), (b_ref, z_b)):
                     tile = ref[at].astype(jnp.float32)
                     cells.append((tile[:size], tile[size:], z, y))
-        place(cells, r_ref, ro_ref, first_ref)
+        place(cells, spread_ref, r_ref, ro_ref, first_ref)
 
     top = HALO + depth
 
@@ -510,19 +519,20 @@
 
     lax.fori_loop(0, groups, group, 0)
 
-    lane_in, x_out = iota((SPLIT * LANES, LANES), 0), iota((SPLIT * LANES, LANES), 1) % NX
-    gather = one_hot(x_out == SPLIT * (lane_in % STEPS) + lane_in // LANES)
+    gather = gather_ref[...]
     left = lane_halves((fields, LANES))
     factor = 4.0 / count * -0.5
     planes = []
+    per_plane = rows * fields
+    acc = jnp.concatenate(
+        [acc_ref[:, :, m].reshape(depth * per_plane, LANES) for m in range(SPLIT)], axis=1
+    )
+    upper = acc.astype(jnp.bfloat16)
+    lower = (acc - upper.astype(jnp.float32)).astype(jnp.bfloat16)
+    totals = bf16_dot(jnp.concatenate([upper, lower], axis=0), gather)
+    totals = totals[: depth * per_plane] + totals[depth * per_plane :]
     for z in range(depth):
-        parts = [
-            jnp.concatenate([acc_ref[z, y, m] for y in range(rows)], axis=0) for m in range(SPLIT)
-        ]
-        acc = jnp.concatenate(parts, axis=1)
-        upper = acc.astype(jnp.bfloat16)
-        lower = (acc - upper.astype(jnp.float32)).astype(jnp.bfloat16)
-        total = bf16_dot(upper, gather) + bf16_dot(lower, gather)
+        total = totals[z * per_plane : (z + 1) * per_plane]
         tiles = []
         for y in range(rows):
             tiles.append(total[y * fields : (y + 1) * fields])
@@ -625,11 +635,15 @@
     parts = lax.all_to_all(windows, "pot", 0, 0, tiled=True)
     parts = parts.reshape(pots * window * depth, LANES)
 
-    inverse_diagonal = call(
+    inverse_diagonal, spread, gather = call(
         diagonal_kernel,
-        out_shape=shape(region + (half, LANES), f32),
+        out_shape=[
+            shape(region + (half, LANES), f32),
+            shape((LANES, SPLIT * LANES), bf16),
+            shape((SPLIT * LANES, LANES), bf16),
+        ],
         in_specs=[SMEM, VMEM],
-        out_specs=VMEM,
+        out_specs=[VMEM] * 3,
         scratch_shapes=[pltpu.VMEM((rows + 2 * LEAD, region[0] * SPLIT, LANES), f32)]
         + [pltpu.VMEM(lp_shape, f32)] * 3,
         name="diagonal",
@@ -657,20 +671,20 @@
     *prepared, later, wide = call(
         prepare_kernel,
         out_shape=own_values + own_values[:1] + [shape((depth * fields,) * 2, bf16)],
-        in_specs=[VMEM] * 6,
+        in_specs=[VMEM] * 7,
         out_specs=[VMEM] * 7,
         scratch_shapes=[pltpu.VMEM((rows, half, LANES), f32)],
         name="prepare",
-    )(*in_vmem(parts, own, got_a, got_b, inverse_diagonal), in_hbm(inverse_factor))
+    )(*in_vmem(parts, own, got_a, got_b, inverse_diagonal, spread), in_hbm(inverse_factor))
     sent, *_ = call(
         sweep_kernel,
         out_shape=[shape((fields, pieces + 1, depth, LANES), bf16)] + own_values,
-        in_specs=[VMEM] * 11,
+        in_specs=[VMEM] * 13,
         out_specs=[VMEM] * 6,
         scratch_shapes=[pltpu.VMEM((fields, LANES), f32)],
-        input_output_aliases={6 + i: 1 + i for i in range(5)},
+        input_output_aliases={8 + i: 1 + i for i in range(5)},
         name="sweeps",
-    )(*in_vmem(parts, z_a, z_b, inverse_diagonal, later, wide, *prepared))
+    )(*in_vmem(parts, z_a, z_b, inverse_diagonal, later, wide, spread, gather, *prepared))
 
     back = lax.all_to_all(sent, "pot", 0, 0, tiled=True)
     updated = back[:, :pieces].astype(f32).reshape(pots * pieces, depth, LANES).transpose(1, 0, 2)

time: 47.1 us -> 47.2 us (level)
  transfers between devices with their start and end apart: 7 -> 7, of which waited for: 4 -> 4; matrix products, arithmetic and copies ran while one was open for 1% -> 1% of each run, Pallas kernels for 13% -> 14%
where the time goes in v6:
time: 47.2 us; the launch traced here: 46.9 us
  starting transfers between devices  17.8 us (38%)
  Pallas kernels  13.8 us (29%)
  blocking collectives  7.49 us (16%)
  waiting for transfers between devices  5.87 us (12%)
  other arithmetic  1.22 us (3%)
  between operations  0.7 us (1%)
    all_to_all x1, blocking collectives, rows_plan(): back = lax.all_to_all(sent, 'pot', 0, 0, tiled=True)  7.49 us
    ppermute x2, starting transfers between devices, rows_plan(): lax.ppermute(margins, 'grid', [(i, i ^ step) for i in range(grids)])  7.24 us
    all_to_all x1, starting transfers between devices, rows_plan(): parts = lax.all_to_all(windows, 'pot', 0, 0, tiled=True)  5.22 us
    pallas_call x1, Pallas kernels, rows_plan(): call(sweep_kernel, out_shape=[shape((fields, pieces + 1, depth, LANES), b...  5.08 us
    pallas_call x1, Pallas kernels, rows_plan(): call(prepare_kernel, out_shape=own_values + own_values[:1] + [shape((dept...  4.65 us
    ppermute x2, starting transfers between devices, swapped(): got_b = lax.ppermute(to_b, axis, pairs_b)  3.19 us
    ppermute x2, waiting for transfers between devices, rows_plan(): lax.ppermute(margins, 'grid', [(i, i ^ step) for i in range(grids)])  2.53 us
    all_to_all x1, waiting for transfers between devices, rows_plan(): parts = lax.all_to_all(windows, 'pot', 0, 0, tiled=True)  2.37 us
  transfers between devices with their start and end apart: 7, of which 4 were waited for; matrix products, arithmetic and copies ran while one was open for 1% of the time, Pallas kernels for 14%

profile of v6, /device:TPU:0, one launch (start us, length us, event | category | flops | bytes accessed | tf_op | source)
XLA Modules:
  0.0 46.9 jit_solution(12127701526270552013)
XLA Ops:
  0.6 2.3 %first.1 = (f32[8,7,8,128]{3,2,1,0:T(8,128)}, bf16[8,8,16,128]{3,2,1,0:T(8,128)(2,1)S(1)}, bf16[24,16,128]{2,1,0:T(8,128)(2,1)S(1)}, bf16[24,16,128]{2,1,0:T(8,128)(2,1)S(1)}, f32[8,32,128]{2,1,0:T(8,128)S(1)}) custom-call(f32[32,8,128]{2,1,0:T(8,128)} %bitcast.16, bf16[32,8,512]{2,1,0:T(8,128)(2,1)} %orbitals_ref.1, f32[32,4096]{1,0:T(8,128)} %potential_ref.1), custom_call_target="tpu_custom_call" | custom-call | tf_op jit(solution)/shard_map/first/pallas_call | solution.py:613
  2.9 5.2 %all-to-all-start = ((f32[8,7,8,128]{3,2,1,0:T(8,128)}), f32[8,7,8,128]{3,2,1,0:T(8,128)S(1)}, u32[]{:S(2)}, u32[]{:S(2)}) async-start(f32[8,7,8,128]{3,2,1,0:T(8,128)} %get-tuple-element.22), calls=%async_computation | async-start | bytes 458752 | tf_op jit(solution)/shard_map/all_to_all | solution.py:635
  8.1 0.5 %collective-permute-start = (bf16[24,16,128]{2,1,0:T(8,128)(2,1)S(1)}, bf16[24,16,128]{2,1,0:T(8,128)(2,1)S(1)}, u32[]{:S(2)}, u32[]{:S(2)}) collective-permute-start(bf16[24,16,128]{2,1,0:T(8,128)(2,1)S(1)} %get-tuple-element.27), channel_id=1, source_target_pairs={{0,4},{4,0},{8,12},{12,8},{16,20},{20,16},{24,28},{28,24},{1,5},{5... | collective-permute-start | bytes 294920 | tf_op jit(solution)/shard_map/ppermute | solution.py:588
  8.6 2.5 %collective-permute-start.1 = (bf16[24,16,128]{2,1,0:T(8,128)(2,1)S(1)}, bf16[24,16,128]{2,1,0:T(8,128)(2,1)S(1)}, u32[]{:S(2)}, u32[]{:S(2)}) collective-permute-start(bf16[24,16,128]{2,1,0:T(8,128)(2,1)S(1)} %get-tuple-element.28), channel_id=1, source_target_pairs={{0,28},{4,8},{8,4},{12,16},{16,12},{20,24},{24,20},{28,0},{1,29},{... | collective-permute-start | bytes 294920 | tf_op jit(solution)/shard_map/ppermute | solution.py:589
  11.2 1.7 %diagonal.1 = (f32[14,14,16,128]{3,2,1,0:T(8,128)S(1)}, bf16[128,512]{1,0:T(8,128)(2,1)S(1)}, bf16[512,128]{1,0:T(8,128)(2,1)S(1)}) custom-call(f32[32]{0:T(128)} %energy_ref.1, f32[8,32,128]{2,1,0:T(8,128)S(1)} %get-tuple-element.23.lp_ref), custom_call_target="tpu_custom_call" | custom-call | tf_op jit(solution)/shard_map/diagonal/pallas_call | solution.py:638
  12.9 2.4 %all-to-all-done = f32[8,7,8,128]{3,2,1,0:T(8,128)S(1)} async-done(((f32[8,7,8,128]{3,2,1,0:T(8,128)}), f32[8,7,8,128]{3,2,1,0:T(8,128)S(1)}, u32[]{:S(2)}, u32[]{:S(2)}) %all-to-all-start) | async-done | bytes 229408 | tf_op jit(solution)/shard_map/all_to_all | solution.py:635
  15.2 0.0 collective-permute-done.a_ref
  15.2 1.0 %collective-permute-done.1.b_ref = bf16[24,16,128]{2,1,0:T(8,128)(2,1)S(1)} collective-permute-done((bf16[24,16,128]{2,1,0:T(8,128)(2,1)S(1)}, bf16[24,16,128]{2,1,0:T(8,128)(2,1)S(1)}, u32[]{:S(2)}, u32[]{:S(2)}) %collective-permute-start.1) | collective-permute-done | bytes 98336 | tf_op jit(solution)/shard_map/ppermute | solution.py:589
  16.2 0.1 sends.1
  16.3 1.6 %collective-permute-start.2 = (bf16[30,24,128]{2,1,0:T(8,128)(2,1)S(1)}, bf16[30,24,128]{2,1,0:T(8,128)(2,1)S(1)}, u32[]{:S(2)}, u32[]{:S(2)}) collective-permute-start(bf16[30,24,128]{2,1,0:T(8,128)(2,1)S(1)} %get-tuple-element.29), channel_id=1, source_target_pairs={{0,1},{1,0},{2,3},{3,2},{4,5},{5,4},{6,7},{7,6},{8,9},{9,8},{10,11... | collective-permute-start | bytes 552968 | tf_op jit(solution)/shard_map/ppermute | solution.py:588
  18.0 0.7 %collective-permute-start.3 = (bf16[30,24,128]{2,1,0:T(8,128)(2,1)S(1)}, bf16[30,24,128]{2,1,0:T(8,128)(2,1)S(1)}, u32[]{:S(2)}, u32[]{:S(2)}) collective-permute-start(bf16[30,24,128]{2,1,0:T(8,128)(2,1)S(1)} %get-tuple-element.30), channel_id=1, source_target_pairs={{1,2},{2,1},{5,6},{6,5},{9,10},{10,9},{13,14},{14,13},{17,18},{18,... | collective-permute-start | bytes 552968 | tf_op jit(solution)/shard_map/ppermute | solution.py:589
  18.6 4.6 %prepare.1 = (f32[14,14,16,128]{3,2,1,0:T(8,128)S(1)}, f32[4,14,14,4,8,128]{5,4,3,2,1,0:T(8,128)S(1)}, f32[4,12,12,4,8,128]{5,4,3,2,1,0:T(8,128)S(1)}, f32[4,10,...) custom-call(f32[448,128]{1,0:T(8,128)S(1)} %bitcast.14, ...), custom_call_target="tpu_custom_call" | custom-call | tf_op jit(solution)/shard_map/prepare/pallas_call | solution.py:671
  23.3 0.0 collective-permute-done.2.a_ref
  23.3 0.0 collective-permute-done.3.b_ref
  23.3 5.1 %sweeps.1 = (bf16[8,5,8,128]{3,2,1,0:T(8,128)(2,1)S(1)}, f32[14,14,16,128]{3,2,1,0:T(8,128)S(1)}, f32[4,14,14,4,8,128]{5,4,3,2,1,0:T(8,128)S(1)}, f32[4,12,12,4,...) custom-call(f32[448,128]{1,0:T(8,128)S(1)} %bitcast.15, ...), custom_call_target="tpu_custom_call", output_to_operand_aliasing={{1}: (8, {}), {2}: (9, {}), {3}: (10, {}), {4}: (11, {}), {... | custom-call | tf_op jit(solution)/shard_map/sweeps/pallas_call | solution.py:679
  28.4 7.5 %all_to_all.10 = bf16[8,5,8,128]{3,2,1,0:T(8,128)(2,1)S(1)} all-to-all(bf16[8,5,8,128]{3,2,1,0:T(8,128)(2,1)S(1)} %get-tuple-element.41), channel_id=1, replica_groups=mesh['pot'=8,'grid'=4] {'pot'}, dimensions={0} | all-to-all | bytes 163840 | tf_op jit(solution)/shard_map/all_to_all | solution.py:689
  35.9 4.4 %collective-permute-start.4 = (f32[1,128]{1,0:T(1,128)S(1)}, f32[1,128]{1,0:T(1,128)S(1)}, u32[]{:S(2)}, u32[]{:S(2)}) collective-permute-start(f32[1,128]{1,0:T(1,128)S(1)} %bitcast.17), channel_id=1, source_target_pairs={{0,1},{1,0},{2,3},{3,2},{4,5},{5,4},{6,7},{7,6},{8,9},{9,8},{10,11... | collective-permute-start | bytes 1544 | tf_op jit(solution)/shard_map/ppermute | solution.py:695
  40.3 1.5 %collective-permute-done.4 = f32[1,128]{1,0:T(1,128)S(1)} collective-permute-done((f32[1,128]{1,0:T(1,128)S(1)}, f32[1,128]{1,0:T(1,128)S(1)}, u32[]{:S(2)}, u32[]{:S(2)}) %collective-permute-start.4) | collective-permute-done | bytes 544 | tf_op jit(solution)/shard_map/ppermute | solution.py:695
  41.9 2.8 %collective-permute-start.5 = (f32[1,128]{1,0:T(1,128)S(1)}, f32[1,128]{1,0:T(1,128)S(1)}, u32[]{:S(2)}, u32[]{:S(2)}) collective-permute-start(f32[1,128]{1,0:T(1,128)S(1)} %bitcast_add_fusion), channel_id=1, source_target_pairs={{0,2},{1,3},{2,0},{3,1},{4,6},{5,7},{6,4},{7,5},{8,10},{9,11},{10,... | collective-permute-start | bytes 1544 | tf_op jit(solution)/shard_map/ppermute | solution.py:695
  44.7 0.7 %convert_bitcast_fusion = f32[1,8,4096]{2,1,0:T(8,128)} fusion(bf16[8,4,8,128]{3,2,1,0:T(8,128)(2,1)S(1)} %slice.12), kind=kLoop, calls=%fused_computation | loop fusion | flops 32768 | bytes 196608 | tf_op jit(solution)/shard_map/reshape | solution.py:691
  45.4 1.0 %collective-permute-done.5 = f32[1,128]{1,0:T(1,128)S(1)} collective-permute-done((f32[1,128]{1,0:T(1,128)S(1)}, f32[1,128]{1,0:T(1,128)S(1)}, u32[]{:S(2)}, u32[]{:S(2)}) %collective-permute-start.5) | collective-permute-done | bytes 544 | tf_op jit(solution)/shard_map/ppermute | solution.py:695
  46.4 0.5 %slice_multiply_fusion = f32[1,8]{1,0:T(1,128)} fusion(f32[1,128]{1,0:T(1,128)S(1)} %add.7), kind=kLoop, calls=%fused_computation.2 | loop fusion | flops 8 | bytes 64 | tf_op jit(solution)/shard_map/div | solution.py:697
  (4 shorter events, 0.0 us)
Async XLA Ops:
  2.9 12.3 %all-to-all-start = ((f32[8,7,8,128]{3,2,1,0:T(8,128)}), f32[8,7,8,128]{3,2,1,0:T(8,128)S(1)}, u32[]{:S(2)}, u32[]{:S(2)}) async-start(f32[8,7,8,128]{3,2,1,0:T(8,128)} %get-tuple-element.22), calls=%async_computation | async-start | bytes 458752 | tf_op jit(solution)/shard_map/all_to_all | solution.py:635
  8.1 7.1 %collective-permute-start = (bf16[24,16,128]{2,1,0:T(8,128)(2,1)S(1)}, bf16[24,16,128]{2,1,0:T(8,128)(2,1)S(1)}, u32[]{:S(2)}, u32[]{:S(2)}) collective-permute-start(bf16[24,16,128]{2,1,0:T(8,128)(2,1)S(1)} %get-tuple-element.27), channel_id=1, source_target_pairs={{0,4},{4,0},{8,12},{12,8},{16,20},{20,16},{24,28},{28,24},{1,5},{5... | collective-permute-start | bytes 294920 | tf_op jit(solution)/shard_map/ppermute | solution.py:588
  8.6 7.6 %collective-permute-start.1 = (bf16[24,16,128]{2,1,0:T(8,128)(2,1)S(1)}, bf16[24,16,128]{2,1,0:T(8,128)(2,1)S(1)}, u32[]{:S(2)}, u32[]{:S(2)}) collective-permute-start(bf16[24,16,128]{2,1,0:T(8,128)(2,1)S(1)} %get-tuple-element.28), channel_id=1, source_target_pairs={{0,28},{4,8},{8,4},{12,16},{16,12},{20,24},{24,20},{28,0},{1,29},{... | collective-permute-start | bytes 294920 | tf_op jit(solution)/shard_map/ppermute | solution.py:589
  16.3 7.0 %collective-permute-start.2 = (bf16[30,24,128]{2,1,0:T(8,128)(2,1)S(1)}, bf16[30,24,128]{2,1,0:T(8,128)(2,1)S(1)}, u32[]{:S(2)}, u32[]{:S(2)}) collective-permute-start(bf16[30,24,128]{2,1,0:T(8,128)(2,1)S(1)} %get-tuple-element.29), channel_id=1, source_target_pairs={{0,1},{1,0},{2,3},{3,2},{4,5},{5,4},{6,7},{7,6},{8,9},{9,8},{10,11... | collective-permute-start | bytes 552968 | tf_op jit(solution)/shard_map/ppermute | solution.py:588
  18.0 5.3 %collective-permute-start.3 = (bf16[30,24,128]{2,1,0:T(8,128)(2,1)S(1)}, bf16[30,24,128]{2,1,0:T(8,128)(2,1)S(1)}, u32[]{:S(2)}, u32[]{:S(2)}) collective-permute-start(bf16[30,24,128]{2,1,0:T(8,128)(2,1)S(1)} %get-tuple-element.30), channel_id=1, source_target_pairs={{1,2},{2,1},{5,6},{6,5},{9,10},{10,9},{13,14},{14,13},{17,18},{18,... | collective-permute-start | bytes 552968 | tf_op jit(solution)/shard_map/ppermute | solution.py:589
  35.9 6.0 %collective-permute-start.4 = (f32[1,128]{1,0:T(1,128)S(1)}, f32[1,128]{1,0:T(1,128)S(1)}, u32[]{:S(2)}, u32[]{:S(2)}) collective-permute-start(f32[1,128]{1,0:T(1,128)S(1)} %bitcast.17), channel_id=1, source_target_pairs={{0,1},{1,0},{2,3},{3,2},{4,5},{5,4},{6,7},{7,6},{8,9},{9,8},{10,11... | collective-permute-start | bytes 1544 | tf_op jit(solution)/shard_map/ppermute | solution.py:695
  41.9 4.5 %collective-permute-start.5 = (f32[1,128]{1,0:T(1,128)S(1)}, f32[1,128]{1,0:T(1,128)S(1)}, u32[]{:S(2)}, u32[]{:S(2)}) collective-permute-start(f32[1,128]{1,0:T(1,128)S(1)} %bitcast_add_fusion), channel_id=1, source_target_pairs={{0,2},{1,3},{2,0},{3,1},{4,6},{5,7},{6,4},{7,5},{8,10},{9,11},{10,... | collective-permute-start | bytes 1544 | tf_op jit(solution)/shard_map/ppermute | solution.py:695
